TPU v7x, 32 devices: a whole 2x2x4 slice. The times are simulated.
32 devices in a mesh: wide: 8 (over z, y), narrow: 4 (over x, core).
Axes of the slice: x: 2, y: 2, z: 4, core: 2. Of those that a mesh axis runs over, the one named last changes fastest.
Arguments:
- inputs: bfloat16 [8192, 768], P(('wide', 'narrow')), may hold values from -6 to 6
- memory: bfloat16 [8192, 768], P(('wide', 'narrow')), may hold values from -6 to 6
- segment_ids: int32 [8, 1024], P('wide'), may hold values from 0 to 3, never falling along the last dimension, each value on 1 to 512 neighbouring positions
- memory_ids: int32 [8, 1024], P('wide'), may hold values from 0 to 3, never falling along the last dimension, each value on 1 to 512 neighbouring positions
- self_gain: float32 [768], replicated, may hold values from 0.25 to 1.75
- self_query: bfloat16 [768, 768], P('wide', 'narrow'), may hold values from -0.02734375 to 0.02734375
- self_key: bfloat16 [768, 768], P('wide', 'narrow'), may hold values from -0.21875 to 0.21875
- self_value: bfloat16 [768, 768], P('wide', 'narrow'), may hold values from -0.21875 to 0.21875
- self_out: bfloat16 [768, 768], P('narrow', 'wide'), may hold values from -1.75 to 1.75
- bias_table: float32 [32, 12], P(None, 'narrow'), may hold values from -4 to 4
- cross_gain: float32 [768], replicated, may hold values from 0.25 to 1.75
- cross_query: bfloat16 [768, 768], P('wide', 'narrow'), may hold values from -0.02734375 to 0.02734375
- cross_key: bfloat16 [768, 768], P('wide', 'narrow'), may hold values from -0.21875 to 0.21875
- cross_value: bfloat16 [768, 768], P('wide', 'narrow'), may hold values from -0.21875 to 0.21875
- cross_out: bfloat16 [768, 768], P('narrow', 'wide'), may hold values from -1.75 to 1.75
- ff_gain: float32 [768], replicated, may hold values from 0.25 to 1.75
- ff_gate: bfloat16 [768, 2048], P('wide', 'narrow'), may hold values from -0.21875 to 0.21875
- ff_up: bfloat16 [768, 2048], P('wide', 'narrow'), may hold values from -0.21875 to 0.21875
- ff_down: bfloat16 [2048, 768], P('narrow', 'wide'), may hold values from -0.1875 to 0.1875
- cotangent: bfloat16 [8192, 768], P(('wide', 'narrow')), may hold values from -6 to 6
Outputs:
- output: bfloat16 [8192, 768], P(('wide', 'narrow'))
- grad_inputs: bfloat16 [8192, 768], P(('wide', 'narrow'))
- grad_memory: bfloat16 [8192, 768], P(('wide', 'narrow'))
- grad_self_gain: float32 [768], replicated
- grad_self_query: float32 [768, 768], P('wide', 'narrow')
- grad_self_key: float32 [768, 768], P('wide', 'narrow')
- grad_self_value: float32 [768, 768], P('wide', 'narrow')
- grad_self_out: float32 [768, 768], P('narrow', 'wide')
- grad_bias_table: float32 [32, 12], replicated
- grad_cross_gain: float32 [768], replicated
- grad_cross_query: float32 [768, 768], P('wide', 'narrow')
- grad_cross_key: float32 [768, 768], P('wide', 'narrow')
- grad_cross_value: float32 [768, 768], P('wide', 'narrow')
- grad_cross_out: float32 [768, 768], P('narrow', 'wide')
- grad_ff_gain: float32 [768], replicated
- grad_ff_gate: float32 [768, 2048], P('wide', 'narrow')
- grad_ff_up: float32 [768, 2048], P('wide', 'narrow')
- grad_ff_down: float32 [2048, 768], P('narrow', 'wide')
Inputs may be any that keep to these rules, and one draw needn't show every extreme that they name: `segment_ids`: along each row the ids never fall; every id of 0 to 3 holds 1 to 512 positions, one exactly 512. `memory_ids`: along each row the ids never fall; every id of 0 to 3 holds 1 to 512 positions, one exactly 512.
All inputs are finite; a program needn't handle non-finite values.
Results may differ from a plain program's by a relative error of at most 0.024.
Values may be sent and summed in bfloat16 or wider, within the bound.
A program may use at most 192 MiB of HBM per device.

v0:
```python
import math

import jax
import jax.numpy as jnp
import numpy as np
from jax import lax
from jax.sharding import PartitionSpec as P

DH = 64
NB = 32
MAX_DIST = 128


def bucket_table(length, buckets, reach):
    exact_part = buckets // 2
    distance = np.arange(length)
    spread = (
        np.log(np.maximum(distance, exact_part) / exact_part)
        / np.log(reach / exact_part)
        * (buckets - exact_part)
    )
    far_bucket = np.minimum(exact_part + np.floor(spread).astype(np.int64), buckets - 1)
    return np.where(distance < exact_part, distance, far_bucket).astype(np.int32)


def bucket_ranges(length):
    table = bucket_table(length, NB, MAX_DIST)
    first_seen = {}
    last_seen = {}
    for position in range(length):
        which = int(table[position])
        if which not in first_seen:
            first_seen[which] = position
        last_seen[which] = position
    ranges = []
    for which in range(NB):
        if which in first_seen:
            ranges.append((which, first_seen[which], last_seen[which] + 1))
    return ranges


def rms_norm(values, norm_gain):
    factor = lax.rsqrt(jnp.mean(values * values, axis=-1, keepdims=True) + 1e-06)
    return values * factor * norm_gain


def gelu_tanh(values):
    return (
        0.5
        * values
        * (
            1.0
            + jnp.tanh(math.sqrt(2.0 / math.pi) * (values + 0.044715 * values * values * values))
        )
    )


def gated(gate_part, up_part):
    return gelu_tanh(gate_part) * up_part


def matmul(left, right):
    return jnp.dot(left, right, preferred_element_type=jnp.float32)


def matmul_left_t(left, right):
    return lax.dot_general(
        left, right, (((0,), (0,)), ((), ())), preferred_element_type=jnp.float32
    )


def matmul_right_t(left, right):
    return lax.dot_general(
        left, right, (((1,), (1,)), ((), ())), preferred_element_type=jnp.float32
    )


def gather_rows(rows):
    return lax.all_gather(rows, "narrow", axis=0, tiled=True)


def add_branch(residual, partial_value):
    return residual + lax.psum_scatter(partial_value, "narrow", scatter_dimension=0, tiled=True)


def gather_grad(rows):
    return lax.all_gather(rows, "narrow", axis=0, tiled=True)


def sum_back(partial_value):
    return lax.psum_scatter(partial_value, "narrow", scatter_dimension=0, tiled=True)


def head_masks(columns):
    heads = columns // DH
    return (
        jnp.arange(columns, dtype=jnp.int32)[None, :] // DH
        == jnp.arange(heads, dtype=jnp.int32)[:, None]
    )


def block_distance(first_row, block_rows, keys):
    return (first_row + jnp.arange(block_rows, dtype=jnp.int32))[:, None] - jnp.arange(
        keys, dtype=jnp.int32
    )[None, :]


def block_scores(q_masked, key_rows, first_row, query_ids, key_ids, self_bias):
    scores = jnp.einsum("hqc,kc->hqk", q_masked, key_rows, preferred_element_type=jnp.float32)
    block_rows = q_masked.shape[1]
    allowed = (
        lax.dynamic_slice_in_dim(query_ids, first_row, block_rows)[:, None] == key_ids[None, :]
    )
    if self_bias is not None:
        table, ranges = self_bias
        distance = block_distance(first_row, block_rows, key_rows.shape[0])
        bias = jnp.zeros(scores.shape, jnp.float32)
        for which, start, stop in ranges:
            bias = jnp.where((distance >= start)[None], table[which][:, None, None], bias)
        scores = scores + bias
        allowed = allowed & (distance >= 0)
    return jnp.where(allowed[None], scores, -1000000000.0)


def attend_forward(queries, key_rows, value_rows, query_ids, key_ids, self_bias):
    length, columns = queries.shape
    masks = head_masks(columns)
    mask_low = masks.astype(jnp.bfloat16)
    mask_wide = masks.astype(jnp.float32)
    block_rows = min(512, length)
    contexts = []
    logsums = []
    for first_row in range(0, length, block_rows):
        q_masked = queries[first_row : first_row + block_rows][None] * mask_low[:, None, :]
        masked = block_scores(q_masked, key_rows, first_row, query_ids, key_ids, self_bias)
        peak = jnp.max(masked, axis=-1, keepdims=True)
        expons = jnp.exp(masked - peak)
        totals = jnp.sum(expons, axis=-1, keepdims=True)
        probs = (expons / totals).astype(jnp.bfloat16)
        per_head = jnp.einsum("hqk,kc->hqc", probs, value_rows, preferred_element_type=jnp.float32)
        context = jnp.sum(per_head * mask_wide[:, None, :], axis=0)
        contexts.append(context.astype(jnp.bfloat16))
        logsums.append((peak + jnp.log(totals))[..., 0])
    return (jnp.concatenate(contexts, axis=0), jnp.concatenate(logsums, axis=1))


def attend_backward(
    queries, key_rows, value_rows, query_ids, key_ids, logsums, grad_context, self_bias
):
    length, columns = queries.shape
    key_count = key_rows.shape[0]
    masks = head_masks(columns)
    heads = masks.shape[0]
    mask_low = masks.astype(jnp.bfloat16)
    mask_wide = masks.astype(jnp.float32)
    block_rows = min(512, length)
    grad_keys = jnp.zeros((key_count, columns), jnp.float32)
    grad_values = jnp.zeros((key_count, columns), jnp.float32)
    grad_buckets = jnp.zeros((NB, heads), jnp.float32)
    grad_queries = []
    for first_row in range(0, length, block_rows):
        q_masked = queries[first_row : first_row + block_rows][None] * mask_low[:, None, :]
        ctx_masked = grad_context[first_row : first_row + block_rows][None] * mask_low[:, None, :]
        masked = block_scores(q_masked, key_rows, first_row, query_ids, key_ids, self_bias)
        probs = jnp.exp(masked - logsums[:, first_row : first_row + block_rows][..., None])
        grad_probs = jnp.einsum(
            "hqc,kc->hqk", ctx_masked, value_rows, preferred_element_type=jnp.float32
        )
        delta = jnp.sum(probs * grad_probs, axis=-1, keepdims=True)
        grad_scores = (probs * (grad_probs - delta)).astype(jnp.bfloat16)
        per_head = jnp.einsum(
            "hqk,kc->hqc", grad_scores, key_rows, preferred_element_type=jnp.float32
        )
        grad_queries.append(jnp.sum(per_head * mask_wide[:, None, :], axis=0).astype(jnp.bfloat16))
        grad_keys = grad_keys + jnp.einsum(
            "hqk,hqc->kc", grad_scores, q_masked, preferred_element_type=jnp.float32
        )
        grad_values = grad_values + jnp.einsum(
            "hqk,hqc->kc",
            probs.astype(jnp.bfloat16),
            ctx_masked,
            preferred_element_type=jnp.float32,
        )
        if self_bias is not None:
            table, ranges = self_bias
            distance = block_distance(first_row, block_rows, key_count)
            scores_wide = grad_scores.astype(jnp.float32)
            rows_list = []
            found = {}
            for which, start, stop in ranges:
                inside = ((distance >= start) & (distance < stop))[None]
                found[which] = jnp.sum(jnp.where(inside, scores_wide, 0.0), axis=(1, 2))
            for which in range(NB):
                rows_list.append(
                    found[which] if which in found else jnp.zeros((heads,), jnp.float32)
                )
            grad_buckets = grad_buckets + jnp.stack(rows_list, axis=0)
    grad_q = jnp.concatenate(grad_queries, axis=0)
    return (grad_q, grad_keys.astype(jnp.bfloat16), grad_values.astype(jnp.bfloat16), grad_buckets)


def shards(
    inputs,
    memory,
    segment_ids,
    memory_ids,
    self_gain,
    self_query,
    self_key,
    self_value,
    self_out,
    bias_table,
    cross_gain,
    cross_query,
    cross_key,
    cross_value,
    cross_out,
    ff_gain,
    ff_gate,
    ff_up,
    ff_down,
    cotangent,
):
    gathered = (
        lax.all_gather(self_query, "wide", axis=0, tiled=True),
        lax.all_gather(self_key, "wide", axis=0, tiled=True),
        lax.all_gather(self_value, "wide", axis=0, tiled=True),
        lax.all_gather(self_out, "wide", axis=1, tiled=True),
        lax.all_gather(cross_query, "wide", axis=0, tiled=True),
        lax.all_gather(cross_key, "wide", axis=0, tiled=True),
        lax.all_gather(cross_value, "wide", axis=0, tiled=True),
        lax.all_gather(cross_out, "wide", axis=1, tiled=True),
        lax.all_gather(ff_gate, "wide", axis=0, tiled=True),
        lax.all_gather(ff_up, "wide", axis=0, tiled=True),
        lax.all_gather(ff_down, "wide", axis=1, tiled=True),
    )
    (
        w_query_self,
        w_key_self,
        w_value_self,
        w_out_self,
        w_query_cross,
        w_key_cross,
        w_value_cross,
        w_out_cross,
        w_gate,
        w_up,
        w_down,
    ) = gathered
    sequences = segment_ids.shape[0]
    length = segment_ids.shape[1]
    memory_length = memory_ids.shape[1]
    heads = w_query_self.shape[1] // DH
    columns = heads * DH

    def by_rows(values, rows):
        return values.reshape(sequences, rows, values.shape[-1])

    self_bias = (bias_table, bucket_ranges(length))
    x_rows = inputs.astype(jnp.float32)
    normed_self = rms_norm(x_rows, self_gain)
    full_self, memory_full = (
        lax.all_gather(normed_self.astype(jnp.bfloat16), "narrow", axis=0, tiled=True),
        lax.all_gather(memory, "narrow", axis=0, tiled=True),
    )
    q_self = matmul(full_self, w_query_self).astype(jnp.bfloat16)
    k_self = matmul(full_self, w_key_self).astype(jnp.bfloat16)
    v_self = matmul(full_self, w_value_self).astype(jnp.bfloat16)
    ctx_self, lse_self = lax.map(
        lambda item: attend_forward(item[0], item[1], item[2], item[3], item[3], self_bias),
        (by_rows(q_self, length), by_rows(k_self, length), by_rows(v_self, length), segment_ids),
    )
    ctx_self = ctx_self.reshape(-1, columns)
    x_two = add_branch(x_rows, matmul(ctx_self, w_out_self))
    full_cross = gather_rows(rms_norm(x_two, cross_gain).astype(jnp.bfloat16))
    q_cross = matmul(full_cross, w_query_cross).astype(jnp.bfloat16)
    k_cross = matmul(memory_full, w_key_cross).astype(jnp.bfloat16)
    v_cross = matmul(memory_full, w_value_cross).astype(jnp.bfloat16)
    ctx_cross, lse_cross = lax.map(
        lambda item: attend_forward(item[0], item[1], item[2], item[3], item[4], None),
        (
            by_rows(q_cross, length),
            by_rows(k_cross, memory_length),
            by_rows(v_cross, memory_length),
            segment_ids,
            memory_ids,
        ),
    )
    ctx_cross = ctx_cross.reshape(-1, columns)
    x_three = add_branch(x_two, matmul(ctx_cross, w_out_cross))
    full_ff = gather_rows(rms_norm(x_three, ff_gain).astype(jnp.bfloat16))
    gate_vals = matmul(full_ff, w_gate)
    up_vals = matmul(full_ff, w_up)
    hidden = gated(gate_vals, up_vals).astype(jnp.bfloat16)
    result = add_branch(x_three, matmul(hidden, w_down)).astype(jnp.bfloat16)
    residual = cotangent.astype(jnp.float32)
    dy_ff = gather_grad(residual.astype(jnp.bfloat16))
    grad_down = matmul_left_t(hidden, dy_ff)
    grad_hidden = matmul_right_t(dy_ff, w_down)
    _, pull_gate = jax.vjp(gated, gate_vals, up_vals)
    grad_gate, grad_up = pull_gate(grad_hidden)
    grad_gate = grad_gate.astype(jnp.bfloat16)
    grad_up = grad_up.astype(jnp.bfloat16)
    grad_w_gate = matmul_left_t(full_ff, grad_gate)
    grad_w_up = matmul_left_t(full_ff, grad_up)
    grad_normed = sum_back(matmul_right_t(grad_gate, w_gate) + matmul_right_t(grad_up, w_up))
    _, pull_norm = jax.vjp(rms_norm, x_three, ff_gain)
    grad_rows_ff, grad_gain_ff = pull_norm(grad_normed)
    residual = residual + grad_rows_ff
    dy_cross = gather_grad(residual.astype(jnp.bfloat16))
    grad_out_cross = matmul_left_t(ctx_cross, dy_cross)
    dctx_cross = matmul_right_t(dy_cross, w_out_cross).astype(jnp.bfloat16)
    dq_cross, dk_cross, dv_cross, _ = lax.map(
        lambda item: attend_backward(
            item[0], item[1], item[2], item[3], item[4], item[5], item[6], None
        ),
        (
            by_rows(q_cross, length),
            by_rows(k_cross, memory_length),
            by_rows(v_cross, memory_length),
            segment_ids,
            memory_ids,
            lse_cross,
            by_rows(dctx_cross, length),
        ),
    )
    dq_cross = dq_cross.reshape(-1, columns)
    dk_cross = dk_cross.reshape(-1, columns)
    dv_cross = dv_cross.reshape(-1, columns)
    grad_query_cross = matmul_left_t(full_cross, dq_cross)
    grad_key_cross = matmul_left_t(memory_full, dk_cross)
    grad_value_cross = matmul_left_t(memory_full, dv_cross)
    normed_part = matmul_right_t(dq_cross, w_query_cross)
    memory_part = matmul_right_t(dk_cross, w_key_cross) + matmul_right_t(dv_cross, w_value_cross)
    grad_normed_cross, grad_memory_rows = (
        lax.psum_scatter(
            normed_part.astype(jnp.bfloat16), "narrow", scatter_dimension=0, tiled=True
        ).astype(jnp.float32),
        lax.psum_scatter(
            memory_part.astype(jnp.bfloat16), "narrow", scatter_dimension=0, tiled=True
        ).astype(jnp.float32),
    )
    _, pull_cross = jax.vjp(rms_norm, x_two, cross_gain)
    grad_rows_cross, grad_gain_cross = pull_cross(grad_normed_cross)
    residual = residual + grad_rows_cross
    dy_self = gather_grad(residual.astype(jnp.bfloat16))
    grad_out_self = matmul_left_t(ctx_self, dy_self)
    dctx_self = matmul_right_t(dy_self, w_out_self).astype(jnp.bfloat16)
    dq_self, dk_self, dv_self, bucket_grads = lax.map(
        lambda item: attend_backward(
            item[0], item[1], item[2], item[3], item[3], item[4], item[5], self_bias
        ),
        (
            by_rows(q_self, length),
            by_rows(k_self, length),
            by_rows(v_self, length),
            segment_ids,
            lse_self,
            by_rows(dctx_self, length),
        ),
    )
    dq_self = dq_self.reshape(-1, columns)
    dk_self = dk_self.reshape(-1, columns)
    dv_self = dv_self.reshape(-1, columns)
    grad_table_local = jnp.sum(bucket_grads, axis=0)
    narrow_count = lax.axis_size("narrow")
    placed = (jnp.arange(narrow_count, dtype=jnp.int32) == lax.axis_index("narrow")).astype(
        jnp.float32
    )
    table_full = (placed[None, :, None] * grad_table_local[:, None, :]).reshape(
        NB, narrow_count * heads
    )
    grad_query_self = matmul_left_t(full_self, dq_self)
    grad_key_self = matmul_left_t(full_self, dk_self)
    grad_value_self = matmul_left_t(full_self, dv_self)
    grad_normed_self = sum_back(
        matmul_right_t(dq_self, w_query_self)
        + matmul_right_t(dk_self, w_key_self)
        + matmul_right_t(dv_self, w_value_self)
    )
    _, pull_self = jax.vjp(rms_norm, x_rows, self_gain)
    grad_rows_self, grad_gain_self = pull_self(grad_normed_self)
    grad_input_rows = (residual + grad_rows_self).astype(jnp.bfloat16)
    final_sums = (
        lax.psum_scatter(grad_query_self, "wide", scatter_dimension=0, tiled=True),
        lax.psum_scatter(grad_key_self, "wide", scatter_dimension=0, tiled=True),
        lax.psum_scatter(grad_value_self, "wide", scatter_dimension=0, tiled=True),
        lax.psum_scatter(grad_out_self, "wide", scatter_dimension=1, tiled=True),
        lax.psum_scatter(grad_query_cross, "wide", scatter_dimension=0, tiled=True),
        lax.psum_scatter(grad_key_cross, "wide", scatter_dimension=0, tiled=True),
        lax.psum_scatter(grad_value_cross, "wide", scatter_dimension=0, tiled=True),
        lax.psum_scatter(grad_out_cross, "wide", scatter_dimension=1, tiled=True),
        lax.psum_scatter(grad_w_gate, "wide", scatter_dimension=0, tiled=True),
        lax.psum_scatter(grad_w_up, "wide", scatter_dimension=0, tiled=True),
        lax.psum_scatter(grad_down, "wide", scatter_dimension=1, tiled=True),
    )
    gain_self_sum, gain_cross_sum, gain_ff_sum, table_sum = lax.psum(
        (grad_gain_self, grad_gain_cross, grad_gain_ff, table_full), ("wide", "narrow")
    )
    return (
        result,
        grad_input_rows,
        grad_memory_rows.astype(jnp.bfloat16),
        gain_self_sum,
        final_sums[0],
        final_sums[1],
        final_sums[2],
        final_sums[3],
        table_sum,
        gain_cross_sum,
        final_sums[4],
        final_sums[5],
        final_sums[6],
        final_sums[7],
        gain_ff_sum,
        final_sums[8],
        final_sums[9],
        final_sums[10],
    )


def solution(mesh):
    placed = (
        P(("wide", "narrow"), None),
        P(("wide", "narrow"), None),
        P("wide", None),
        P("wide", None),
        P(),
        P("wide", "narrow"),
        P("wide", "narrow"),
        P("wide", "narrow"),
        P("narrow", "wide"),
        P(None, "narrow"),
        P(),
        P("wide", "narrow"),
        P("wide", "narrow"),
        P("wide", "narrow"),
        P("narrow", "wide"),
        P(),
        P("wide", "narrow"),
        P("wide", "narrow"),
        P("narrow", "wide"),
        P(("wide", "narrow"), None),
    )
    return jax.shard_map(
        shards,
        mesh=mesh,
        in_specs=placed,
        out_specs=(
            P(("wide", "narrow"), None),
            P(("wide", "narrow"), None),
            P(("wide", "narrow"), None),
            P(),
            P("wide", "narrow"),
            P("wide", "narrow"),
            P("wide", "narrow"),
            P("narrow", "wide"),
            P(),
            P(),
            P("wide", "narrow"),
            P("wide", "narrow"),
            P("wide", "narrow"),
            P("narrow", "wide"),
            P(),
            P("wide", "narrow"),
            P("wide", "narrow"),
            P("narrow", "wide"),
        ),
        check_vma=False,
    )
```

profile of v0, /device:TPU:0, one launch (start us, length us, event | category | flops | bytes accessed | tf_op | source)
XLA Modules:
  0.0 1634.2 jit_solution(14689022726666973465)
XLA Ops:
  31.8 30.5 %compare_and_fusion.1 = (pred[512,1024]{1,0:T(8,128)(4,1)}, pred[512,1024]{1,0:T(8,128)(4,1)}, pred[512,1024]{1,0:T(8,128)(4,1)S(1)}, pred[512,1024]{1,0:T(8,128...) fusion(s32[1024]{0:T(1024)S(1)} %bitcast.218, ...), kind=kLoop, calls=%fused_computation.385 | loop fusion | flops 55050240 | bytes 35665920 | tf_op jit(solution)/shard_map/while/body/eval_jaxpr/and | solution.py:121
  75.1 34.9 %all_gather.56 = bf16[768,192]{1,0:T(8,128)(2,1)} all-gather(bf16[96,192]{1,0:T(8,128)(2,1)S(1)} %copy-done.137), channel_id=1, replica_groups=mesh['wide'=8,'narrow'=4] {'wide'}, dimensions={0}, use_global_device_ids=true | all-gather | bytes 331776 | tf_op jit(solution)/shard_map/all_gather | solution.py:226
  110.1 31.3 %all_gather.55 = bf16[768,192]{1,0:T(8,128)(2,1)S(1)} all-gather(bf16[96,192]{1,0:T(8,128)(2,1)S(1)} %copy-done.138), channel_id=1, replica_groups=mesh['wide'=8,'narrow'=4] {'wide'}, dimensions={0}, use_global_device_ids=true | all-gather | bytes 331776 | tf_op jit(solution)/shard_map/all_gather | solution.py:225
  141.3 31.2 %all_gather.57 = bf16[768,192]{1,0:T(8,128)(2,1)S(1)} all-gather(bf16[96,192]{1,0:T(8,128)(2,1)S(1)} %copy-done.139), channel_id=1, replica_groups=mesh['wide'=8,'narrow'=4] {'wide'}, dimensions={0}, use_global_device_ids=true | all-gather | bytes 331776 | tf_op jit(solution)/shard_map/all_gather | solution.py:227
  172.5 33.0 %all_gather.58 = bf16[192,768]{0,1:T(8,128)(2,1)} all-gather(bf16[192,96]{0,1:T(8,128)(2,1)S(1)} %copy.44), channel_id=1, replica_groups=mesh['wide'=8,'narrow'=4] {'wide'}, dimensions={1}, use_global_device_ids=true | all-gather | bytes 331776 | tf_op jit(solution)/shard_map/all_gather | solution.py:228
  211.6 27.6 %fusion.433 = (f32[3,512]{1,0:T(4,128)S(1)}, f32[3,512,1024]{2,1,0:T(8,128)}) fusion(f32[3]{0:T(128)S(1)} %copy-done.202, pred[512,1024]{1,0:T(8,128)(4,1)} %fusion.225, f32[3]{0:T(128)S(1)} %copy-done.203, pred[512,1024]{1,0:T(8,128)(4,1)} %fusion.194, f32[3]{0:T(128)S(1)} %get-tuple-element.260, pred[512,1024]{1,0:T(8,128)(4,1)} %fusion.195, ...), kind=kOutput, calls=%fused_computation.608 | convolution fusion | flops 659323392 | bytes 24190464 | tf_op jit(solution)/shard_map/while/body/eval_jaxpr/hqc,kc->hqk/dot_general | solution.py:109
  243.8 28.2 %fusion.432 = (f32[3,512]{1,0:T(4,128)}, f32[3,512,1024]{2,1,0:T(8,128)}) fusion(f32[3]{0:T(128)} %get-tuple-element.289, pred[512,1024]{1,0:T(8,128)(4,1)} %get-tuple-element.386, f32[3]{0:T(128)} %get-tuple-element.290, pred[512,1024]{1,0:T(8,128)(4,1)} %get-tuple-element.355, f32[3]{0:T(128)} %copy-done.205, pred[512,1024]{1,0:T(8,128)(4,1)} %get-tuple-element.356, ...), kind=kOutput, calls=%fused_computation.607 | convolution fusion | flops 659323392 | bytes 24190464 | tf_op jit(solution)/shard_map/while/body/eval_jaxpr/hqc,kc->hqk/dot_general | solution.py:109
  284.7 37.9 %reduce-scatter.27.cloned.1.call-done = f32[256,768]{1,0:T(8,128)} async-done(((f32[1024,768]{1,0:T(8,128)}), f32[256,768]{1,0:T(8,128)}) %reduce-scatter.27.cloned.1.call-update) | async-done | bytes 786448 | tf_op jit(solution)/shard_map/reduce_scatter | solution.py:83
  325.1 31.4 %all_gather.60 = bf16[768,192]{1,0:T(8,128)(2,1)S(1)} all-gather(bf16[96,192]{1,0:T(8,128)(2,1)S(1)} %copy-done.140), channel_id=1, replica_groups=mesh['wide'=8,'narrow'=4] {'wide'}, dimensions={0}, use_global_device_ids=true | all-gather | bytes 331776 | tf_op jit(solution)/shard_map/all_gather | solution.py:229
  356.5 31.0 %all_gather.62 = bf16[768,192]{1,0:T(8,128)(2,1)S(1)} all-gather(bf16[96,192]{1,0:T(8,128)(2,1)S(1)} %copy-done.141), channel_id=1, replica_groups=mesh['wide'=8,'narrow'=4] {'wide'}, dimensions={0}, use_global_device_ids=true | all-gather | bytes 331776 | tf_op jit(solution)/shard_map/all_gather | solution.py:230
  387.4 31.3 %all_gather.63 = bf16[768,192]{1,0:T(8,128)(2,1)S(1)} all-gather(bf16[96,192]{1,0:T(8,128)(2,1)} %param.33), channel_id=1, replica_groups=mesh['wide'=8,'narrow'=4] {'wide'}, dimensions={0}, use_global_device_ids=true | all-gather | bytes 331776 | tf_op jit(solution)/shard_map/all_gather | solution.py:231
  418.8 33.0 %all_gather.64 = bf16[192,768]{0,1:T(8,128)(2,1)} all-gather(bf16[192,96]{0,1:T(8,128)(2,1)S(1)} %copy.45), channel_id=1, replica_groups=mesh['wide'=8,'narrow'=4] {'wide'}, dimensions={1}, use_global_device_ids=true | all-gather | bytes 331776 | tf_op jit(solution)/shard_map/all_gather | solution.py:232
  472.3 38.1 %reduce-scatter.29.cloned.1.call-done = f32[256,768]{1,0:T(8,128)} async-done(((f32[1024,768]{1,0:T(8,128)}), f32[256,768]{1,0:T(8,128)}) %reduce-scatter.29.cloned.1.call-update) | async-done | bytes 786448 | tf_op jit(solution)/shard_map/reduce_scatter | solution.py:83
  513.9 34.2 %all_gather.66 = bf16[768,512]{1,0:T(8,128)(2,1)} all-gather(bf16[96,512]{1,0:T(8,128)(2,1)S(1)} %copy-done.131), channel_id=1, replica_groups=mesh['wide'=8,'narrow'=4] {'wide'}, dimensions={0}, use_global_device_ids=true | all-gather | bytes 884736 | tf_op jit(solution)/shard_map/all_gather | solution.py:233
  548.2 34.2 %all_gather.67 = bf16[768,512]{1,0:T(8,128)(2,1)} all-gather(bf16[96,512]{1,0:T(8,128)(2,1)} %param.37), channel_id=1, replica_groups=mesh['wide'=8,'narrow'=4] {'wide'}, dimensions={0}, use_global_device_ids=true | all-gather | bytes 884736 | tf_op jit(solution)/shard_map/all_gather | solution.py:234
  582.4 35.0 %all_gather.68 = bf16[512,768]{0,1:T(8,128)(2,1)} all-gather(bf16[512,96]{0,1:T(8,128)(2,1)} %param.38), channel_id=1, replica_groups=mesh['wide'=8,'narrow'=4] {'wide'}, dimensions={1}, use_global_device_ids=true | all-gather | bytes 884736 | tf_op jit(solution)/shard_map/all_gather | solution.py:235
  635.2 38.3 %reduce-scatter.33.cloned.1.call-done = f32[256,768]{1,0:T(8,128)} async-done(((f32[1024,768]{1,0:T(8,128)}), f32[256,768]{1,0:T(8,128)}) %reduce-scatter.33.cloned.1.call-update) | async-done | bytes 786448 | tf_op jit(solution)/shard_map/reduce_scatter | solution.py:91
  677.9 19.5 %all-gather.18.cloned.1.call-done = bf16[1024,768]{1,0:T(8,128)(2,1)} async-done(((bf16[256,768]{1,0:T(8,128)(2,1)}), bf16[1024,768]{1,0:T(8,128)(2,1)}) %all-gather.18.cloned.1.call-update) | async-done | bytes 1572880 | tf_op jit(solution)/shard_map/all_gather | solution.py:87
  732.7 21.3 %reduce-scatter.35.cloned.1.call-done = bf16[256,768]{1,0:T(8,128)(2,1)} async-done(((bf16[1024,768]{1,0:T(8,128)(2,1)}), bf16[256,768]{1,0:T(8,128)(2,1)}) %reduce-scatter.35.cloned.1.call-update) | async-done | bytes 393232 | tf_op jit(solution)/shard_map/reduce_scatter | solution.py:336
  755.8 38.7 %reduce-scatter.31.cloned.1.call-done = f32[256,768]{1,0:T(8,128)} async-done(((f32[1024,768]{1,0:T(8,128)}), f32[256,768]{1,0:T(8,128)}) %reduce-scatter.31.cloned.1.call-update) | async-done | bytes 786448 | tf_op jit(solution)/shard_map/reduce_scatter | solution.py:83
  824.9 25.4 %fusion.63 = (f32[3]{0:T(128)}, f32[3]{0:T(128)}, f32[3]{0:T(128)}, f32[3]{0:T(128)}, f32[3]{0:T(128)}, /*index=5*/f32[3]{0:T(128)}, f32[3]{0:T(128)}, f32[3]{0:...) fusion(pred[512,1024]{1,0:T(8,128)(4,1)} %get-tuple-element.354, ...), kind=kLoop, calls=%fused_computation.127 | loop fusion | flops 64487356 | bytes 25178328 | tf_op jit(solution)/shard_map/while/body/eval_jaxpr/reduce_sum | solution.py:192
  855.7 24.7 %fusion.31 = (f32[3]{0:T(128)}, f32[3]{0:T(128)}, f32[3]{0:T(128)}, f32[3]{0:T(128)}, f32[3]{0:T(128)}, /*index=5*/f32[3]{0:T(128)}, f32[3]{0:T(128)}, f32[3]{0:...) fusion(pred[512,1024]{1,0:T(8,128)(4,1)S(1)} %copy-done.86, ...), kind=kLoop, calls=%fused_computation.95 | loop fusion | flops 64487356 | bytes 25178328 | tf_op jit(solution)/shard_map/while/body/eval_jaxpr/reduce_sum | solution.py:192
  1007.9 40.3 %all-reduce = (f32[768]{0:T(1024)}, f32[32,12]{0,1:T(8,128)}, f32[768]{0:T(1024)}, f32[768]{0:T(1024)}) all-reduce(f32[768]{0:T(1024)S(1)} %get-tuple-element.257, f32[32,12]{0,1:T(8,128)S(1)} %broadcast_multiply_fusion, f32[768]{0:T(1024)S(1)} %copy-done.159, ...), channel_id=1, replica_groups=mesh['wide'=8,'narrow'=4] {'wide','narrow'}, use_global_device_ids=true, to_apply=%region_34.35 | all-reduce | flops 2688 | bytes 21504 | tf_op jit(solution)/shard_map/psum | solution.py:397
  1067.2 68.0 %reduce-scatter.51.cloned.1.call-done = f32[96,512]{1,0:T(8,128)} async-done(((f32[768,512]{1,0:T(8,128)}), f32[96,512]{1,0:T(8,128)}) %reduce-scatter.51.cloned.1.call-update) | async-done | bytes 196624 | tf_op jit(solution)/shard_map/reduce_scatter | solution.py:394
  1135.2 67.6 %reduce-scatter.53.cloned.1.call-done = f32[512,96]{0,1:T(8,128)} async-done(((f32[512,768]{0,1:T(8,128)}), f32[512,96]{0,1:T(8,128)}) %reduce-scatter.53.cloned.1.call-update) | async-done | bytes 196624 | tf_op jit(solution)/shard_map/reduce_scatter | solution.py:395
  1202.9 65.6 %reduce-scatter.47.cloned.1.call-done = f32[96,192]{1,0:T(8,128)} async-done(((f32[768,192]{1,0:T(8,128)}), f32[96,192]{1,0:T(8,128)}) %reduce-scatter.47.cloned.1.call-update) | async-done | bytes 73744 | tf_op jit(solution)/shard_map/reduce_scatter | solution.py:389
  1268.5 65.2 %reduce-scatter.59.cloned.1.call-done = f32[96,192]{1,0:T(8,128)} async-done(((f32[768,192]{1,0:T(8,128)}), f32[96,192]{1,0:T(8,128)}) %reduce-scatter.59.cloned.1.call-update) | async-done | bytes 73744
  1333.7 65.8 %reduce-scatter.57.cloned.1.call-done = f32[96,192]{1,0:T(8,128)} async-done(((f32[768,192]{1,0:T(8,128)}), f32[96,192]{1,0:T(8,128)}) %reduce-scatter.57.cloned.1.call-update) | async-done | bytes 73744
  1399.5 30.3 %reduce-scatter.39.cloned.1.call-done = bf16[256,768]{1,0:T(8,128)(2,1)} async-done(((bf16[1024,768]{1,0:T(8,128)(2,1)}), bf16[256,768]{1,0:T(8,128)(2,1)}) %reduce-scatter.39.cloned.1.call-update) | async-done | bytes 393232 | tf_op jit(solution)/shard_map/reduce_scatter | solution.py:339
  1429.8 66.8 %reduce-scatter.41.cloned.1.call-done = f32[96,192]{1,0:T(8,128)} async-done(((f32[768,192]{1,0:T(8,128)}), f32[96,192]{1,0:T(8,128)}) %reduce-scatter.41.cloned.1.call-update) | async-done | bytes 73744 | tf_op jit(solution)/shard_map/reduce_scatter | solution.py:385
  1496.5 65.2 %reduce-scatter.45.cloned.1.call-done = f32[96,192]{1,0:T(8,128)} async-done(((f32[768,192]{1,0:T(8,128)}), f32[96,192]{1,0:T(8,128)}) %reduce-scatter.45.cloned.1.call-update) | async-done | bytes 73744 | tf_op jit(solution)/shard_map/reduce_scatter | solution.py:387
  1561.8 65.7 %reduce-scatter.43.cloned.1.call-done = f32[96,192]{1,0:T(8,128)} async-done(((f32[768,192]{1,0:T(8,128)}), f32[96,192]{1,0:T(8,128)}) %reduce-scatter.43.cloned.1.call-update) | async-done | bytes 73744 | tf_op jit(solution)/shard_map/reduce_scatter | solution.py:386
  (759 shorter events, 325.9 us)
Async XLA Ops:
  7.2 198.4 %all-gather.8.cloned.1.call-start = ((), (), s32[]{:S(2)}) async-start(), calls=%async_computation.18 | async-start | bytes 1966080 | tf_op jit(solution)/shard_map/all_gather | solution.py:263
  11.4 311.2 %reduce-scatter.27.cloned.1.call-start = ((), (), s32[]{:S(2)}) async-start(), calls=%async_computation.19 | async-start | bytes 3932160 | tf_op jit(solution)/shard_map/reduce_scatter | solution.py:83
  31.8 179.5 %copy-start.191 = (f32[3]{0:T(128)}, f32[3]{0:T(128)S(1)}, u32[]{:S(2)}) copy-start(f32[3]{0:T(128)S(1)} %get-tuple-element.278) | copy-start | bytes 40
  31.8 179.5 %copy-start.192 = (f32[3]{0:T(128)}, f32[3]{0:T(128)S(1)}, u32[]{:S(2)}) copy-start(f32[3]{0:T(128)S(1)} %get-tuple-element.279) | copy-start | bytes 40
  31.8 179.5 %copy-start.193 = (f32[3]{0:T(128)}, f32[3]{0:T(128)S(1)}, u32[]{:S(2)}) copy-start(f32[3]{0:T(128)S(1)} %get-tuple-element.280) | copy-start | bytes 40
  63.5 147.9 %copy-start.207 = (f32[3]{0:T(128)}, f32[3]{0:T(128)S(1)}, u32[]{:S(2)}) copy-start(f32[3]{0:T(128)S(1)} %get-tuple-element.262) | copy-start | bytes 40
  63.5 147.9 %copy-start.208 = (f32[3]{0:T(128)}, f32[3]{0:T(128)S(1)}, u32[]{:S(2)}) copy-start(f32[3]{0:T(128)S(1)} %get-tuple-element.263) | copy-start | bytes 40
  205.6 261.1 %copy-start.169 = (f32[3,192]{1,0:T(4,128)}, f32[3,192]{1,0:T(4,128)S(1)}, u32[]{:S(2)}) copy-start(f32[3,192]{1,0:T(4,128)S(1)} %get-tuple-element.387) | copy-start | bytes 6916
  205.6 500.6 %copy-start.127 = (bf16[3,192]{1,0:T(4,128)(2,1)}, bf16[3,192]{1,0:T(4,128)(2,1)S(1)}, u32[]{:S(2)}) copy-start(bf16[3,192]{1,0:T(4,128)(2,1)S(1)} %get-tuple-element.388) | copy-start | bytes 3460
  283.9 167.8 %all-gather.12.cloned.1.call-start = ((), (), s32[]{:S(2)}) async-start(), calls=%async_computation.21 | async-start | bytes 1966080 | tf_op jit(solution)/shard_map/all_gather | solution.py:264
  284.6 170.7 %all-gather.10.cloned.1.call-start = ((), (), s32[]{:S(2)}) async-start(), calls=%async_computation.20 | async-start | bytes 1966080 | tf_op jit(solution)/shard_map/all_gather | solution.py:79
  324.9 185.4 %reduce-scatter.29.cloned.1.call-start = ((), (), s32[]{:S(2)}) async-start(), calls=%async_computation.22 | async-start | bytes 3932160 | tf_op jit(solution)/shard_map/reduce_scatter | solution.py:83
  472.2 145.2 %all-gather.14.cloned.1.call-start = ((), (), s32[]{:S(2)}) async-start(), calls=%async_computation.23 | async-start | bytes 1966080 | tf_op jit(solution)/shard_map/all_gather | solution.py:79
  513.1 110.7 %all-gather.16.cloned.1.call-start = ((), (), s32[]{:S(2)}) async-start(), calls=%async_computation.25 | async-start | bytes 1966080 | tf_op jit(solution)/shard_map/all_gather | solution.py:87
  513.9 159.7 %reduce-scatter.33.cloned.1.call-start = ((), (), s32[]{:S(2)}) async-start(), calls=%async_computation.26 | async-start | bytes 3932160 | tf_op jit(solution)/shard_map/reduce_scatter | solution.py:91
  635.2 62.3 %all-gather.18.cloned.1.call-start = ((), (), s32[]{:S(2)}) async-start(), calls=%async_computation.27 | async-start | bytes 1966080 | tf_op jit(solution)/shard_map/all_gather | solution.py:87
  677.6 76.3 %reduce-scatter.35.cloned.1.call-start = ((), (), s32[]{:S(2)}) async-start(), calls=%async_computation.28 | async-start | bytes 1966080 | tf_op jit(solution)/shard_map/reduce_scatter | solution.py:336
  725.6 68.9 %reduce-scatter.31.cloned.1.call-start = ((), (), s32[]{:S(2)}) async-start(), calls=%async_computation.24 | async-start | bytes 3932160 | tf_op jit(solution)/shard_map/reduce_scatter | solution.py:83
  730.0 87.5 %all-gather.20.cloned.1.call-start = ((), (), s32[]{:S(2)}) async-start(), calls=%async_computation.29 | async-start | bytes 1966080 | tf_op jit(solution)/shard_map/all_gather | solution.py:87
  797.6 156.9 %reduce-scatter.61.cloned.1.call-start = ((), (), s32[]{:S(2)}) async-start(), calls=%async_computation.42 | async-start | bytes 884736
  808.8 196.0 %reduce-scatter.55.cloned.1.call-start = ((), (), s32[]{:S(2)}) async-start(), calls=%async_computation.39 | async-start | bytes 884736
  896.2 110.2 %reduce-scatter.37.cloned.1.call-start = ((), (), s32[]{:S(2)}) async-start(), calls=%async_computation.30 | async-start | bytes 3932160 | tf_op jit(solution)/shard_map/reduce_scatter | solution.py:91
  904.7 162.5 %reduce-scatter.49.cloned.1.call-start = ((), (), s32[]{:S(2)}) async-start(), calls=%async_computation.36 | async-start | bytes 1769472 | tf_op jit(solution)/shard_map/reduce_scatter | solution.py:393
  909.5 225.7 %reduce-scatter.51.cloned.1.call-start = ((), (), s32[]{:S(2)}) async-start(), calls=%async_computation.37 | async-start | bytes 1769472 | tf_op jit(solution)/shard_map/reduce_scatter | solution.py:394
  913.5 289.4 %reduce-scatter.53.cloned.1.call-start = ((), (), s32[]{:S(2)}) async-start(), calls=%async_computation.38 | async-start | bytes 1769472 | tf_op jit(solution)/shard_map/reduce_scatter | solution.py:395
  917.6 350.9 %reduce-scatter.47.cloned.1.call-start = ((), (), s32[]{:S(2)}) async-start(), calls=%async_computation.35 | async-start | bytes 884736 | tf_op jit(solution)/shard_map/reduce_scatter | solution.py:389
  920.2 413.5 %reduce-scatter.59.cloned.1.call-start = ((), (), s32[]{:S(2)}) async-start(), calls=%async_computation.41 | async-start | bytes 884736
  932.3 467.1 %reduce-scatter.57.cloned.1.call-start = ((), (), s32[]{:S(2)}) async-start(), calls=%async_computation.40 | async-start | bytes 884736
  938.0 491.8 %reduce-scatter.39.cloned.1.call-start = ((), (), s32[]{:S(2)}) async-start(), calls=%async_computation.31 | async-start | bytes 1966080 | tf_op jit(solution)/shard_map/reduce_scatter | solution.py:339
  941.6 554.9 %reduce-scatter.41.cloned.1.call-start = ((), (), s32[]{:S(2)}) async-start(), calls=%async_computation.32 | async-start | bytes 884736 | tf_op jit(solution)/shard_map/reduce_scatter | solution.py:385
  943.2 618.6 %reduce-scatter.45.cloned.1.call-start = ((), (), s32[]{:S(2)}) async-start(), calls=%async_computation.34 | async-start | bytes 884736 | tf_op jit(solution)/shard_map/reduce_scatter | solution.py:387
  948.9 678.5 %reduce-scatter.43.cloned.1.call-start = ((), (), s32[]{:S(2)}) async-start(), calls=%async_computation.33 | async-start | bytes 884736 | tf_op jit(solution)/shard_map/reduce_scatter | solution.py:386
  (229 other events, 3573.7 us)
Sparse Core Ops, SparseCore 0:
  11.5 22.3 all-gather.7
  284.0 38.5 reduce-scatter.26
  324.2 19.6 all-gather.11
  345.4 19.6 all-gather.9
  472.3 37.9 reduce-scatter.28
  513.3 19.6 all-gather.13
  534.5 19.6 all-gather.15
  635.3 38.2 reduce-scatter.32
  677.7 19.6 all-gather.17
  725.8 28.1 reduce-scatter.34
  756.5 37.9 reduce-scatter.30
  797.7 19.6 all-gather.19
  821.1 62.4 reduce-scatter.60
  896.3 62.4 reduce-scatter.54
  961.4 36.9 reduce-scatter.36
  1002.2 64.9 reduce-scatter.48
  1071.5 63.7 reduce-scatter.50
  1139.1 63.7 reduce-scatter.52
  1207.1 61.3 reduce-scatter.46
  1272.2 61.4 reduce-scatter.58
  1337.9 61.4 reduce-scatter.56
  1402.6 27.1 reduce-scatter.38
  1434.0 62.4 reduce-scatter.40
  1500.2 61.4 reduce-scatter.44
  1566.0 61.4 reduce-scatter.42
where the time goes:
time: 1640 us; the launch traced here: 1630 us
  waiting for transfers between devices  781 us (48%)
  blocking collectives  401 us (24%)
  other arithmetic  202 us (12%)
  matrix products  192 us (12%)
  local copies, waits for them, and re-layouts  39.4 us (2%)
  between operations  17.2 us (1%)
    unnamed x29, waiting for transfers between devices  133 us
    reduce_scatter x3, waiting for transfers between devices, add_branch(): lax.psum_scatter(partial_value, 'narrow', scatter_dimension=0, tiled=True)  115 us
    reduce_sum x4, other arithmetic, attend_backward(): found[which] = jnp.sum(jnp.where(inside, scores_wide, 0.0), axis=(1, 2))  78.6 us
    reduce_scatter x1, waiting for transfers between devices, shards(): lax.psum_scatter(grad_w_up, 'wide', scatter_dimension=0, tiled=True)  68 us
    reduce_scatter x1, waiting for transfers between devices, shards(): lax.psum_scatter(grad_down, 'wide', scatter_dimension=1, tiled=True)  67.6 us
    reduce_scatter x1, waiting for transfers between devices, shards(): lax.psum_scatter(grad_query_self, 'wide', scatter_dimension=0, tiled=True)  66.8 us
    reduce_scatter x1, waiting for transfers between devices, shards(): lax.psum_scatter(grad_key_self, 'wide', scatter_dimension=0, tiled=True)  65.7 us
    reduce_scatter x1, waiting for transfers between devices, shards(): lax.psum_scatter(grad_query_cross, 'wide', scatter_dimension=0, tiled=True)  65.6 us
  transfers between devices with their start and end apart: 25, of which 17 were waited for; matrix products, arithmetic and copies ran while one was open for 17% of the time, Pallas kernels for 0%

commit v1 on v0

v1 whole, which is shorter than its diff:
```python
import functools
import math

import jax
import jax.numpy as jnp
import numpy as np
from jax import lax
from jax.experimental import pallas as pl
from jax.experimental.pallas import tpu as pltpu
from jax.sharding import PartitionSpec as P

DH = 64
NB = 32
MAX_DIST = 128
EPS = 1e-06
NEG = -1e30
QB = 256
ROW_CHUNKS = 4
MESH = pl.DeviceIdType.MESH
F32 = jnp.float32
BF16 = jnp.bfloat16


def bucket_table(length, buckets, reach):
    exact_part = buckets // 2
    distance = np.arange(length)
    spread = (
        np.log(np.maximum(distance, exact_part) / exact_part)
        / np.log(reach / exact_part)
        * (buckets - exact_part)
    )
    far_bucket = np.minimum(exact_part + np.floor(spread).astype(np.int64), buckets - 1)
    return np.where(distance < exact_part, distance, far_bucket).astype(np.int32)


class Spot:
    def __init__(self, wide_split):
        n = lax.axis_index("narrow")
        self.n = n
        self.x = n // 2
        self.c = n % 2
        self.sib = self.x * 2 + (1 - self.c)
        self.xp = (1 - self.x) * 2 + self.c
        self.xsib = (1 - self.x) * 2 + (1 - self.c)
        self.wide_split = wide_split
        if wide_split:
            w = lax.axis_index("wide")
            self.w = w
            self.z = w // 2
            self.y = w % 2
            self.yp = self.z * 2 + (1 - self.y)

    def at_n(self, n):
        return {"narrow": n}

    def at_w(self, w):
        return {"wide": w}


def remote(src, dst, send, recv, dev):
    return pltpu.make_async_remote_copy(
        src_ref=src, dst_ref=dst, send_sem=send, recv_sem=recv, device_id=dev, device_id_type=MESH
    )


def greet(spot, use_zy, use_all_z=False):
    barrier = pltpu.get_barrier_semaphore()

    def hello(dev):
        pl.semaphore_signal(barrier, inc=1, device_id=dev, device_id_type=MESH)

    hello(spot.at_n(spot.sib))
    hello(spot.at_n(spot.xp))
    count = 2
    if use_zy:
        hello(spot.at_w(spot.yp))
        count = count + 1
        if use_all_z:
            for step in range(1, 4):
                hello(spot.at_w(((spot.z + step) % 4) * 2 + spot.y))
            count = count + 3
        else:

            @pl.when(spot.z > 0)
            def _():
                hello(spot.at_w(spot.w - 2))

            @pl.when(spot.z < 3)
            def _():
                hello(spot.at_w(spot.w + 2))

            inner = jnp.where(jnp.logical_and(spot.z > 0, spot.z < 3), 1, 0)
            count = count + 1 + inner
    pl.semaphore_wait(barrier, count)


class RowGather:
    def __init__(self, name, chunks=ROW_CHUNKS):
        self.name = name
        self.chunks = chunks

    def need(self, scratch):
        dma = pltpu.SemaphoreType.DMA((self.chunks,))
        for part in ("xs", "xr", "ss", "sr", "fs", "fr", "lo"):
            scratch[self.name + part] = dma

    def bind(self, env, spot, src, full):
        self.env, self.spot, self.src, self.full = env, spot, src, full
        self.size = src.shape[0] // self.chunks

    def sem(self, part, k):
        return self.env[self.name + part].at[k]

    def rows(self, k):
        return pl.ds(k * self.size, self.size)

    def to_x(self, k):
        s = self.spot
        return remote(
            self.src.at[self.rows(k)],
            self.full.at[s.n, self.rows(k)],
            self.sem("xs", k),
            self.sem("xr", k),
            s.at_n(s.xp),
        )

    def to_sib(self, k):
        s = self.spot
        return remote(
            self.src.at[self.rows(k)],
            self.full.at[s.n, self.rows(k)],
            self.sem("ss", k),
            self.sem("sr", k),
            s.at_n(s.sib),
        )

    def onward(self, k):
        s = self.spot
        here = self.full.at[s.xp, self.rows(k)]
        return remote(here, here, self.sem("fs", k), self.sem("fr", k), s.at_n(s.sib))

    def local(self, k):
        return pltpu.make_async_copy(
            self.src.at[self.rows(k)],
            self.full.at[self.spot.n, self.rows(k)],
            self.sem("lo", k),
        )

    def send(self, k):
        self.to_x(k).start()
        self.to_sib(k).start()
        self.local(k).start()

    def forward(self, k):
        self.to_x(k).wait_recv()
        self.onward(k).start()

    def finish(self):
        for k in range(self.chunks):
            self.to_sib(k).wait_recv()
            self.onward(k).wait_recv()
            self.to_x(k).wait_send()
            self.to_sib(k).wait_send()
            self.onward(k).wait_send()
            self.local(k).wait()


class RowReduce:
    def __init__(self, name, rows, cols, chunks=ROW_CHUNKS):
        self.name, self.nrows, self.ncols, self.chunks = name, rows, cols, chunks

    def need(self, scratch):
        dma = pltpu.SemaphoreType.DMA((self.chunks,))
        for part in ("as", "ar", "bs", "br", "xs", "xr"):
            scratch[self.name + part] = dma
        shape = (self.nrows, self.ncols)
        for part in ("fars", "owns", "out", "inn"):
            scratch[self.name + part] = pltpu.VMEM(shape, BF16)

    def bind(self, env, spot, part):
        self.env, self.spot, self.part = env, spot, part
        self.size = self.nrows // self.chunks

    def sem(self, part, k):
        return self.env[self.name + part].at[k]

    def rows(self, k):
        return pl.ds(k * self.size, self.size)

    def buf(self, part, k):
        return self.env[self.name + part].at[self.rows(k)]

    def far_sib(self, k):
        s = self.spot
        return remote(
            self.part.at[s.xsib, self.rows(k)],
            self.buf("fars", k),
            self.sem("as", k),
            self.sem("ar", k),
            s.at_n(s.sib),
        )

    def own_sib(self, k):
        s = self.spot
        return remote(
            self.part.at[s.sib, self.rows(k)],
            self.buf("owns", k),
            self.sem("bs", k),
            self.sem("br", k),
            s.at_n(s.sib),
        )

    def across(self, k):
        s = self.spot
        return remote(
            self.buf("out", k), self.buf("inn", k), self.sem("xs", k), self.sem("xr", k), s.at_n(s.xp)
        )

    def open(self):
        for k in range(self.chunks):
            self.far_sib(k).start()
        for k in range(self.chunks):
            self.own_sib(k).start()

    def cross(self, k):
        self.far_sib(k).wait_recv()
        mine = self.part[self.spot.xp, self.rows(k), :].astype(F32)
        self.buf("out", k)[...] = (mine + self.buf("fars", k)[...].astype(F32)).astype(BF16)
        self.across(k).start()

    def total(self, k):
        self.own_sib(k).wait_recv()
        self.across(k).wait_recv()
        mine = self.part[self.spot.n, self.rows(k), :].astype(F32)
        return (mine + self.buf("owns", k)[...].astype(F32)) + self.buf("inn", k)[...].astype(F32)

    def finish(self):
        for k in range(self.chunks):
            self.far_sib(k).wait_send()
            self.own_sib(k).wait_send()
            self.across(k).wait_send()


class WideGather:
    def __init__(self, name, halves=2):
        self.name, self.halves = name, halves

    def need(self, scratch):
        h = self.halves
        scratch[self.name + "rs"] = pltpu.SemaphoreType.DMA((4, h))
        scratch[self.name + "ls"] = pltpu.SemaphoreType.DMA((4, h))
        scratch[self.name + "ys"] = pltpu.SemaphoreType.DMA((7, h))
        scratch[self.name + "rv"] = pltpu.SemaphoreType.DMA((8, h))
        scratch[self.name + "lo"] = pltpu.SemaphoreType.DMA

    def bind(self, env, spot, src, full):
        self.env, self.spot, self.src, self.full = env, spot, src, full
        self.size = src.shape[0] // self.halves

    def hop(self, kind, k, slab, half, own):
        s = self.spot
        dev = {"rs": s.w + 2, "ls": s.w - 2, "ys": s.yp}[kind]
        rows = pl.ds(half * self.size, self.size)
        src = self.src.at[rows] if own else self.full.at[slab, rows]
        return remote(
            src,
            self.full.at[slab, rows],
            self.env[self.name + kind].at[k, half],
            self.env[self.name + "rv"].at[slab, half],
            s.at_w(dev),
        )

    def own_copy(self):
        return pltpu.make_async_copy(
            self.src, self.full.at[self.spot.w], self.env[self.name + "lo"]
        )

    def open(self):
        s = self.spot
        self.own_copy().start()

        @pl.when(s.z < 3)
        def _():
            for half in range(self.halves):
                self.hop("rs", 0, s.w, half, True).start()

        @pl.when(s.z > 0)
        def _():
            for half in range(self.halves):
                self.hop("ls", 0, s.w, half, True).start()

        for half in range(self.halves):
            self.hop("ys", 0, s.w, half, True).start()

    def step(self, k):
        s = self.spot

        @pl.when(s.z - k >= 0)
        def _():
            slab = s.w - 2 * k
            for half in range(self.halves):
                self.hop("rs", k, slab, half, False).wait_recv()

                @pl.when(s.z < 3)
                def _():
                    self.hop("rs", k, slab, half, False).start()

                self.hop("ys", k, slab, half, False).start()

        @pl.when(s.z + k <= 3)
        def _():
            slab = s.w + 2 * k
            for half in range(self.halves):
                self.hop("ls", k, slab, half, False).wait_recv()

                @pl.when(s.z > 0)
                def _():
                    self.hop("ls", k, slab, half, False).start()

                self.hop("ys", 3 + k, slab, half, False).start()

    def finish(self):
        s = self.spot
        self.own_copy().wait()
        for half in range(self.halves):
            for zo in range(4):
                self.hop("ys", 0, zo * 2 + (1 - s.y), half, False).wait_recv()
            self.hop("ys", 0, s.w, half, False).wait_send()

            @pl.when(s.z < 3)
            def _():
                self.hop("rs", 0, s.w, half, False).wait_send()

            @pl.when(s.z > 0)
            def _():
                self.hop("ls", 0, s.w, half, False).wait_send()

            for k in range(1, 4):

                @pl.when(s.z - k >= 0)
                def _():
                    @pl.when(s.z < 3)
                    def _():
                        self.hop("rs", k, s.w - 2 * k, half, False).wait_send()

                    self.hop("ys", k, s.w - 2 * k, half, False).wait_send()

                @pl.when(s.z + k <= 3)
                def _():
                    @pl.when(s.z > 0)
                    def _():
                        self.hop("ls", k, s.w + 2 * k, half, False).wait_send()

                    self.hop("ys", 3 + k, s.w + 2 * k, half, False).wait_send()


class WideReduce:
    def __init__(self, name, rows, cols):
        self.name, self.nrows, self.ncols = name, rows, cols

    def need(self, scratch):
        for part in ("ys", "yr", "rs", "rr", "ls", "lr"):
            scratch[self.name + part] = pltpu.SemaphoreType.DMA((4,))
        shape = (4, self.nrows, self.ncols)
        for part in ("yin", "acc", "rin", "rout", "lin", "lout"):
            scratch[self.name + part] = pltpu.VMEM(shape, BF16)

    def bind(self, env, spot, part):
        self.env, self.spot, self.part = env, spot, part

    def buf(self, part, d):
        return self.env[self.name + part].at[d]

    def sem(self, part, d):
        return self.env[self.name + part].at[d]

    def over_y(self, d):
        s = self.spot
        return remote(
            self.part.at[d * 2 + (1 - s.y)],
            self.buf("yin", d),
            self.sem("ys", d),
            self.sem("yr", d),
            s.at_w(s.yp),
        )

    def right(self, d, first):
        src = self.buf("acc" if first else "rout", d)
        return remote(
            src, self.buf("rin", d), self.sem("rs", d), self.sem("rr", d), self.spot.at_w(self.spot.w + 2)
        )

    def left(self, d, first):
        src = self.buf("acc" if first else "lout", d)
        return remote(
            src, self.buf("lin", d), self.sem("ls", d), self.sem("lr", d), self.spot.at_w(self.spot.w - 2)
        )

    def open(self):
        for d in (3, 0, 2, 1):
            self.over_y(d).start()

    def first(self, d):
        s = self.spot
        self.over_y(d).wait_recv()
        mine = self.part[d * 2 + s.y].astype(F32)
        self.buf("acc", d)[...] = (mine + self.buf("yin", d)[...].astype(F32)).astype(BF16)
        if d > 0:

            @pl.when(s.z == 0)
            def _():
                self.right(d, True).start()

        if d < 3:

            @pl.when(s.z == 3)
            def _():
                self.left(d, True).start()

    def chain_right(self, d):
        s = self.spot

        @pl.when(jnp.logical_and(s.z > 0, s.z < d))
        def _():
            self.right(d, False).wait_recv()
            self.buf("rout", d)[...] = (
                self.buf("rin", d)[...].astype(F32) + self.buf("acc", d)[...].astype(F32)
            ).astype(BF16)
            self.right(d, False).start()

    def chain_left(self, d):
        s = self.spot

        @pl.when(jnp.logical_and(s.z < 3, s.z > d))
        def _():
            self.left(d, False).wait_recv()
            self.buf("lout", d)[...] = (
                self.buf("lin", d)[...].astype(F32) + self.buf("acc", d)[...].astype(F32)
            ).astype(BF16)
            self.left(d, False).start()

    def total(self, out):
        s = self.spot
        for d in range(4):

            @pl.when(s.z == d)
            def _():
                value = self.buf("acc", d)[...].astype(F32)
                if d > 0:
                    self.right(d, False).wait_recv()
                    value = value + self.buf("rin", d)[...].astype(F32)
                if d < 3:
                    self.left(d, False).wait_recv()
                    value = value + self.buf("lin", d)[...].astype(F32)
                out[...] = value

    def finish(self):
        s = self.spot
        for d in range(4):
            self.over_y(d).wait_send()

            @pl.when(s.z < d)
            def _():
                self.right(d, False).wait_send()

            @pl.when(s.z > d)
            def _():
                self.left(d, False).wait_send()


class SmallSum:
    def __init__(self, name, rows, cols):
        self.name, self.shape = name, (rows, cols)

    def need(self, scratch):
        for part in ("s", "r"):
            scratch[self.name + part] = pltpu.SemaphoreType.DMA((3,))
        scratch[self.name + "zs"] = pltpu.SemaphoreType.DMA((4,))
        scratch[self.name + "zr"] = pltpu.SemaphoreType.DMA((4,))
        scratch[self.name + "v"] = pltpu.VMEM((4,) + self.shape, F32)
        scratch[self.name + "in"] = pltpu.VMEM((3,) + self.shape, F32)
        scratch[self.name + "z"] = pltpu.VMEM((4,) + self.shape, F32)

    def run(self, env, spot, value, out):
        held, inn, zin = env[self.name + "v"], env[self.name + "in"], env[self.name + "z"]
        held[0] = value
        devs = (spot.at_n(spot.sib), spot.at_n(spot.xp), spot.at_w(spot.yp))
        copies = []
        for i in range(3):
            copy = remote(
                held.at[i], inn.at[i], env[self.name + "s"].at[i], env[self.name + "r"].at[i], devs[i]
            )
            copy.start()
            copies.append(copy)
            copy.wait_recv()
            held[i + 1] = held[i] + inn[i]
        zin[spot.z] = held[3]

        def hop(step):
            other = (spot.z + step) % 4
            return remote(
                held.at[3],
                zin.at[spot.z],
                env[self.name + "zs"].at[step],
                env[self.name + "zr"].at[spot.z],
                spot.at_w(other * 2 + spot.y),
            )

        def came(step):
            other = (spot.z + step) % 4
            return remote(
                held.at[3],
                zin.at[other],
                env[self.name + "zs"].at[step],
                env[self.name + "zr"].at[other],
                spot.at_w(other * 2 + spot.y),
            )

        for step in range(1, 4):
            hop(step).start()
        for step in range(1, 4):
            came(step).wait_recv()
        out[...] = ((zin[0] + zin[1]) + zin[2]) + zin[3]
        for copy in copies:
            copy.wait_send()
        for step in range(1, 4):
            hop(step).wait_send()


VM = pltpu.VMEM
ANY = pl.ANY


def call(body, inputs, outputs, scratch, cid, name):
    in_names, out_names, scr_names = list(inputs), list(outputs), list(scratch)

    def kernel(*refs):
        body(dict(zip(in_names + out_names + scr_names, refs)))

    results = pl.pallas_call(
        kernel,
        out_shape=[jax.ShapeDtypeStruct(outputs[k][0], outputs[k][1]) for k in out_names],
        in_specs=[pl.BlockSpec(memory_space=inputs[k][1]) for k in in_names],
        out_specs=[pl.BlockSpec(memory_space=outputs[k][2]) for k in out_names],
        scratch_shapes=[scratch[k] for k in scr_names],
        compiler_params=pltpu.CompilerParams(
            collective_id=cid, has_side_effects=True, vmem_limit_bytes=60 * 1024 * 1024
        ),
        name=name,
    )(*[inputs[k][0] for k in in_names])
    return dict(zip(out_names, results))


def mean_square(values):
    return jnp.mean(values * values, axis=-1, keepdims=True)


def norm_rows(values, gain):
    return values * lax.rsqrt(mean_square(values) + EPS) * gain


def norm_back(values, gain, dn):
    r = lax.rsqrt(mean_square(values) + EPS)
    u = values * r
    dg = dn * gain
    rows = r * (dg - u * jnp.mean(dg * u, axis=-1, keepdims=True))
    return rows, jnp.sum(dn * u, axis=0, keepdims=True)


def first_gather(inputs, memory, gain, shard, zy):
    rows, cols = inputs.shape
    scratch = {"own": pltpu.VMEM((rows, cols), BF16)}
    ga, gm, wg = RowGather("ga"), RowGather("gm"), WideGather("wg")
    tasks = [ga, gm] + ([wg] if zy else [])
    for t in tasks:
        t.need(scratch)
    ins = {"x": (inputs, VM), "m": (memory, VM), "g": (gain, VM)}
    outs = {"full": ((4, rows, cols), BF16, ANY), "mem": ((4, rows, cols), BF16, ANY)}
    if zy:
        ins["w"] = (shard, VM)
        outs["wf"] = ((8,) + shard.shape, BF16, ANY)

    def body(env):
        spot = Spot(zy)
        greet(spot, zy)
        ga.bind(env, spot, env["own"], env["full"])
        gm.bind(env, spot, env["m"], env["mem"])
        if zy:
            wg.bind(env, spot, env["w"], env["wf"])
            wg.open()
        for k in range(ga.chunks):
            part = env["x"][ga.rows(k), :].astype(F32)
            env["own"][ga.rows(k), :] = norm_rows(part, env["g"][...]).astype(BF16)
            ga.send(k)
        for k in range(gm.chunks):
            gm.send(k)
        for k in range(ga.chunks):
            ga.forward(k)
            if zy and k in (1, 3):
                wg.step((k + 1) // 2)
        for k in range(gm.chunks):
            gm.forward(k)
            if zy and k == 0:
                wg.step(3)
        ga.finish()
        gm.finish()
        if zy:
            wg.finish()

    return call(body, ins, outs, scratch, 0, "gather_first")


def forward_phase(part, x_rows, gain, shard, zy, extra, cid, name):
    rows, cols = x_rows.shape
    scratch = {"own": pltpu.VMEM((rows, cols), BF16)}
    rr, ga, wg, ge = RowReduce("rr", rows, cols), RowGather("ga"), WideGather("wg"), RowGather("ge")
    tasks = [rr, ga] + ([wg] if zy else []) + ([ge] if extra is not None else [])
    for t in tasks:
        t.need(scratch)
    ins = {"p": (part, VM), "x": (x_rows, VM), "g": (gain, VM)}
    outs = {"sum": ((rows, cols), F32, VM), "full": ((4, rows, cols), BF16, ANY)}
    if zy:
        ins["w"] = (shard, VM)
        outs["wf"] = ((8,) + shard.shape, BF16, ANY)
    if extra is not None:
        ins["e"] = (extra, VM)
        outs["ef"] = ((4, rows, cols), BF16, ANY)

    def body(env):
        spot = Spot(zy)
        greet(spot, zy)
        rr.bind(env, spot, env["p"])
        ga.bind(env, spot, env["own"], env["full"])
        if zy:
            wg.bind(env, spot, env["w"], env["wf"])
            wg.open()
        rr.open()
        for k in range(rr.chunks):
            rr.cross(k)
        for k in range(rr.chunks):
            value = env["x"][rr.rows(k), :].astype(F32) + rr.total(k)
            env["sum"][rr.rows(k), :] = value
            env["own"][rr.rows(k), :] = norm_rows(value, env["g"][...]).astype(BF16)
            ga.send(k)
            if zy and k in (0, 2):
                wg.step(k // 2 + 1)
        if extra is not None:
            ge.bind(env, spot, env["e"], env["ef"])
            for k in range(ge.chunks):
                ge.send(k)
        for k in range(ga.chunks):
            ga.forward(k)
            if zy and k == 0:
                wg.step(3)
        if extra is not None:
            for k in range(ge.chunks):
                ge.forward(k)
            ge.finish()
        rr.finish()
        ga.finish()
        if zy:
            wg.finish()

    return call(body, ins, outs, scratch, cid, name)


def backward_phase(part, values, gain, res, grads, zy, extra, extra_base, last, small, cid, name):
    rows, cols = values.shape
    scratch = {}
    rr = RowReduce("rr", rows, cols)
    ga, re = RowGather("ga"), RowReduce("re", rows, cols)
    tasks = [rr]
    ins = {"p": (part, VM), "v": (values, VM), "g": (gain, VM), "res": (res, VM)}
    outs = {"gg": ((1, cols), F32, VM)}
    if last:
        outs["gx"] = ((rows, cols), BF16, VM)
    else:
        tasks.append(ga)
        scratch["own"] = pltpu.VMEM((rows, cols), BF16)
        outs["sum"] = ((rows, cols), F32, VM)
        outs["full"] = ((4, rows, cols), BF16, ANY)
    if zy:
        wr = WideReduce("wr", grads.shape[1], grads.shape[2])
        tasks.append(wr)
        ins["w"] = (grads, VM)
        outs["wg"] = (grads.shape[1:], F32, VM)
    if extra is not None:
        tasks.append(re)
        ins["e"] = (extra, VM)
        outs["eo"] = ((rows, cols), BF16, VM)
        if extra_base is not None:
            ins["eb"] = (extra_base, VM)
    if small is not None and zy:
        ss = SmallSum("ss", *small.shape)
        tasks.append(ss)
        ins["small"] = (small, VM)
        outs["tot"] = (small.shape, F32, VM)
    for t in tasks:
        t.need(scratch)

    def body(env):
        spot = Spot(zy)
        greet(spot, zy, small is not None)
        rr.bind(env, spot, env["p"])
        if zy:
            wr.bind(env, spot, env["w"])
            wr.open()
        rr.open()
        for k in range(rr.chunks):
            rr.cross(k)
        if not last:
            ga.bind(env, spot, env["own"], env["full"])
        if extra is not None:
            re.bind(env, spot, env["e"])
            re.open()
        order = (3, 0, 2, 1)
        gain_sum = jnp.zeros((1, cols), F32)
        for k in range(rr.chunks):
            dn = rr.total(k)
            add, gsum = norm_back(env["v"][rr.rows(k), :].astype(F32), env["g"][...], dn)
            gain_sum = gain_sum + gsum
            value = env["res"][rr.rows(k), :].astype(F32) + add
            if last:
                env["gx"][rr.rows(k), :] = value.astype(BF16)
            else:
                env["sum"][rr.rows(k), :] = value
                env["own"][rr.rows(k), :] = value.astype(BF16)
                ga.send(k)
            if zy:
                wr.first(order[k])
        env["gg"][...] = gain_sum
        if extra is not None:
            for k in range(re.chunks):
                re.cross(k)
        hops = [
            (wr.chain_right, 3),
            (wr.chain_left, 0),
            (wr.chain_right, 2),
            (wr.chain_left, 1),
        ] if zy else []
        if not last:
            for k in range(ga.chunks):
                ga.forward(k)
                if hops:
                    fn, d = hops.pop(0)
                    fn(d)
        for fn, d in hops:
            fn(d)
        if small is not None and zy:
            row = lax.broadcasted_iota(jnp.int32, small.shape, 0)
            value = jnp.where(row == 0, jnp.broadcast_to(gain_sum, small.shape), env["small"][...])
            ss.run(env, spot, value, env["tot"])
        if extra is not None:
            for k in range(re.chunks):
                value = re.total(k)
                if extra_base is not None:
                    value = env["eb"][re.rows(k), :] + value
                env["eo"][re.rows(k), :] = value.astype(BF16)
            re.finish()
        if zy:
            wr.total(env["wg"])
            wr.finish()
        rr.finish()
        if not last:
            ga.finish()

    return call(body, ins, outs, scratch, cid, name)


def nt(left, right):
    return lax.dot_general(left, right, (((1,), (1,)), ((), ())), preferred_element_type=F32)


def nn(left, right):
    return lax.dot_general(left, right, (((1,), (0,)), ((), ())), preferred_element_type=F32)


def tn(left, right):
    return lax.dot_general(left, right, (((0,), (0,)), ((), ())), preferred_element_type=F32)


def head_rows(values, h):
    lane = lax.broadcasted_iota(jnp.int32, values.shape, 1)
    return jnp.where(lane // DH == h, values, jnp.zeros_like(values))


def make_toeplitz(bias_ref, near_ref, heads):
    for h in range(heads):
        row = jnp.broadcast_to(bias_ref[h], (QB, 2 * QB))
        near_ref[h] = pltpu.roll(row, 0, 1, stride=1, stride_axis=0)


def diagonal_sums(tile):
    rows, width = tile.shape
    while rows > 1:
        rows = rows // 2
        tile = tile[:rows] + pltpu.roll(tile[rows:], width - rows, 1)
    return tile


def fill_mask(mask_ref, segk_ref, segq_ref, qb, nk, causal):
    sq = segq_ref[:, qb * QB : (qb + 1) * QB]
    for first in range(0, nk, QB):
        sk = segk_ref[first : first + QB, :]
        sk = jnp.concatenate([sk] * (QB // sk.shape[1]), axis=1)
        ok = sk == sq
        if causal and first == qb * QB:
            j = lax.broadcasted_iota(jnp.int32, (QB, QB), 0)
            i = lax.broadcasted_iota(jnp.int32, (QB, QB), 1)
            ok = jnp.logical_and(ok, j <= i)
        mask_ref[first : first + QB, :] = jnp.where(ok, 0.0, NEG)


def score_tiles(k_ref, qh, mask_ref, near_ref, far_ref, h, qb, nk, causal):
    tiles = []
    for first in range(0, nk, QB):
        s = nt(k_ref[first : first + QB, :], qh) + mask_ref[first : first + QB, :]
        if causal:
            back = qb - first // QB
            if back == 0:
                s = s + near_ref[h][:, 0:QB]
            elif back == 1:
                s = s + near_ref[h][:, QB : 2 * QB]
            else:
                s = s + far_ref[h]
        tiles.append(s)
    return tiles


def attend_fwd(q, k, vt, segq, segk, bias):
    length, columns = q.shape
    keys = k.shape[0]
    heads = columns // DH
    causal = bias is not None

    def kernel(*refs):
        if causal:
            q_ref, k_ref, vt_ref, sq_ref, sk_ref, b_ref, far_ref, ctx_ref, lse_ref, mask_ref, near_ref = refs
            make_toeplitz(b_ref, near_ref, heads)
        else:
            q_ref, k_ref, vt_ref, sq_ref, sk_ref, ctx_ref, lse_ref, mask_ref = refs
            near_ref = far_ref = None
        for qb in range(length // QB):
            nk = (qb + 1) * QB if causal else keys
            cols = slice(qb * QB, (qb + 1) * QB)
            fill_mask(mask_ref, sk_ref, sq_ref, qb, nk, causal)

            def one(h, carry):
                qh = head_rows(q_ref[cols, :], h)
                tiles = score_tiles(k_ref, qh, mask_ref, near_ref, far_ref, h, qb, nk, causal)
                peak = functools.reduce(
                    jnp.maximum, [jnp.max(t, axis=0, keepdims=True) for t in tiles]
                )
                total = jnp.zeros((1, QB), F32)
                acc = jnp.zeros((DH, QB), F32)
                hrows = pl.ds(pl.multiple_of(h * DH, DH), DH)
                for i, t in enumerate(tiles):
                    e = jnp.exp(t - peak)
                    total = total + jnp.sum(e, axis=0, keepdims=True)
                    acc = acc + nn(vt_ref[hrows, i * QB : (i + 1) * QB], e.astype(BF16))
                ctx_ref[hrows, cols] = (acc / total).astype(BF16)
                lse_ref[h, :, cols] = peak + jnp.log(total)
                return carry

            lax.fori_loop(0, heads, one, 0)

    args = [q, k, vt, segq, segk]
    specs = [pl.BlockSpec(memory_space=VM)] * 5
    scratch = [pltpu.VMEM((keys, QB), F32)]
    if causal:
        args += [bias[0], bias[1]]
        specs += [pl.BlockSpec(memory_space=VM), pl.BlockSpec(memory_space=pltpu.SMEM)]
        scratch.append(pltpu.VMEM((heads, QB, 2 * QB), F32))
    return pl.pallas_call(
        kernel,
        out_shape=[
            jax.ShapeDtypeStruct((columns, length), BF16),
            jax.ShapeDtypeStruct((heads, 1, length), F32),
        ],
        in_specs=specs,
        out_specs=[pl.BlockSpec(memory_space=VM)] * 2,
        scratch_shapes=scratch,
        name="self_fwd" if causal else "cross_fwd",
    )(*args)


def attend_bwd(q, k, kt, v, dctx, segq, segk, lse, bias):
    length, columns = q.shape
    keys = k.shape[0]
    heads = columns // DH
    causal = bias is not None

    def kernel(*refs):
        q_ref, k_ref, kt_ref, v_ref, d_ref, sq_ref, sk_ref, lse_ref = refs[:8]
        refs = refs[8:]
        if causal:
            b_ref, far_ref = refs[:2]
            refs = refs[2:]
            dq_ref, dk_ref, dv_ref, gn_ref, gf_ref = refs[:5]
            dka, dva, mask_ref, near_ref, gnear = refs[5:]
            make_toeplitz(b_ref, near_ref, heads)
            gnear[...] = jnp.zeros_like(gnear)
            gf_ref[...] = jnp.zeros_like(gf_ref)
        else:
            dq_ref, dk_ref, dv_ref, dka, dva, mask_ref = refs
            near_ref = far_ref = None
        dka[...] = jnp.zeros_like(dka)
        dva[...] = jnp.zeros_like(dva)
        for qb in range(length // QB):
            nk = (qb + 1) * QB if causal else keys
            cols = slice(qb * QB, (qb + 1) * QB)
            fill_mask(mask_ref, sk_ref, sq_ref, qb, nk, causal)

            def one(h, carry):
                qh = head_rows(q_ref[cols, :], h)
                dh = head_rows(d_ref[cols, :], h)
                lrow = lse_ref[h, :, cols]
                tiles = score_tiles(k_ref, qh, mask_ref, near_ref, far_ref, h, qb, nk, causal)
                probs, dps = [], []
                delta = jnp.zeros((1, QB), F32)
                for i, t in enumerate(tiles):
                    p = jnp.exp(t - lrow)
                    dp = nt(v_ref[i * QB : (i + 1) * QB, :], dh)
                    delta = delta + jnp.sum(p * dp, axis=0, keepdims=True)
                    dva[i * QB : (i + 1) * QB, :] += nn(p.astype(BF16), dh)
                    probs.append(p)
                    dps.append(dp)
                hrows = pl.ds(pl.multiple_of(h * DH, DH), DH)
                acc = jnp.zeros((DH, QB), F32)
                far_sum = jnp.zeros((1, QB), F32)
                for i, (p, dp) in enumerate(zip(probs, dps)):
                    ds = p * (dp - delta)
                    low = ds.astype(BF16)
                    if causal:
                        back = qb - i
                        if back == 0:
                            gnear[h, :, 0:QB] += ds
                        elif back == 1:
                            gnear[h, :, QB : 2 * QB] += ds
                        else:
                            far_sum = far_sum + jnp.sum(ds, axis=0, keepdims=True)
                    dka[i * QB : (i + 1) * QB, :] += nn(low, qh)
                    acc = acc + nn(kt_ref[hrows, i * QB : (i + 1) * QB], low)
                dq_ref[hrows, cols] = acc.astype(BF16)
                if causal:
                    gf_ref[h] += far_sum
                return carry

            lax.fori_loop(0, heads, one, 0)
        dk_ref[...] = dka[...].astype(BF16)
        dv_ref[...] = dva[...].astype(BF16)
        if causal:
            for h in range(heads):
                gn_ref[h] = diagonal_sums(gnear[h])

    args = [q, k, kt, v, dctx, segq, segk, lse]
    specs = [pl.BlockSpec(memory_space=VM)] * 8
    outs = [
        jax.ShapeDtypeStruct((columns, length), BF16),
        jax.ShapeDtypeStruct((keys, columns), BF16),
        jax.ShapeDtypeStruct((keys, columns), BF16),
    ]
    scratch = [
        pltpu.VMEM((keys, columns), F32),
        pltpu.VMEM((keys, columns), F32),
        pltpu.VMEM((keys, QB), F32),
    ]
    if causal:
        args += [bias[0], bias[1]]
        specs += [pl.BlockSpec(memory_space=VM), pl.BlockSpec(memory_space=pltpu.SMEM)]
        outs += [
            jax.ShapeDtypeStruct((heads, 1, 2 * QB), F32),
            jax.ShapeDtypeStruct((heads, 1, QB), F32),
        ]
        scratch += [pltpu.VMEM((heads, QB, 2 * QB), F32), pltpu.VMEM((heads, QB, 2 * QB), F32)]
    return pl.pallas_call(
        kernel,
        out_shape=outs,
        in_specs=specs,
        out_specs=[pl.BlockSpec(memory_space=VM)] * len(outs),
        scratch_shapes=scratch,
        name="self_bwd" if causal else "cross_bwd",
    )(*args)


def gelu_parts(v):
    c = math.sqrt(2.0 / math.pi)
    t = jnp.tanh(c * (v + 0.044715 * v * v * v))
    value = 0.5 * v * (1.0 + t)
    slope = 0.5 * (1.0 + t) + 0.5 * v * (1.0 - t * t) * c * (1.0 + 3.0 * 0.044715 * v * v)
    return value, slope


def shards(
    zy,
    inputs,
    memory,
    segment_ids,
    memory_ids,
    self_gain,
    self_query,
    self_key,
    self_value,
    self_out,
    bias_table,
    cross_gain,
    cross_query,
    cross_key,
    cross_value,
    cross_out,
    ff_gain,
    ff_gate,
    ff_up,
    ff_down,
    cotangent,
):
    model = inputs.shape[1]
    length = segment_ids.shape[1]
    cols = self_query.shape[1]
    hidden_cols = ff_gate.shape[1]
    heads = cols // DH

    sh_self = jnp.concatenate([self_query, self_key, self_value, self_out.T], axis=1)
    sh_cross = jnp.concatenate([cross_query, cross_key, cross_value, cross_out.T], axis=1)
    sh_ff = jnp.concatenate([ff_gate, ff_up, ff_down.T], axis=1)
    wrows = sh_self.shape[0]
    wide = model // wrows

    def whole(shard):
        return lax.all_gather(shard, "wide", axis=0, tiled=True)

    gain_s, gain_c, gain_f = (g.reshape(1, model) for g in (self_gain, cross_gain, ff_gain))
    segq = segment_ids.reshape(1, length)
    segk_self = jnp.broadcast_to(segment_ids.reshape(length, 1), (length, 128))
    segk_mem = jnp.broadcast_to(memory_ids.reshape(-1, 1), (memory_ids.shape[1], 128))

    buckets = bucket_table(2 * QB, NB, MAX_DIST)
    bias_row = jnp.zeros((heads, 2 * QB), F32)
    where = jnp.asarray(buckets)[None, :]
    for b in range(NB):
        bias_row = jnp.where(where == b, bias_table[b][:, None], bias_row)
    bias = (bias_row.reshape(heads, 1, 2 * QB), bias_table[NB - 1])

    got = first_gather(inputs, memory, gain_s, sh_self, zy)
    w_self = (got["wf"].reshape(model, -1) if zy else whole(sh_self))
    full_self = got["full"].reshape(length, model)
    full_mem = got["mem"].reshape(-1, model)
    wq, wk, wv, wo = (w_self[:, i * cols : (i + 1) * cols] for i in range(4))
    q1 = nn(full_self, wq).astype(BF16)
    k1 = nn(full_self, wk).astype(BF16)
    kt1 = lax.dot_general(wk, full_self, (((0,), (1,)), ((), ())), preferred_element_type=F32).astype(BF16)
    v1 = nn(full_self, wv).astype(BF16)
    vt1 = lax.dot_general(wv, full_self, (((0,), (1,)), ((), ())), preferred_element_type=F32).astype(BF16)
    ctx1, lse1 = attend_fwd(q1, k1, vt1, segq, segk_self, bias)
    part1 = lax.dot_general(ctx1, wo, (((0,), (1,)), ((), ())), preferred_element_type=F32).astype(BF16)

    got = forward_phase(
        part1.reshape(4, -1, model), inputs, gain_c, sh_cross, zy, None, 1, "phase_cross"
    )
    w_cross = (got["wf"].reshape(model, -1) if zy else whole(sh_cross))
    x_two = got["sum"]
    full_cross = got["full"].reshape(length, model)
    cq, ck, cv, co = (w_cross[:, i * cols : (i + 1) * cols] for i in range(4))
    q2 = nn(full_cross, cq).astype(BF16)
    k2 = nn(full_mem, ck).astype(BF16)
    kt2 = lax.dot_general(ck, full_mem, (((0,), (1,)), ((), ())), preferred_element_type=F32).astype(BF16)
    v2 = nn(full_mem, cv).astype(BF16)
    vt2 = lax.dot_general(cv, full_mem, (((0,), (1,)), ((), ())), preferred_element_type=F32).astype(BF16)
    ctx2, lse2 = attend_fwd(q2, k2, vt2, segq, segk_mem, None)
    part2 = lax.dot_general(ctx2, co, (((0,), (1,)), ((), ())), preferred_element_type=F32).astype(BF16)

    got = forward_phase(
        part2.reshape(4, -1, model), x_two, gain_f, sh_ff, zy, cotangent, 2, "phase_ff"
    )
    w_ff = (got["wf"].reshape(model, -1) if zy else whole(sh_ff))
    x_three = got["sum"]
    full_ff = got["full"].reshape(length, model)
    dy3 = got["ef"].reshape(length, model)
    w_gu, w_down_t = w_ff[:, : 2 * hidden_cols], w_ff[:, 2 * hidden_cols :]

    gate_up = nn(full_ff, w_gu)
    gate, up = gate_up[:, :hidden_cols], gate_up[:, hidden_cols:]
    value, slope = gelu_parts(gate)
    hidden = (value * up).astype(BF16)
    part3 = nt(hidden, w_down_t).astype(BF16)
    dhid = nn(dy3, w_down_t)
    dgu = jnp.concatenate([(dhid * up * slope).astype(BF16), (dhid * value).astype(BF16)], axis=1)
    g_ff = jnp.concatenate([tn(full_ff, dgu).astype(BF16), tn(dy3, hidden).astype(BF16)], axis=1)
    dn3 = nt(dgu, w_gu).astype(BF16)

    got = backward_phase(
        dn3.reshape(4, -1, model), x_three, gain_f, cotangent,
        g_ff.reshape(wide, wrows, -1), zy, part3.reshape(4, -1, model), x_three, False, None, 3, "phase_back_ff",
    )
    result = got["eo"]
    g2 = got["sum"]
    dy2 = got["full"].reshape(length, model)
    gg_ff = got["gg"]
    red_ff = got.get("wg")

    dctx2 = nn(dy2, co).astype(BF16)
    dqt2, dk2, dv2 = attend_bwd(q2, k2, kt2, v2, dctx2, segq, segk_mem, lse2, None)
    g_cross = jnp.concatenate(
        [
            lax.dot_general(full_cross, dqt2, (((0,), (1,)), ((), ())), preferred_element_type=F32).astype(BF16),
            tn(full_mem, dk2).astype(BF16),
            tn(full_mem, dv2).astype(BF16),
            lax.dot_general(dy2, ctx2, (((0,), (1,)), ((), ())), preferred_element_type=F32).astype(BF16),
        ],
        axis=1,
    )
    dn2 = lax.dot_general(dqt2, cq, (((0,), (1,)), ((), ())), preferred_element_type=F32).astype(BF16)
    dmem = (nt(dk2, ck) + nt(dv2, cv)).astype(BF16)
    got = backward_phase(
        dn2.reshape(4, -1, model), x_two, gain_c, g2,
        g_cross.reshape(wide, wrows, -1), zy, dmem.reshape(4, -1, model), None, False, None, 4, "phase_back_cross",
    )
    grad_memory = got["eo"]
    g1 = got["sum"]
    dy1 = got["full"].reshape(length, model)
    gg_cross = got["gg"]
    red_cross = got.get("wg")

    dctx1 = nn(dy1, wo).astype(BF16)
    dqt1, dk1, dv1, g_near, g_far = attend_bwd(q1, k1, kt1, v1, dctx1, segq, segk_self, lse1, bias)
    g_self = jnp.concatenate(
        [
            lax.dot_general(full_self, dqt1, (((0,), (1,)), ((), ())), preferred_element_type=F32).astype(BF16),
            tn(full_self, dk1).astype(BF16),
            tn(full_self, dv1).astype(BF16),
            lax.dot_general(dy1, ctx1, (((0,), (1,)), ((), ())), preferred_element_type=F32).astype(BF16),
        ],
        axis=1,
    )
    dn1 = (
        lax.dot_general(dqt1, wq, (((0,), (1,)), ((), ())), preferred_element_type=F32)
        + nt(dk1, wk)
        + nt(dv1, wv)
    ).astype(BF16)

    pick = jnp.asarray((buckets[:, None] == np.arange(NB)[None, :]).astype(np.float32))
    table = jnp.sum(pick[:, :, None] * g_near.reshape(heads, 2 * QB).T[:, None, :], axis=0)
    far = jnp.sum(g_far, axis=(1, 2))
    table = jnp.where(jnp.arange(NB)[:, None] == NB - 1, table + far[None, :], table)
    place = (jnp.arange(4, dtype=jnp.int32) == lax.axis_index("narrow")).astype(F32)
    table = (place[None, :, None] * table[:, None, :]).reshape(1, NB * 4 * heads)
    small = jnp.concatenate(
        [
            jnp.zeros((1, model), F32),
            gg_cross,
            gg_ff,
            jnp.pad(table, ((0, 0), (0, model - table.shape[1]))),
            jnp.zeros((4, model), F32),
        ],
        axis=0,
    )
    got = backward_phase(
        dn1.reshape(4, -1, model), inputs, gain_s, g1,
        g_self.reshape(wide, wrows, -1), zy, None, None, True, small, 5, "phase_back_self",
    )
    grad_inputs = got["gx"]
    if zy:
        total = got["tot"]
        red_self = got["wg"]
    else:
        total = lax.psum(small.at[0].set(got["gg"][0]), ("wide", "narrow"))

        def scatter(g):
            return lax.psum_scatter(g, "wide", scatter_dimension=0, tiled=True).astype(F32)

        red_self, red_cross, red_ff = scatter(g_self), scatter(g_cross), scatter(g_ff)

    def four(red):
        return [red[:, i * cols : (i + 1) * cols] for i in range(3)] + [red[:, 3 * cols :].T]

    s_self, s_cross = four(red_self), four(red_cross)
    return (
        result,
        grad_inputs,
        grad_memory,
        total[0],
        *s_self,
        total[3, : NB * 4 * heads].reshape(NB, 4 * heads),
        total[1],
        *s_cross,
        total[2],
        red_ff[:, :hidden_cols],
        red_ff[:, hidden_cols : 2 * hidden_cols],
        red_ff[:, 2 * hidden_cols :].T,
    )


def solution(mesh):
    zy = mesh.shape["wide"] == 8
    rows = P(("wide", "narrow"), None)
    w_in, w_out = P("wide", "narrow"), P("narrow", "wide")
    placed = (
        rows, rows, P("wide", None), P("wide", None), P(),
        w_in, w_in, w_in, w_out, P(None, "narrow"), P(),
        w_in, w_in, w_in, w_out, P(), w_in, w_in, w_out, rows,
    )
    outs = (
        rows, rows, rows, P(), w_in, w_in, w_in, w_out, P(), P(),
        w_in, w_in, w_in, w_out, P(), w_in, w_in, w_out,
    )
    return jax.shard_map(
        functools.partial(shards, zy), mesh=mesh, in_specs=placed, out_specs=outs, check_vma=False
    )
```

time: 1640 us -> 383 us (0.23)
  waiting for transfers between devices: 781 us -> 0 us
  blocking collectives: 401 us -> 0 us
  Pallas kernels: 0 us -> 271 us
  other arithmetic: 202 us -> 9.86 us
  matrix products: 192 us -> 60.6 us
    reduce_scatter x14 -> x0, waiting for transfers between devices: 620 us -> none  [the longest x3 115 us: add_branch(): lax.psum_scatter(partial_value, 'narrow', scatter_dimension=0, tiled=True)]
    all_gather x11 -> x0, blocking collectives: 360 us -> none  [the longest x1 35 us: shards(): lax.all_gather(ff_down, 'wide', axis=1, tiled=True)]
    pallas_call x0 -> x10, Pallas kernels: none -> 271 us  [the longest x6 218 us: call(): pl.pallas_call(kernel, out_shape=[jax.ShapeDtypeStruct(outputs[k][0], out...]
    unnamed x29 -> x0, waiting for transfers between devices: 133 us -> none
    dot_general x55 -> x34, matrix products: 189 us -> 60.6 us  [the longest x10 20.7 us: nn(): lax.dot_general(left, right, (((1,), (0,)), ((), ())), preferred_element_...]
    reduce_sum x14 -> x2, other arithmetic: 99.9 us -> 1.73 us  [the longest x1 0.94 us: shards(): jnp.sum(pick[:, :, None] * g_near.reshape(heads, 2 * QB).T[:, None, :], a...]
    and x17 -> x0, other arithmetic: 51.8 us -> none  [the longest x1 30.5 us: block_scores(): allowed = allowed & (distance >= 0)]
    psum x1 -> x0, blocking collectives: 40.3 us -> none  [shards(): lax.psum((grad_gain_self, grad_gain_cross, grad_gain_ff, table_full), ('w...]
  transfers between devices with their start and end apart: 25 -> 0, of which waited for: 17 -> 0; matrix products, arithmetic and copies ran while one was open for 17% -> 0% of each run, Pallas kernels for 0% -> 0%
where the time goes in v1:
time: 383 us; the launch traced here: 376 us
  Pallas kernels  271 us (71%)
  matrix products  60.6 us (16%)
  local copies, waits for them, and re-layouts  32.9 us (9%)
  other arithmetic  9.86 us (3%)
    pallas_call x6, Pallas kernels, call(): pl.pallas_call(kernel, out_shape=[jax.ShapeDtypeStruct(outputs[k][0], out...  218 us
    pallas_call x2, Pallas kernels, attend_bwd(): pl.pallas_call(kernel, out_shape=outs, in_specs=specs, out_specs=[pl.Bloc...  31.1 us
    pallas_call x2, Pallas kernels, attend_fwd(): pl.pallas_call(kernel, out_shape=[jax.ShapeDtypeStruct((columns, length),...  22.4 us
    dot_general x10, matrix products, nn(): lax.dot_general(left, right, (((1,), (0,)), ((), ())), preferred_element_...  20.7 us
    dot_general x6, matrix products, nt(): lax.dot_general(left, right, (((1,), (1,)), ((), ())), preferred_element_...  13.7 us
    unnamed x83, local copies, waits for them, and re-layouts  9.17 us

profile of v1, /device:TPU:0, one launch (start us, length us, event | category | flops | bytes accessed | tf_op | source)
XLA Modules:
  0.0 376.2 jit_solution(11379317215506240145)
XLA Ops:
  0.7 1.9 slice_reduce_fusion.3
  4.1 1.9 broadcast_select_fusion.31.refs_5_.refs_8_
  9.8 26.0 %gather_first.1 = (bf16[4,256,768]{2,1,0:T(8,128)(2,1)}, bf16[4,256,768]{2,1,0:T(8,128)(2,1)}, bf16[8,96,768]{2,1,0:T(8,128)(2,1)}) custom-call(bf16[256,768]{1,0:T(8,128)(2,1)} %refs_1_.5, bf16[256,768]{1,0:T(8,128)(2,1)} %refs_1_.3, f32[1,768]{1,0:T(1,128)} %reshape.1806.refs_2_, bf16[96,768]{1,0:T(8,128)(2,1)} %pad_maximum_fusion.7.refs_3_), custom_call_target="tpu_custom_call" | custom-call | tf_op jit(solution)/shard_map/gather_first/pallas_call | solution.py:540
  35.8 3.2 convolution_convert_fusion.9.refs_1_
  42.9 10.0 %self_fwd.1 = (bf16[192,1024]{1,0:T(8,128)(2,1)}, f32[3,1,1024]{2,1,0:T(1,128)}) custom-call(bf16[1024,192]{1,0:T(8,128)(2,1)} %convolution_convert_fusion.10.refs_0_, bf16[1024,192]{1,0:T(8,128)(2,1)} %convolution_convert_fusion.9.refs_1_, bf16[192,1024]{1,0:T(8,128)(2,1)} %convolution_convert_fusion.18.refs_2_, s32[1,1024]{1,0:T(1,128)} %refs_5_.3, ...), custom_call_target="tpu_custom_call" | custom-call | tf_op jit(solution)/shard_map/self_fwd/pallas_call | solution.py:874
  52.9 3.0 convolution_convert_fusion.5
  57.5 25.3 %phase_cross.1 = (f32[256,768]{1,0:T(8,128)}, bf16[4,256,768]{2,1,0:T(8,128)(2,1)}, bf16[8,96,768]{2,1,0:T(8,128)(2,1)}) custom-call(bf16[4,256,768]{2,1,0:T(8,128)(2,1)} %bitcast.117, bf16[256,768]{1,0:T(8,128)(2,1)} %refs_1_.5, f32[1,768]{1,0:T(1,128)} %reshape.1810.refs_2_, bf16[96,768]{1,0:T(8,128)(2,1)} %pad_maximum_fusion.8.refs_3_), custom_call_target="tpu_custom_call" | custom-call | tf_op jit(solution)/shard_map/phase_cross/pallas_call | solution.py:540
  82.8 2.5 convolution_convert_fusion.17.refs_2_
  89.3 12.4 %cross_fwd.1 = (bf16[192,1024]{1,0:T(8,128)(2,1)}, f32[3,1,1024]{2,1,0:T(1,128)}) custom-call(bf16[1024,192]{1,0:T(8,128)(2,1)} %convolution_convert_fusion.8.refs_0_, bf16[1024,192]{1,0:T(8,128)(2,1)} %convolution_convert_fusion.7.refs_1_, bf16[192,1024]{1,0:T(8,128)(2,1)} %convolution_convert_fusion.17.refs_2_, s32[1,1024]{1,0:T(1,128)} %refs_5_.3, ...), custom_call_target="tpu_custom_call" | custom-call | tf_op jit(solution)/shard_map/cross_fwd/pallas_call | solution.py:874
  101.7 3.1 convolution_convert_fusion.4
  106.2 35.9 %phase_ff.1 = (f32[256,768]{1,0:T(8,128)}, bf16[4,256,768]{2,1,0:T(8,128)(2,1)}, bf16[8,96,1536]{2,1,0:T(8,128)(2,1)}, bf16[4,256,768]{2,1,0:T(8,128)(2,1)}) custom-call(bf16[4,256,768]{2,1,0:T(8,128)(2,1)} %bitcast.118, f32[256,768]{1,0:T(8,128)} %get-tuple-element.60.refs_1_, f32[1,768]{1,0:T(1,128)} %reshape.1815.refs_2_, ...), custom_call_target="tpu_custom_call" | custom-call | tf_op jit(solution)/shard_map/phase_ff/pallas_call | solution.py:540
  142.1 3.9 %fusion.8 = f32[1024,1024]{0,1:T(8,128)S(1)} fusion(bf16[1024,768]{1,0:T(8,128)(2,1)} %bitcast.140, bf16[768,1536]{1,0:T(8,128)(2,1)} %bitcast.134), kind=kOutput, calls=%fused_computation.24 | convolution fusion | flops 1610612736 | bytes 7340032 | tf_op jit(solution)/shard_map/dot_general | solution.py:775
  146.0 2.6 fusion.6
  148.5 2.2 convolution_convert_fusion
  150.8 1.8 convolution_convert_fusion.2
  155.2 3.0 convolution_convert_fusion.3
  158.3 57.5 %phase_back_ff.1 = (f32[1,768]{1,0:T(1,128)}, f32[256,768]{1,0:T(8,128)}, bf16[4,256,768]{2,1,0:T(8,128)(2,1)}, f32[96,1536]{1,0:T(8,128)}, bf16[256,768]{1,0:T(8,128)(2,1)}) custom-call(bf16[4,256,768]{2,1,0:T(8,128)(2,1)} %bitcast.127, f32[256,768]{1,0:T(8,128)} %get-tuple-element.64.refs_1_.refs_6_, f32[1,768]{1,0:T(1,128)} %reshape.1815.refs_2_, ...), custom_call_target="tpu_custom_call" | custom-call | tf_op jit(solution)/shard_map/phase_back_ff/pallas_call | solution.py:540
  215.8 2.2 convolution_convert_fusion.12
  221.7 2.7 convolution_convert_fusion.14.refs_2_
  224.5 16.6 %cross_bwd.1 = (bf16[192,1024]{1,0:T(8,128)(2,1)}, bf16[1024,192]{1,0:T(8,128)(2,1)}, bf16[1024,192]{1,0:T(8,128)(2,1)}) custom-call(bf16[1024,192]{1,0:T(8,128)(2,1)} %convolution_convert_fusion.8.refs_0_, bf16[1024,192]{1,0:T(8,128)(2,1)} %convolution_convert_fusion.7.refs_1_, bf16[192,1024]{1,0:T(8,128)(2,1)} %convolution_convert_fusion.14.refs_2_, ...), custom_call_target="tpu_custom_call" | custom-call | tf_op jit(solution)/shard_map/cross_bwd/pallas_call | solution.py:976
  241.0 2.0 fusion.25
  243.1 3.0 add_convert_fusion.1
  251.1 2.8 convolution_convert_fusion.1
  253.9 34.9 %phase_back_cross.1 = (f32[1,768]{1,0:T(1,128)}, f32[256,768]{1,0:T(8,128)}, bf16[4,256,768]{2,1,0:T(8,128)(2,1)}, f32[96,768]{1,0:T(8,128)}, bf16[256,768]{1,0:T(8,128)(2,1)}) custom-call(bf16[4,256,768]{2,1,0:T(8,128)(2,1)} %bitcast.119, f32[256,768]{1,0:T(8,128)} %get-tuple-element.60.refs_1_, f32[1,768]{1,0:T(1,128)} %reshape.1810.refs_2_, ...), custom_call_target="tpu_custom_call" | custom-call | tf_op jit(solution)/shard_map/phase_back_cross/pallas_call | solution.py:540
  288.8 2.2 convolution_convert_fusion.11
  293.7 1.7 convolution_convert_fusion.16.refs_2_
  295.4 14.6 %self_bwd.1 = (bf16[192,1024]{1,0:T(8,128)(2,1)}, bf16[1024,192]{1,0:T(8,128)(2,1)}, bf16[1024,192]{1,0:T(8,128)(2,1)}, f32[3,1,512]{2,1,0:T(1,128)}, f32[3,1,256]{2,1,0:T(1,128)}) custom-call(bf16[1024,192]{1,0:T(8,128)(2,1)} %convolution_convert_fusion.10.refs_0_, bf16[1024,192]{1,0:T(8,128)(2,1)} %convolution_convert_fusion.9.refs_1_, ...), custom_call_target="tpu_custom_call" | custom-call | tf_op jit(solution)/shard_map/self_bwd/pallas_call | solution.py:976
  317.6 1.9 convolution_convert_fusion.19
  323.6 1.7 fusion.32
  326.4 1.8 add_convert_fusion
  328.2 38.2 %phase_back_self.1 = (f32[1,768]{1,0:T(1,128)}, bf16[256,768]{1,0:T(8,128)(2,1)}, f32[96,768]{1,0:T(8,128)}, f32[8,768]{1,0:T(8,128)}) custom-call(bf16[4,256,768]{2,1,0:T(8,128)(2,1)} %bitcast.121, bf16[256,768]{1,0:T(8,128)(2,1)} %refs_1_.5, f32[1,768]{1,0:T(1,128)} %reshape.1806.refs_2_, f32[256,768]{1,0:T(8,128)} %get-tuple-element.77.refs_3_, ...), custom_call_target="tpu_custom_call" | custom-call | tf_op jit(solution)/shard_map/phase_back_self/pallas_call | solution.py:540
  366.4 2.1 slice_bitcast_fusion.1
  (132 shorter events, 50.2 us)
Async XLA Ops:
  4.1 34.9 %copy-start.30 = (f32[3]{0:T(128)}, f32[3]{0:T(128)S(1)}, u32[]{:S(2)}) copy-start(f32[3]{0:T(128)S(1)} %get-tuple-element.182.refs_6_.refs_9_) | copy-start | bytes 40
  35.8 3.2 copy-start
  35.8 3.2 copy-start.2
  40.4 1.4 copy-start.22
  52.9 3.1 copy-start.32
  52.9 3.6 copy-start.26
  52.9 3.8 copy-start.27
  52.9 3.7 copy-start.28
  52.9 3.7 copy-start.29
  56.0 26.8 %copy-start.1 = (bf16[4,256,768]{2,1,0:T(8,128)(2,1)S(1)}, bf16[4,256,768]{2,1,0:T(8,128)(2,1)}, u32[]{:S(2)}) copy-start(bf16[4,256,768]{2,1,0:T(8,128)(2,1)} %get-tuple-element.58) | copy-start | bytes 4718596
  82.8 2.5 copy-start.4
  85.3 1.5 copy-start.6
  101.7 3.2 copy-start.33
  101.7 3.8 copy-start.23
  101.7 3.8 copy-start.24
  101.7 3.7 copy-start.25
  142.1 3.9 %copy-start.34 = (bf16[8,96,1536]{2,1,0:T(8,128)(2,1)S(1)}, bf16[8,96,1536]{2,1,0:T(8,128)(2,1)}, u32[]{:S(2)}) copy-start(bf16[8,96,1536]{2,1,0:T(8,128)(2,1)} %get-tuple-element.62) | copy-start | bytes 7077892
  142.1 3.9 %copy-start.35 = (bf16[4,256,768]{2,1,0:T(8,128)(2,1)S(1)}, bf16[4,256,768]{2,1,0:T(8,128)(2,1)}, u32[]{:S(2)}) copy-start(bf16[4,256,768]{2,1,0:T(8,128)(2,1)} %get-tuple-element.61) | copy-start | bytes 4718596
  148.5 2.2 copy-start.36
  241.0 2.0 copy-start.17
  243.0 3.0 copy-start.7
  243.0 3.0 copy-start.10
  247.6 1.4 copy-start.5
  247.6 1.5 copy-start.9
  253.9 35.0 %copy-start.3 = (bf16[8,96,768]{2,1,0:T(8,128)(2,1)S(1)}, bf16[8,96,768]{2,1,0:T(8,128)(2,1)}, u32[]{:S(2)}) copy-start(bf16[8,96,768]{2,1,0:T(8,128)(2,1)} %get-tuple-element.54) | copy-start | bytes 3538948
  295.4 22.2 %copy-start.8 = (bf16[192,1024]{1,0:T(8,128)(2,1)S(1)}, bf16[192,1024]{1,0:T(8,128)(2,1)}, u32[]{:S(2)}) copy-start(bf16[192,1024]{1,0:T(8,128)(2,1)} %get-tuple-element.55) | copy-start | bytes 1179652
  309.9 9.5 %copy-start.11 = (bf16[192,1024]{1,0:T(8,128)(2,1)S(1)}, bf16[192,1024]{1,0:T(8,128)(2,1)}, u32[]{:S(2)}) copy-start(bf16[192,1024]{1,0:T(8,128)(2,1)} %get-tuple-element.74) | copy-start | bytes 1179652
  328.2 38.2 %copy-start.15 = (f32[96,768]{1,0:T(8,128)S(1)}, f32[96,768]{1,0:T(8,128)}, u32[]{:S(2)}) copy-start(f32[96,768]{1,0:T(8,128)} %get-tuple-element.86) | copy-start | bytes 884740
  366.4 6.6 %copy-start.12 = (f32[96,1536]{1,0:T(8,128)S(1)}, f32[96,1536]{1,0:T(8,128)}, u32[]{:S(2)}) copy-start(f32[96,1536]{1,0:T(8,128)} %get-tuple-element.87) | copy-start | bytes 1769476
  366.4 7.4 %copy-start.19 = (bf16[256,768]{1,0:T(8,128)(2,1)S(1)}, bf16[256,768]{1,0:T(8,128)(2,1)}, u32[]{:S(2)}) copy-start(bf16[256,768]{1,0:T(8,128)(2,1)} %get-tuple-element.231) | copy-start | bytes 1179652
  368.5 6.0 %copy-start.21 = (bf16[256,768]{1,0:T(8,128)(2,1)S(1)}, bf16[256,768]{1,0:T(8,128)(2,1)}, u32[]{:S(2)}) copy-start(bf16[256,768]{1,0:T(8,128)(2,1)} %get-tuple-element.232) | copy-start | bytes 1179652
  369.2 6.1 %copy-start.20 = (bf16[256,768]{1,0:T(8,128)(2,1)S(1)}, bf16[256,768]{1,0:T(8,128)(2,1)}, u32[]{:S(2)}) copy-start(bf16[256,768]{1,0:T(8,128)(2,1)} %get-tuple-element.233) | copy-start | bytes 1179652
  (5 other events, 5.6 us)

commit v2 on v0

v2 whole, which is shorter than its diff:
```python
import math
from types import SimpleNamespace

import jax
import jax.numpy as jnp
import numpy as np
from jax import lax
from jax.experimental import pallas as pl
from jax.experimental.pallas import tpu as pltpu
from jax.sharding import PartitionSpec as P

DH = 64
NB = 32
MAX_DIST = 128
EPS = 1e-06
NEG = -1e30
QB = 256
ROW_CHUNKS = 4
WIDE = "wide"
NARROW = "narrow"
MESH = pl.DeviceIdType.MESH
F32 = jnp.float32
BF16 = jnp.bfloat16
VM = pltpu.VMEM
DMA = pltpu.SemaphoreType.DMA


def bucket_table(length, buckets, reach):
    exact_part = buckets // 2
    distance = np.arange(length)
    spread = (
        np.log(np.maximum(distance, exact_part) / exact_part)
        / np.log(reach / exact_part)
        * (buckets - exact_part)
    )
    far_bucket = np.minimum(exact_part + np.floor(spread).astype(np.int64), buckets - 1)
    return np.where(distance < exact_part, distance, far_bucket).astype(np.int32)


def bucket_ranges(length):
    table = bucket_table(length, NB, MAX_DIST)
    found = []
    for which in range(NB):
        places = np.nonzero(table == which)[0]
        if len(places):
            found.append((which, int(places[0]), int(places[-1]) + 1))
    return found


class Slots:
    def __init__(self):
        self.items = []

    def add(self, holder, **specs):
        for name, spec in specs.items():
            self.items.append((holder, name, spec))

    def fill(self, refs):
        for (holder, name, _), ref in zip(self.items, refs):
            setattr(holder, name, ref)


def run_kernel(body, ins, outs, scratch, cid, name):
    counts = len(ins.items), len(outs.items)

    def kernel(*refs):
        ins.fill(refs[: counts[0]])
        outs.fill(refs[counts[0] : counts[0] + counts[1]])
        scratch.fill(refs[counts[0] + counts[1] :])
        body()

    params = {} if cid is None else dict(collective_id=cid, has_side_effects=True)
    return pl.pallas_call(
        kernel,
        out_shape=[jax.ShapeDtypeStruct(*spec) for _, _, spec in outs.items],
        in_specs=[pl.BlockSpec(memory_space=spec[1]) for _, _, spec in ins.items],
        out_specs=[pl.BlockSpec(memory_space=VM) for _ in outs.items],
        scratch_shapes=[spec for _, _, spec in scratch.items],
        compiler_params=pltpu.CompilerParams(vmem_limit_bytes=66_900_000, **params),
        name=name,
    )(*[spec[0] for _, _, spec in ins.items])


class Spot:
    def __init__(self, wide_split):
        n = lax.axis_index(NARROW)
        self.n = n
        self.x = n // 2
        self.c = n % 2
        self.sib = self.x * 2 + (1 - self.c)
        self.xp = (1 - self.x) * 2 + self.c
        self.xsib = (1 - self.x) * 2 + (1 - self.c)
        if wide_split:
            w = lax.axis_index(WIDE)
            self.w = w
            self.z = w // 2
            self.y = w % 2
            self.yp = self.z * 2 + (1 - self.y)

    def at_n(self, n):
        return {NARROW: n}

    def at_w(self, w):
        return {WIDE: w}

    def at_z(self, z):
        return {WIDE: z * 2 + self.y}


def remote(src, dst, send, recv, dev):
    return pltpu.make_async_remote_copy(
        src_ref=src, dst_ref=dst, send_sem=send, recv_sem=recv, device_id=dev, device_id_type=MESH
    )


def greet(spot, zy):
    barrier = pltpu.get_barrier_semaphore()

    def hello(dev):
        pl.semaphore_signal(barrier, inc=1, device_id=dev, device_id_type=MESH)

    hello(spot.at_n(spot.sib))
    hello(spot.at_n(spot.xp))
    if zy:
        hello(spot.at_w(spot.yp))
        for step in range(1, 4):
            hello(spot.at_z((spot.z + step) % 4))
    pl.semaphore_wait(barrier, 6 if zy else 2)


def aligned(start, size):
    return pl.ds(pl.multiple_of(start, 16), size)


class RowGather:
    def __init__(self, slots, rows, chunks=ROW_CHUNKS):
        self.nrows, self.chunks, self.size = rows, chunks, rows // chunks
        sems = DMA((chunks,))
        slots.add(self, xs=sems, xr=sems, ss=sems, sr=sems, fs=sems, fr=sems)

    def bind(self, spot, full):
        self.spot, self.full = spot, full

    def hop(self, k, block, dev, send, recv):
        rows = self.full.at[aligned(block * self.nrows + k * self.size, self.size)]
        return remote(rows, rows, send.at[k], recv.at[k], self.spot.at_n(dev))

    def to_x(self, k):
        return self.hop(k, self.spot.n, self.spot.xp, self.xs, self.xr)

    def from_x(self, k):
        return self.hop(k, self.spot.xp, self.spot.xp, self.xs, self.xr)

    def to_sib(self, k):
        return self.hop(k, self.spot.n, self.spot.sib, self.ss, self.sr)

    def from_sib(self, k):
        return self.hop(k, self.spot.sib, self.spot.sib, self.ss, self.sr)

    def onward(self, k):
        return self.hop(k, self.spot.xp, self.spot.sib, self.fs, self.fr)

    def from_onward(self, k):
        return self.hop(k, self.spot.xsib, self.spot.sib, self.fs, self.fr)

    def send(self, k):
        self.to_x(k).start()
        self.to_sib(k).start()

    def send_all(self):
        for k in range(self.chunks):
            self.send(k)

    def forward(self, first, after):
        for k in range(first, after):
            self.from_x(k).wait_recv()
            self.onward(k).start()

    def have_sib(self):
        for k in range(self.chunks):
            self.from_sib(k).wait_recv()

    def have_xsib(self):
        for k in range(self.chunks):
            self.from_onward(k).wait_recv()

    def finish(self):
        for k in range(self.chunks):
            self.to_x(k).wait_send()
            self.to_sib(k).wait_send()
            self.onward(k).wait_send()


class RowReduce:
    def __init__(self, slots, rows, cols, chunks=ROW_CHUNKS):
        self.nrows, self.chunks, self.size = rows, chunks, rows // chunks
        sems, buf = DMA((chunks,)), VM((rows, cols), BF16)
        slots.add(self, as_=sems, ar=sems, bs=sems, br=sems, xs=sems, xr=sems, far=buf, own=buf, inn=buf)

    def bind(self, spot, part):
        self.spot, self.part = spot, part

    def buf(self, ref, k):
        return ref.at[pl.ds(k * self.size, self.size)]

    def mine(self, block, k):
        return self.part.at[aligned(block * self.nrows + k * self.size, self.size)]

    def far_sib(self, k):
        s = self.spot
        return remote(self.mine(s.xsib, k), self.buf(self.far, k), self.as_.at[k], self.ar.at[k], s.at_n(s.sib))

    def own_sib(self, k):
        s = self.spot
        return remote(self.mine(s.sib, k), self.buf(self.own, k), self.bs.at[k], self.br.at[k], s.at_n(s.sib))

    def across(self, k):
        s = self.spot
        return remote(self.buf(self.far, k), self.buf(self.inn, k), self.xs.at[k], self.xr.at[k], s.at_n(s.xp))

    def send_far(self):
        for k in range(self.chunks):
            self.far_sib(k).start()

    def send_own(self):
        for k in range(self.chunks):
            self.own_sib(k).start()

    def cross(self):
        for k in range(self.chunks):
            self.far_sib(k).wait_recv()
            here = self.buf(self.far, k)
            here[...] = (self.mine(self.spot.xp, k)[...].astype(F32) + here[...].astype(F32)).astype(BF16)
            self.across(k).start()

    def total(self, k):
        self.own_sib(k).wait_recv()
        self.across(k).wait_recv()
        value = self.mine(self.spot.n, k)[...].astype(F32) + self.buf(self.own, k)[...].astype(F32)
        return value + self.buf(self.inn, k)[...].astype(F32)

    def finish(self):
        for k in range(self.chunks):
            self.far_sib(k).wait_send()
            self.own_sib(k).wait_send()
            self.across(k).wait_send()


class WideGather:
    steps = (1, -1, 2, -2, 3, -3)

    def __init__(self, slots, rows, halves=2):
        self.nrows, self.halves, self.size = rows, halves, rows // halves
        slots.add(self, zs=DMA((6, halves)), zr=DMA((4, halves)), ys=DMA((4, halves)), yr=DMA((4, halves)))

    def bind(self, spot, full):
        self.spot, self.full = spot, full

    def rows(self, z, y, half):
        return self.full.at[aligned((z * 2 + y) * self.nrows + half * self.size, self.size)]

    def along(self, i, half):
        s = self.spot
        rows = self.rows(s.z, s.y, half)
        return remote(rows, rows, self.zs.at[i, half], self.zr.at[s.z, half], s.at_z(s.z + self.steps[i]))

    def came(self, z, half):
        s = self.spot
        rows = self.rows(z, s.y, half)
        return remote(rows, rows, self.zs.at[0, half], self.zr.at[z, half], s.at_z(z))

    def over(self, z, half):
        s = self.spot
        rows = self.rows(z, s.y, half)
        return remote(rows, rows, self.ys.at[z, half], self.yr.at[z, half], s.at_w(s.yp))

    def crossed(self, z, half):
        s = self.spot
        rows = self.rows(z, 1 - s.y, half)
        return remote(rows, rows, self.ys.at[z, half], self.yr.at[z, half], s.at_w(s.yp))

    def when_inside(self, step, fn):
        there = self.spot.z + step

        @pl.when(there >= 0 if step < 0 else there <= 3)
        def _():
            fn(there)

    def open(self):
        for half in range(self.halves):
            self.over(self.spot.z, half).start()
        for i, step in enumerate(self.steps):
            for half in range(self.halves):
                self.when_inside(step, lambda there: self.along(i, half).start())

    def forward(self, distance):
        for half in range(self.halves):
            for step in (distance, -distance):

                def pass_on(there):
                    self.came(there, half).wait_recv()
                    self.over(there, half).start()

                self.when_inside(step, pass_on)

    def have(self):
        for half in range(self.halves):
            for z in range(4):
                self.crossed(z, half).wait_recv()

    def finish(self):
        for half in range(self.halves):
            for z in range(4):
                self.over(z, half).wait_send()
            for i, step in enumerate(self.steps):
                self.when_inside(step, lambda there: self.along(i, half).wait_send())


class WideReduce:
    steps = (2, 3, 1, 0)

    def __init__(self, slots, rows, cols, width):
        self.nrows, self.width, self.chunks = rows, width, cols // width
        sems, buf = DMA((self.chunks, 4)), VM((4, rows, cols), BF16)
        slots.add(self, ys=sems, yr=sems, zs=sems, zr=sems, acc=buf, inn=buf)

    def bind(self, spot, part, out, out_col):
        self.spot, self.part, self.out, self.out_col = spot, part, out, out_col

    def cols(self, c):
        return pl.ds(c * self.width, self.width)

    def slab(self, c, z, y):
        return self.part.at[aligned((z * 2 + y) * self.nrows, self.nrows), self.cols(c)]

    def over(self, c, z):
        s = self.spot
        return remote(
            self.slab(c, z, 1 - s.y), self.acc.at[z, :, self.cols(c)], self.ys.at[c, z], self.yr.at[c, z], s.at_w(s.yp)
        )

    def along(self, c, z):
        s = self.spot
        return remote(
            self.acc.at[z, :, self.cols(c)], self.inn.at[s.z, :, self.cols(c)],
            self.zs.at[c, z], self.zr.at[c, s.z], s.at_z(z),
        )

    def came(self, c, z):
        here = self.inn.at[z, :, self.cols(c)]
        return remote(here, here, self.zs.at[c, z], self.zr.at[c, z], self.spot.at_z(z))

    def targets(self):
        return [(self.spot.z + step) % 4 for step in self.steps]

    def open(self, c):
        for z in self.targets():
            self.over(c, z).start()

    def first(self, c):
        for step, z in zip(self.steps, self.targets()):
            self.over(c, z).wait_recv()
            here = self.acc.at[z, :, self.cols(c)]
            here[...] = (self.slab(c, z, self.spot.y)[...].astype(F32) + here[...].astype(F32)).astype(BF16)
            if step:
                self.along(c, z).start()

    def total(self, c):
        value = self.acc[self.spot.z, :, self.cols(c)].astype(F32)
        for z in self.targets()[:3]:
            self.came(c, z).wait_recv()
            value = value + self.inn[z, :, self.cols(c)].astype(F32)
        self.out[:, pl.ds(self.out_col + c * self.width, self.width)] = value

    def finish(self):
        for c in range(self.chunks):
            for step, z in zip(self.steps, self.targets()):
                self.over(c, z).wait_send()
                if step:
                    self.along(c, z).wait_send()


class SmallSum:
    def __init__(self, slots, rows, cols):
        four = VM((4, rows, cols), F32)
        slots.add(
            self, ps=DMA((3,)), pr=DMA((3,)), zs=DMA((4,)), zr=DMA((4,)), held=four, inn=VM((3, rows, cols), F32), zin=four
        )

    def run(self, spot, value, out):
        held, inn, zin = self.held, self.inn, self.zin
        held[0] = value
        devs = (spot.at_n(spot.sib), spot.at_n(spot.xp), spot.at_w(spot.yp))
        copies = []
        for i in range(3):
            copy = remote(held.at[i], inn.at[i], self.ps.at[i], self.pr.at[i], devs[i])
            copy.start()
            copies.append(copy)
            copy.wait_recv()
            held[i + 1] = held[i] + inn[i]
        zin[spot.z] = held[3]

        def hop(step, landed):
            other = (spot.z + step) % 4
            return remote(
                held.at[3], zin.at[landed], self.zs.at[step], self.zr.at[landed], spot.at_z(other)
            )

        for step in range(1, 4):
            hop(step, spot.z).start()
        for step in range(1, 4):
            hop(step, (spot.z + step) % 4).wait_recv()
        out[...] = ((zin[0] + zin[1]) + zin[2]) + zin[3]
        for copy in copies:
            copy.wait_send()
        for step in range(1, 4):
            hop(step, spot.z).wait_send()


class Idle:
    chunks = 0

    def bind(self, *args):
        pass

    open = forward = have = finish = first = total = bind


def nt(left, right):
    return lax.dot_general(left, right, (((1,), (1,)), ((), ())), preferred_element_type=F32)


def nn(left, right):
    return lax.dot_general(left, right, (((1,), (0,)), ((), ())), preferred_element_type=F32)


def tn(left, right):
    return lax.dot_general(left, right, (((0,), (0,)), ((), ())), preferred_element_type=F32)


def mean_square(values):
    return jnp.mean(values * values, axis=-1, keepdims=True)


def norm_rows(values, gain):
    return values * lax.rsqrt(mean_square(values) + EPS) * gain


def norm_back(values, gain, dn):
    r = lax.rsqrt(mean_square(values) + EPS)
    u = values * r
    dg = dn * gain
    rows = r * (dg - u * jnp.mean(dg * u, axis=-1, keepdims=True))
    return rows, jnp.sum(dn * u, axis=0, keepdims=True)


def gelu_parts(v):
    c = math.sqrt(2.0 / math.pi)
    t = jnp.tanh(c * (v + 0.044715 * v * v * v))
    value = 0.5 * v * (1.0 + t)
    slope = 0.5 * (1.0 + t) + 0.5 * v * (1.0 - t * t) * c * (1.0 + 3.0 * 0.044715 * v * v)
    return value, slope


def head_rows(values, h):
    lane = lax.broadcasted_iota(jnp.int32, values.shape, 1)
    return jnp.where(lane // DH == h, values, jnp.zeros_like(values))


def diagonal_sums(tile):
    rows, width = tile.shape
    while rows > 1:
        rows = rows // 2
        tile = tile[:rows] + pltpu.roll(tile[rows:], width - rows, 1)
    return tile


class Attention:
    def __init__(self, slots, shared, length, cols, causal):
        self.shared, self.cols, self.heads, self.causal = shared, cols, cols // DH, causal
        rows, turned = VM((length, cols), BF16), VM((4, cols, QB), BF16)
        slots.add(
            self, q=rows, k=rows, v=rows, ctx=rows, kt=turned, vt=turned,
            lse=VM((4, self.heads, 1, QB), F32), kcol=VM((length, 128), F32),
        )

    def bind(self, weights):
        self.w = weights

    def blk(self, b):
        return aligned(b * QB, QB)

    def wcols(self, first, count):
        return self.w[:, first * self.cols : (first + count) * self.cols]

    def mask(self, b, kb):
        sk = self.kcol[self.blk(kb), :]
        sk = jnp.concatenate([sk, sk], axis=1)
        return jnp.where(sk == self.shared.segq[b], 0.0, NEG)

    def score(self, k, q, madd, h, kind):
        s = nt(k, q) + madd
        if self.causal:
            s = s + self.shared.bias[kind, h]
        return s

    def kind(self, b, kb):
        return jnp.minimum(b - kb, 2) if self.causal else None

    def key_blocks(self, b):
        return b + 1 if self.causal else 4

    def project_kv(self, source):
        c = self.cols

        def one(b, carry):
            kv = nn(source[self.blk(b), :], self.wcols(1, 2))
            k, v = kv[:, :c], kv[:, c:]
            self.k[self.blk(b), :] = k.astype(BF16)
            self.v[self.blk(b), :] = v.astype(BF16)
            self.kt[b] = k.T.astype(BF16)
            self.vt[b] = v.T.astype(BF16)
            return carry

        lax.fori_loop(0, 4, one, 0)

    def project_q(self, source, b):
        self.q[self.blk(b), :] = nn(source[self.blk(b), :], self.wcols(0, 1)).astype(BF16)

    def out_part(self, dest, b):
        dest[self.blk(b), :] = nt(self.ctx[self.blk(b), :], self.wcols(3, 1)).astype(BF16)

    def rows_of(self, h):
        return slice(h * DH, (h + 1) * DH)

    def wide_of(self, h):
        return slice(h * QB, (h + 1) * QB)

    def forward(self, b):
        s_ = self.shared
        q = self.q[self.blk(b), :]
        for h in range(self.heads):
            s_.qm[self.wide_of(h), :] = head_rows(q, h)
        s_.peak[...] = jnp.full_like(s_.peak, NEG)
        s_.total[...] = jnp.zeros_like(s_.total)
        s_.oacc[...] = jnp.zeros_like(s_.oacc)

        def tile(kb, carry):
            madd = self.mask(b, kb)
            k = self.k[self.blk(kb), :]
            for h in range(self.heads):
                hs = self.rows_of(h)
                s = self.score(k, s_.qm[self.wide_of(h), :], madd, h, self.kind(b, kb))
                old = s_.peak[h]
                new = jnp.maximum(old, jnp.max(s, axis=0, keepdims=True))
                fade = jnp.exp(old - new)
                x = jnp.exp(s - new)
                s_.peak[h] = new
                s_.total[h] = s_.total[h] * fade + jnp.sum(x, axis=0, keepdims=True)
                s_.oacc[hs, :] = s_.oacc[hs, :] * fade + nn(self.vt[kb, hs, :], x.astype(BF16))
            return carry

        lax.fori_loop(0, self.key_blocks(b), tile, 0)
        for h in range(self.heads):
            hs = self.rows_of(h)
            s_.oacc[hs, :] = s_.oacc[hs, :] / s_.total[h]
            self.lse[b, h] = s_.peak[h] + jnp.log(s_.total[h])
        self.ctx[self.blk(b), :] = s_.oacc[...].T.astype(BF16)

    def backward(self, b, dctx):
        s_ = self.shared
        q = self.q[self.blk(b), :]
        prod = (dctx.astype(F32) * self.ctx[self.blk(b), :].astype(F32)).T
        for h in range(self.heads):
            s_.qm[self.wide_of(h), :] = head_rows(q, h)
            s_.dm[self.wide_of(h), :] = head_rows(dctx, h)
            s_.total[h] = jnp.sum(prod[self.rows_of(h), :], axis=0, keepdims=True)
        s_.oacc[...] = jnp.zeros_like(s_.oacc)

        def tile(kb, carry):
            madd = self.mask(b, kb)
            keys = self.blk(kb)
            k, v = self.k[keys, :], self.v[keys, :]
            kind = self.kind(b, kb)
            for h in range(self.heads):
                hs, wide = self.rows_of(h), self.wide_of(h)
                p = jnp.exp(self.score(k, s_.qm[wide, :], madd, h, kind) - self.lse[b, h])
                ds = p * (nt(v, s_.dm[wide, :]) - s_.total[h])
                if self.causal:
                    s_.gb[kind, h] += ds
                low = ds.astype(BF16)
                s_.pcat[:, wide] = p.astype(BF16)
                s_.dcat[:, wide] = low
                s_.oacc[hs, :] += nn(self.kt[kb, hs, :], low)
            s_.dva[keys, :] += nn(s_.pcat[...], s_.dm[...])
            s_.dka[keys, :] += nn(s_.dcat[...], s_.qm[...])
            return carry

        lax.fori_loop(0, self.key_blocks(b), tile, 0)
        return s_.oacc[...].T.astype(BF16)


def make_bias(s_, table, heads, ranges):
    lane = lax.broadcasted_iota(jnp.int32, (1, 2 * QB), 1)
    jj = lax.broadcasted_iota(jnp.int32, (QB, QB), 0)
    ii = lax.broadcasted_iota(jnp.int32, (QB, QB), 1)
    for h in range(heads):
        row = jnp.full((1, 2 * QB), table[h, NB - 1])
        for which, start, stop in reversed(ranges[:-1]):
            row = jnp.where(lane < stop, table[h, which], row)
        turned = pltpu.roll(jnp.broadcast_to(row, (QB, 2 * QB)), 0, 1, stride=1, stride_axis=0)
        s_.bias[0, h] = jnp.where(jj <= ii, turned[:, :QB], NEG)
        s_.bias[1, h] = turned[:, QB:]
        s_.bias[2, h] = jnp.full((QB, QB), table[h, NB - 1])
    s_.gb[...] = jnp.zeros_like(s_.gb)


def table_rows(s_, heads, ranges, n):
    near = [diagonal_sums(jnp.concatenate([s_.gb[0, h], s_.gb[1, h]], axis=1)) for h in range(heads)]
    near = jnp.concatenate(near + [jnp.zeros((8 - heads, 2 * QB), F32)], axis=0)
    lane = lax.broadcasted_iota(jnp.int32, (1, 128), 1)
    first = jnp.full((1, 128), 2 * QB, jnp.int32)
    after = jnp.zeros((1, 128), jnp.int32)
    for which, start, stop in ranges:
        first = jnp.where(lane == which, start, first)
        after = jnp.where(lane == which, stop, after)
    dist = lax.broadcasted_iota(jnp.int32, (2 * QB, 128), 0)
    pick = jnp.where(jnp.logical_and(dist >= first, dist < after), 1.0, 0.0)
    sums = lax.dot_general(
        near, pick, (((1,), (0,)), ((), ())), precision=lax.Precision.HIGHEST, preferred_element_type=F32
    )
    place = lax.broadcasted_iota(jnp.int32, (16, 128), 0)
    rows = jnp.zeros((16, 128), F32)
    for h in range(heads):
        far = jnp.sum(jnp.sum(s_.gb[2, h], axis=0, keepdims=True), axis=1, keepdims=True)
        line = sums[h : h + 1, :] + jnp.where(lane == NB - 1, far, 0.0)
        rows = jnp.where(place == n * heads + h, jnp.broadcast_to(line, (16, 128)), rows)
    return rows


def weight_grad(dest, column, left, right):
    width = right.shape[1]

    def one(m, carry):
        part = pl.ds(pl.multiple_of(m * 256, 256), 256)
        dest[part, column : column + width] = tn(left[:, part], right[...]).astype(BF16)
        return carry

    lax.fori_loop(0, left.shape[1] // 256, one, 0)


class Layer:
    def __init__(self, zy, sizes, ins, outs, slots):
        self.zy, self.sizes = zy, sizes
        rows, model, cols, hid, wrows, length = sizes
        heads = cols // DH
        self.heads = heads
        s_ = self.shared = SimpleNamespace()
        self.one = Attention(slots, s_, length, cols, True)
        self.two = Attention(slots, s_, length, cols, False)
        wide_rows, acc = VM((heads * QB, cols), BF16), VM((length, cols), F32)
        line, tiles, cat = VM((heads, 1, QB), F32), VM((3, heads, QB, QB), F32), VM((QB, heads * QB), BF16)
        slots.add(
            s_, segq=VM((4, 1, QB), F32), bias=tiles, gb=tiles, qm=wide_rows, dm=wide_rows, peak=line, total=line,
            oacc=VM((cols, QB), F32), pcat=cat, dcat=cat, dva=acc, dka=acc,
        )
        full, own, head_out = VM((length, model), BF16), VM((rows, model), F32), VM((length, cols), BF16)
        slots.add(
            self, full_self=full, full_mem=full, full_cross=full, full_ff=full, dy3=full, dy2=full, dy1=full,
            pa=full, pb=full, x_two=own, x_three=own, g=own, dq=head_out, dk=head_out, dv=head_out,
            hidden=VM((length, hid), BF16), dgu=VM((length, 2 * hid), BF16), small=VM((16, model), F32),
        )
        self.gathers = [RowGather(slots, rows) for _ in range(7)]
        self.g_self, self.g_mem, self.g_cross, self.g_ff, self.g_dy3, self.g_dy2, self.g_dy1 = self.gathers
        self.reduces = [RowReduce(slots, rows, model) for _ in range(7)]
        self.r_out1, self.r_out2, self.r_out3, self.r_dn3, self.r_dn2, self.r_mem, self.r_dn1 = self.reduces
        self.groups = [SimpleNamespace(width=w) for w in (4 * cols, 4 * cols, 3 * hid)]
        self.ws, self.wc, self.wf = self.groups
        for group in self.groups:
            if zy:
                both = VM((model, group.width), BF16)
                slots.add(group, w=both, gp=both)
                group.gather = WideGather(slots, wrows)
                group.reduce = WideReduce(slots, wrows, group.width, 384)
            else:
                outs.add(group, gp=((model, group.width), BF16))
                group.gather = group.reduce = Idle()
        if zy:
            self.ss = SmallSum(slots, 16, model)

    def blk(self, b):
        return aligned(b * QB, QB)

    def chunk(self, k, block=0):
        size = self.sizes[0] // ROW_CHUNKS
        return aligned(block * self.sizes[0] + k * size, size)

    def far_first(self, i):
        s = self.spot
        far = jnp.where(i < 2, 1 - s.x, s.x)
        return far * 2 + jnp.where(i % 2 == 0, 1 - s.c, s.c)

    def near_first(self, i):
        s = self.spot
        far = jnp.where(i < 2, s.x, 1 - s.x)
        return far * 2 + jnp.where(jnp.logical_or(i == 0, i == 3), s.c, 1 - s.c)

    def near_waits(self, i, gather):
        @pl.when(i == 1)
        def _():
            gather.have_sib()
            gather.forward(0, 1)

        @pl.when(i == 2)
        def _():
            gather.forward(1, ROW_CHUNKS)
            gather.have_xsib()

    def near_sends(self, i, reduce):
        @pl.when(i == 1)
        def _():
            reduce.send_own()

        @pl.when(i == 2)
        def _():
            reduce.send_far()

        @pl.when(i == 3)
        def _():
            reduce.cross()

    def at(self, i, *actions):
        for j, action in enumerate(actions):
            if action is not None:
                pl.when(i == j)(action)

    def pack(self, group, *shards):
        rows = self.sizes[4]
        parts = [ref[...].astype(F32) for ref in shards]
        parts = [p if p.shape[0] == rows else p.T for p in parts]
        group.w[aligned(self.spot.w * rows, rows), :] = jnp.concatenate(parts, axis=1).astype(BF16)

    def ff_block(self, b):
        f = self.sizes[3]
        step = f // 2
        w, blk = self.wf.w, self.blk(b)
        x, dy = self.full_ff[blk, :], self.dy3[blk, :]
        for j in range(0, f, step):
            gate = nn(x, w[:, j : j + step])
            up = nn(x, w[:, f + j : f + j + step])
            dh = nn(dy, w[:, 2 * f + j : 2 * f + j + step])
            value, slope = gelu_parts(gate)
            self.hidden[blk, j : j + step] = (value * up).astype(BF16)
            self.dgu[blk, j : j + step] = (dh * up * slope).astype(BF16)
            self.dgu[blk, f + j : f + j + step] = (dh * value).astype(BF16)
        self.pa[blk, :] = nt(self.dgu[blk, :], w[:, : 2 * f]).astype(BF16)

    def norm_backward(self, values, gain, reduce, base, done):
        gain_sum = jnp.zeros((1, self.sizes[1]), F32)
        for k in range(ROW_CHUNKS):
            rows = self.chunk(k)
            add, part = norm_back(values[rows, :].astype(F32), gain, reduce.total(k))
            gain_sum = gain_sum + part
            done(k, rows, base[rows, :].astype(F32) + add)
        return gain_sum

    def run(self):
        rows, model, cols, hid, wrows, length = self.sizes
        zy, heads, s_ = self.zy, self.heads, self.shared
        spot = self.spot = Spot(zy)
        one, two = self.one, self.two
        ws, wc, wf = self.groups
        greet(spot, zy)
        for gather, full in zip(
            self.gathers, (self.full_self, self.full_mem, self.full_cross, self.full_ff, self.dy3, self.dy2, self.dy1)
        ):
            gather.bind(spot, full)
        for reduce, part in zip(
            self.reduces, (self.pa, self.pb, self.pb, self.pa, self.pa, self.pb, self.pa)
        ):
            reduce.bind(spot, part)
        column = 0
        for group in self.groups:
            group.gather.bind(spot, group.w)
            group.reduce.bind(spot, group.gp, self.red if zy else None, column)
            column += group.width
        one.bind(ws.w)
        two.bind(wc.w)
        gain_s, gain_c, gain_f = (ref[...].reshape(1, model) for ref in (self.gain_s, self.gain_c, self.gain_f))

        if zy:
            self.pack(ws, self.sq, self.sk, self.sv, self.so)
        ws.gather.open()
        for k in range(ROW_CHUNKS):
            x = self.x[self.chunk(k), :].astype(F32)
            self.full_self[self.chunk(k, spot.n), :] = norm_rows(x, gain_s).astype(BF16)
            self.g_self.send(k)
        self.full_mem[self.blk(spot.n), :] = self.m[...]
        self.g_mem.send_all()
        if zy:
            self.pack(wc, self.cq, self.ck, self.cv, self.co)
            self.pack(wf, self.fg, self.fu, self.fd)
        ranges = bucket_ranges(2 * QB)
        for attention, ids in ((one, self.sid), (two, self.mid)):
            values = ids[...].astype(F32)
            attention.kcol[...] = jnp.broadcast_to(values, (128, length)).T
        for b in range(4):
            s_.segq[b] = self.sid[:, b * QB : (b + 1) * QB].astype(F32)
        make_bias(s_, self.table, heads, ranges)
        ws.gather.forward(1)
        self.g_self.forward(0, 2)
        ws.gather.forward(2)
        self.g_self.forward(2, 4)
        ws.gather.forward(3)
        wc.gather.open()
        self.g_self.have_sib()
        self.g_self.have_xsib()
        ws.gather.have()

        one.project_kv(self.full_self)

        def self_block(i, carry):
            b = self.far_first(i)
            one.project_q(self.full_self, b)
            one.forward(b)
            one.out_part(self.pa, b)

            def after_first():
                self.r_out1.send_far()
                wc.gather.forward(1)

            def after_second():
                self.r_out1.cross()
                self.g_mem.forward(0, 4)

            def after_third():
                self.r_out1.send_own()
                wc.gather.forward(2)

            self.at(i, after_first, after_second, after_third)
            return carry

        lax.fori_loop(0, 4, self_block, 0)
        wc.gather.forward(3)
        wf.gather.open()
        self.g_mem.have_sib()
        self.g_mem.have_xsib()
        wc.gather.have()
        two.project_kv(self.full_mem)
        wf.gather.forward(1)
        for k in range(ROW_CHUNKS):
            value = self.x[self.chunk(k), :].astype(F32) + self.r_out1.total(k)
            self.x_two[self.chunk(k), :] = value
            self.full_cross[self.chunk(k, spot.n), :] = norm_rows(value, gain_c).astype(BF16)
            self.g_cross.send(k)
        self.dy3[self.blk(spot.n), :] = self.cot[...]
        self.g_dy3.send_all()

        def cross_block(i, carry):
            b = self.near_first(i)
            self.near_waits(i, self.g_cross)
            two.project_q(self.full_cross, b)
            two.forward(b)
            two.out_part(self.pb, b)
            self.near_sends(i, self.r_out2)
            self.at(i, None, lambda: wf.gather.forward(2), None, lambda: wf.gather.forward(3))
            return carry

        lax.fori_loop(0, 4, cross_block, 0)
        self.g_dy3.forward(0, 4)
        for k in range(ROW_CHUNKS):
            value = self.x_two[self.chunk(k), :] + self.r_out2.total(k)
            self.x_three[self.chunk(k), :] = value
            self.full_ff[self.chunk(k, spot.n), :] = norm_rows(value, gain_f).astype(BF16)
            self.g_ff.send(k)
        self.r_out1.finish()
        self.r_out2.finish()
        self.g_dy3.have_sib()
        self.g_dy3.have_xsib()
        wf.gather.have()

        def ff_step(i, carry):
            b = self.near_first(i)
            self.near_waits(i, self.g_ff)
            self.ff_block(b)
            self.near_sends(i, self.r_dn3)
            return carry

        lax.fori_loop(0, 4, ff_step, 0)
        weight_grad(wf.gp, 0, self.full_ff, self.dgu)
        split = wf.reduce.chunks * 2 // 3
        for c in range(split):
            wf.reduce.open(c)

        def ff_out(b, carry):
            self.pb[self.blk(b), :] = nt(self.hidden[self.blk(b), :], wf.w[:, 2 * hid :]).astype(BF16)
            return carry

        lax.fori_loop(0, 4, ff_out, 0)
        self.r_out3.send_far()
        self.r_out3.send_own()
        weight_grad(wf.gp, 2 * hid, self.dy3, self.hidden)
        for c in range(split, wf.reduce.chunks):
            wf.reduce.open(c)

        def back_three(k, at, value):
            self.g[at, :] = value
            self.dy2[self.chunk(k, spot.n), :] = value.astype(BF16)
            self.g_dy2.send(k)

        gain_ff = self.norm_backward(self.x_three, gain_f, self.r_dn3, self.cot, back_three)
        self.small[14:15, :] = gain_ff
        self.r_out3.cross()

        self.r_dn3.finish()
        s_.dka[...] = jnp.zeros_like(s_.dka)
        s_.dva[...] = jnp.zeros_like(s_.dva)

        def cross_back(i, carry):
            b = self.near_first(i)
            blk = self.blk(b)
            self.near_waits(i, self.g_dy2)
            dctx = nn(self.dy2[blk, :], two.wcols(3, 1)).astype(BF16)
            dq = two.backward(b, dctx)
            self.dq[blk, :] = dq
            self.pa[blk, :] = nt(dq, two.wcols(0, 1)).astype(BF16)
            self.near_sends(i, self.r_dn2)
            if zy:
                self.at(i, lambda: wf.reduce.first(0), lambda: wf.reduce.first(1), None, lambda: wf.reduce.first(2))
            return carry

        lax.fori_loop(0, 4, cross_back, 0)
        for k in range(ROW_CHUNKS):
            value = self.x_three[self.chunk(k), :] + self.r_out3.total(k)
            self.result[self.chunk(k), :] = value.astype(BF16)
        self.r_out3.finish()
        self.dk[...] = s_.dka[...].astype(BF16)
        self.dv[...] = s_.dva[...].astype(BF16)

        def memory_part(b, carry):
            blk = self.blk(b)
            self.pb[blk, :] = (nt(self.dk[blk, :], two.wcols(1, 1)) + nt(self.dv[blk, :], two.wcols(2, 1))).astype(BF16)
            return carry

        lax.fori_loop(0, 4, memory_part, 0)
        self.r_mem.send_far()
        self.r_mem.send_own()
        if zy:
            wf.reduce.first(3)

        def back_two(k, at, value):
            self.g[at, :] = value
            self.dy1[self.chunk(k, spot.n), :] = value.astype(BF16)
            self.g_dy1.send(k)

        gain_cross = self.norm_backward(self.x_two, gain_c, self.r_dn2, self.g, back_two)
        self.small[13:14, :] = gain_cross
        self.r_mem.cross()
        weight_grad(wc.gp, 0, self.full_cross, self.dq)
        weight_grad(wc.gp, cols, self.full_mem, self.dk)
        wc.reduce.open(0)
        weight_grad(wc.gp, 2 * cols, self.full_mem, self.dv)
        weight_grad(wc.gp, 3 * cols, self.dy2, two.ctx)
        wc.reduce.open(1)

        s_.dka[...] = jnp.zeros_like(s_.dka)
        s_.dva[...] = jnp.zeros_like(s_.dva)

        def self_back(i, carry):
            b = self.near_first(i)
            blk = self.blk(b)
            self.near_waits(i, self.g_dy1)
            dctx = nn(self.dy1[blk, :], one.wcols(3, 1)).astype(BF16)
            self.dq[blk, :] = one.backward(b, dctx)

            def ff_totals():
                for c in range(wf.reduce.chunks):
                    wf.reduce.total(c)

            self.at(i, lambda: wc.reduce.first(0), ff_totals, lambda: wc.reduce.first(1))
            return carry

        lax.fori_loop(0, 4, self_back, 0)
        self.dk[...] = s_.dka[...].astype(BF16)
        self.dv[...] = s_.dva[...].astype(BF16)
        self.r_dn2.finish()

        def last_part(i, carry):
            blk = self.blk(self.far_first(i))
            self.pa[blk, :] = (
                nt(self.dq[blk, :], one.wcols(0, 1))
                + nt(self.dk[blk, :], one.wcols(1, 1))
                + nt(self.dv[blk, :], one.wcols(2, 1))
            ).astype(BF16)
            self.at(i, self.r_dn1.send_far, self.r_dn1.cross, self.r_dn1.send_own)
            return carry

        lax.fori_loop(0, 4, last_part, 0)
        weight_grad(ws.gp, 0, self.full_self, self.dq)
        weight_grad(ws.gp, cols, self.full_self, self.dk)
        ws.reduce.open(0)
        weight_grad(ws.gp, 2 * cols, self.full_self, self.dv)
        weight_grad(ws.gp, 3 * cols, self.dy1, one.ctx)
        ws.reduce.open(1)

        keep = self.small[13:15, :]
        self.small[...] = jnp.zeros_like(self.small)
        self.small[:, 0:128] = table_rows(s_, heads, ranges, spot.n)
        self.small[13:15, :] = keep
        wc.reduce.total(0)
        wc.reduce.total(1)
        ws.reduce.first(0)

        def back_one(k, at, value):
            self.gx[at, :] = value.astype(BF16)

        gain_self = self.norm_backward(self.x, gain_s, self.r_dn1, self.g, back_one)
        self.small[12:13, :] = gain_self
        ws.reduce.first(1)
        if zy:
            self.ss.run(spot, self.small[...], self.tot)
        else:
            self.tot[...] = self.small[...]
        for k in range(ROW_CHUNKS):
            self.gm[self.chunk(k), :] = self.r_mem.total(k).astype(BF16)
        ws.reduce.total(0)
        ws.reduce.total(1)

        for gather in self.gathers:
            gather.finish()
        self.r_mem.finish()
        self.r_dn1.finish()
        for group in self.groups:
            group.gather.finish()
            group.reduce.finish()


def deliver(red, tot, passed, sizes, heads):
    rows, model, cols, hid, wrows, length = sizes
    ins, outs = Slots(), Slots()
    packed, small = SimpleNamespace(), SimpleNamespace()
    ins.add(packed, ref=(red, VM))
    ins.add(small, ref=(tot, VM))
    sources, dests = [SimpleNamespace() for _ in passed], [SimpleNamespace() for _ in passed]
    for value, source, dest in zip(passed, sources, dests):
        ins.add(source, ref=(value, VM))
        outs.add(dest, ref=(value.shape, value.dtype))
    cuts, at = [], 0
    for width, turn in [(cols, False)] * 3 + [(cols, True)] + [(cols, False)] * 3 + [(cols, True)] + [(hid, False)] * 3:
        cut = SimpleNamespace(at=at, width=width, turn=turn)
        outs.add(cut, ref=((width, wrows) if turn else (wrows, width), F32))
        cuts.append(cut)
        at += width
    gains, table = [SimpleNamespace() for _ in range(3)], SimpleNamespace()
    for gain in gains:
        outs.add(gain, ref=((model,), F32))
    outs.add(table, ref=((4 * heads, NB), F32))

    def body():
        for source, dest in zip(sources, dests):
            dest.ref[...] = source.ref[...]
        for cut in cuts:
            part = packed.ref[:, cut.at : cut.at + cut.width]
            cut.ref[...] = part.T if cut.turn else part
        for i, gain in enumerate(gains):
            gain.ref[...] = small.ref[12 + i : 13 + i, :].reshape(model)
        table.ref[...] = small.ref[0 : 4 * heads, 0:NB]

    got = run_kernel(body, ins, outs, Slots(), None, "deliver")
    return got[:3], got[3:14], got[14:17], got[17]


def shards(
    zy, inputs, memory, segment_ids, memory_ids, self_gain, self_query, self_key, self_value, self_out, bias_table,
    cross_gain, cross_query, cross_key, cross_value, cross_out, ff_gain, ff_gate, ff_up, ff_down, cotangent,
):
    rows, model = inputs.shape
    length = segment_ids.shape[1]
    wrows, cols = self_query.shape
    hid = ff_gate.shape[1]
    heads = cols // DH
    assert segment_ids.shape[0] == 1 and rows == QB and length == 4 * QB == memory_ids.shape[1]
    sizes = (rows, model, cols, hid, wrows, length)
    ins, outs, slots = Slots(), Slots(), Slots()
    layer = Layer.__new__(Layer)
    outs.add(
        layer, result=((rows, model), BF16), gx=((rows, model), BF16), gm=((rows, model), BF16), tot=((16, model), F32)
    )
    if zy:
        outs.add(layer, red=((wrows, 8 * cols + 3 * hid), F32))
    layer.__init__(zy, sizes, ins, outs, slots)
    ins.add(
        layer, x=(inputs, VM), m=(memory, VM), cot=(cotangent, VM), sid=(segment_ids, VM), mid=(memory_ids, VM),
        gain_s=(self_gain, VM), gain_c=(cross_gain, VM), gain_f=(ff_gain, VM), table=(bias_table.T, pltpu.SMEM),
    )
    if zy:
        ins.add(
            layer, sq=(self_query, VM), sk=(self_key, VM), sv=(self_value, VM), so=(self_out, VM),
            cq=(cross_query, VM), ck=(cross_key, VM), cv=(cross_value, VM), co=(cross_out, VM),
            fg=(ff_gate, VM), fu=(ff_up, VM), fd=(ff_down.T, VM),
        )
    else:

        def whole(*parts):
            return lax.all_gather(jnp.concatenate(parts, axis=1), WIDE, axis=0, tiled=True)

        ins.add(layer.ws, w=(whole(self_query, self_key, self_value, self_out.T), VM))
        ins.add(layer.wc, w=(whole(cross_query, cross_key, cross_value, cross_out.T), VM))
        ins.add(layer.wf, w=(whole(ff_gate, ff_up, ff_down.T), VM))
    got = run_kernel(layer.run, ins, outs, slots, 0, "layer")
    if zy:
        total, red = got[3], got[4]
    else:
        packed = jnp.concatenate(got[4:7], axis=1)
        red = lax.psum_scatter(packed, WIDE, scatter_dimension=0, tiled=True).astype(F32)
        total = lax.psum(got[3], (WIDE, NARROW))
    row_outs, grads, gains, table = deliver(red, total, got[:3], sizes, heads)
    return (
        *row_outs,
        gains[0],
        *grads[0:4],
        table.T,
        gains[1],
        *grads[4:8],
        gains[2],
        grads[8],
        grads[9],
        grads[10].T,
    )


def solution(mesh):
    zy = mesh.shape[WIDE] == 8
    rows = P((WIDE, NARROW), None)
    w_in, w_out = P(WIDE, NARROW), P(NARROW, WIDE)
    placed = (
        rows, rows, P(WIDE, None), P(WIDE, None), P(),
        w_in, w_in, w_in, w_out, P(None, NARROW), P(),
        w_in, w_in, w_in, w_out, P(), w_in, w_in, w_out, rows,
    )
    outs = (
        rows, rows, rows, P(), w_in, w_in, w_in, w_out, P(), P(),
        w_in, w_in, w_in, w_out, P(), w_in, w_in, w_out,
    )

    def program(*args):
        return shards(zy, *args)

    return jax.shard_map(program, mesh=mesh, in_specs=placed, out_specs=outs, check_vma=False)
```

time: 1640 us -> 206 us (0.13)
  waiting for transfers between devices: 781 us -> 0 us
  blocking collectives: 401 us -> 0 us
  Pallas kernels: 0 us -> 204 us
  other arithmetic: 202 us -> 0 us
  matrix products: 192 us -> 0 us
  local copies, waits for them, and re-layouts: 39.4 us -> 0 us
    reduce_scatter x14 -> x0, waiting for transfers between devices: 620 us -> none  [the longest x3 115 us: add_branch(): lax.psum_scatter(partial_value, 'narrow', scatter_dimension=0, tiled=True)]
    all_gather x11 -> x0, blocking collectives: 360 us -> none  [the longest x1 35 us: shards(): lax.all_gather(ff_down, 'wide', axis=1, tiled=True)]
    pallas_call x0 -> x2, Pallas kernels: none -> 204 us  [run_kernel(): pl.pallas_call(kernel, out_shape=[jax.ShapeDtypeStruct(*spec) for _, _, s...]
    dot_general x55 -> x0, matrix products: 189 us -> none  [the longest x4 58.5 us: block_scores(): jnp.einsum('hqc,kc->hqk', q_masked, key_rows, preferred_element_type=jnp....]
    unnamed x29 -> x0, waiting for transfers between devices: 133 us -> none
    reduce_sum x14 -> x0, other arithmetic: 99.9 us -> none  [the longest x4 78.6 us: attend_backward(): found[which] = jnp.sum(jnp.where(inside, scores_wide, 0.0), axis=(1, 2))]
    and x17 -> x0, other arithmetic: 51.8 us -> none  [the longest x1 30.5 us: block_scores(): allowed = allowed & (distance >= 0)]
    psum x1 -> x0, blocking collectives: 40.3 us -> none  [shards(): lax.psum((grad_gain_self, grad_gain_cross, grad_gain_ff, table_full), ('w...]
  transfers between devices with their start and end apart: 25 -> 0, of which waited for: 17 -> 0; matrix products, arithmetic and copies ran while one was open for 17% -> 0% of each run, Pallas kernels for 0% -> 0%
where the time goes in v2:
time: 206 us; the launch traced here: 205 us
  Pallas kernels  204 us (99%)
    pallas_call x2, Pallas kernels, run_kernel(): pl.pallas_call(kernel, out_shape=[jax.ShapeDtypeStruct(*spec) for _, _, s...  204 us

profile of v2, /device:TPU:0, one launch (start us, length us, event | category | flops | bytes accessed | tf_op | source)
XLA Modules:
  0.0 204.5 jit_solution(210551018134635187)
XLA Ops:
  0.7 200.4 %layer.1 = (bf16[256,768]{1,0:T(8,128)(2,1)}, bf16[256,768]{1,0:T(8,128)(2,1)}, bf16[256,768]{1,0:T(8,128)(2,1)}, f32[16,768]{1,0:T(8,128)}, f32[96,3072]{1,0:T(8,128)}) custom-call(bf16[256,768]{1,0:T(8,128)(2,1)} %refs_0_.1, bf16[256,768]{1,0:T(8,128)(2,1)} %refs_1_.1, bf16[256,768]{1,0:T(8,128)(2,1)} %refs_2_.1, s32[1,1024]{1,0:T(1,128)} %refs_3_.1, ...), custom_call_target="tpu_custom_call" | custom-call | tf_op jit(solution)/shard_map/layer/pallas_call | solution.py:73
  201.1 3.3 %deliver.1 = (bf16[256,768]{1,0:T(8,128)(2,1)}, bf16[256,768]{1,0:T(8,128)(2,1)}, bf16[256,768]{1,0:T(8,128)(2,1)}, f32[96,192]{1,0:T(8,128)}, f32[96,192]{1,0:T...) custom-call(f32[96,3072]{1,0:T(8,128)} %get-tuple-element.41.refs_0_, ...), custom_call_target="tpu_custom_call" | custom-call | tf_op jit(solution)/shard_map/deliver/pallas_call | solution.py:73

commit v3 on v2

--- a/solution.py
+++ b/solution.py
@@ -15,6 +15,7 @@
 EPS = 1e-06
 NEG = -1e30
 QB = 256
+HALF = 128
 ROW_CHUNKS = 4
 WIDE = "wide"
 NARROW = "narrow"
@@ -167,8 +168,8 @@
         self.to_x(k).start()
         self.to_sib(k).start()
 
-    def send_all(self):
-        for k in range(self.chunks):
+    def send_all(self, first=0, after=ROW_CHUNKS):
+        for k in range(first, after):
             self.send(k)
 
     def forward(self, first, after):
@@ -180,8 +181,8 @@
         for k in range(self.chunks):
             self.from_sib(k).wait_recv()
 
-    def have_xsib(self):
-        for k in range(self.chunks):
+    def have_xsib(self, first, after):
+        for k in range(first, after):
             self.from_onward(k).wait_recv()
 
     def finish(self):
@@ -193,7 +194,7 @@
 
 class RowReduce:
     def __init__(self, slots, rows, cols, chunks=ROW_CHUNKS):
-        self.nrows, self.chunks, self.size = rows, chunks, rows // chunks
+        self.nrows, self.ncols, self.chunks, self.size = rows, cols, chunks, rows // chunks
         sems, buf = DMA((chunks,)), VM((rows, cols), BF16)
         slots.add(self, as_=sems, ar=sems, bs=sems, br=sems, xs=sems, xr=sems, far=buf, own=buf, inn=buf)
 
@@ -204,7 +205,7 @@
         return ref.at[pl.ds(k * self.size, self.size)]
 
     def mine(self, block, k):
-        return self.part.at[aligned(block * self.nrows + k * self.size, self.size)]
+        return self.part.at[aligned(block * self.nrows + k * self.size, self.size), pl.ds(0, self.ncols)]
 
     def far_sib(self, k):
         s = self.spot
@@ -218,16 +219,16 @@
         s = self.spot
         return remote(self.buf(self.far, k), self.buf(self.inn, k), self.xs.at[k], self.xr.at[k], s.at_n(s.xp))
 
-    def send_far(self):
-        for k in range(self.chunks):
+    def send_far(self, first=0, after=ROW_CHUNKS):
+        for k in range(first, after):
             self.far_sib(k).start()
 
     def send_own(self):
         for k in range(self.chunks):
             self.own_sib(k).start()
 
-    def cross(self):
-        for k in range(self.chunks):
+    def cross(self, first=0, after=ROW_CHUNKS):
+        for k in range(first, after):
             self.far_sib(k).wait_recv()
             here = self.buf(self.far, k)
             here[...] = (self.mine(self.spot.xp, k)[...].astype(F32) + here[...].astype(F32)).astype(BF16)
@@ -249,35 +250,37 @@
 class WideGather:
     steps = (1, -1, 2, -2, 3, -3)
 
-    def __init__(self, slots, rows, halves=2):
-        self.nrows, self.halves, self.size = rows, halves, rows // halves
-        slots.add(self, zs=DMA((6, halves)), zr=DMA((4, halves)), ys=DMA((4, halves)), yr=DMA((4, halves)))
+    def __init__(self, slots, rows, widths):
+        self.nrows, self.widths, self.parts = rows, widths, range(len(widths))
+        four = DMA((4, len(widths)))
+        slots.add(self, zs=DMA((6, len(widths))), zr=four, ys=four, yr=four)
 
     def bind(self, spot, full):
         self.spot, self.full = spot, full
 
-    def rows(self, z, y, half):
-        return self.full.at[aligned((z * 2 + y) * self.nrows + half * self.size, self.size)]
-
-    def along(self, i, half):
+    def rows(self, z, y, part):
+        cols = pl.ds(sum(self.widths[:part]), self.widths[part])
+        return self.full.at[aligned((z * 2 + y) * self.nrows, self.nrows), cols]
+
+    def along(self, i, part):
         s = self.spot
-        rows = self.rows(s.z, s.y, half)
-        return remote(rows, rows, self.zs.at[i, half], self.zr.at[s.z, half], s.at_z(s.z + self.steps[i]))
-
-    def came(self, z, half):
+        rows = self.rows(s.z, s.y, part)
+        return remote(rows, rows, self.zs.at[i, part], self.zr.at[s.z, part], s.at_z(s.z + self.steps[i]))
+
+    def came(self, z, part):
         s = self.spot
-        rows = self.rows(z, s.y, half)
-        return remote(rows, rows, self.zs.at[0, half], self.zr.at[z, half], s.at_z(z))
-
-    def over(self, z, half):
+        rows = self.rows(z, s.y, part)
+        return remote(rows, rows, self.zs.at[0, part], self.zr.at[z, part], s.at_z(z))
+
+    def over(self, z, part):
         s = self.spot
-        rows = self.rows(z, s.y, half)
-        return remote(rows, rows, self.ys.at[z, half], self.yr.at[z, half], s.at_w(s.yp))
-
-    def crossed(self, z, half):
+        rows = self.rows(z, s.y, part)
+        return remote(rows, rows, self.ys.at[z, part], self.yr.at[z, part], s.at_w(s.yp))
+
+    def crossed(self, z, part):
         s = self.spot
-        rows = self.rows(z, 1 - s.y, half)
-        return remote(rows, rows, self.ys.at[z, half], self.yr.at[z, half], s.at_w(s.yp))
+        rows = self.rows(z, 1 - s.y, part)
+        return remote(rows, rows, self.ys.at[z, part], self.yr.at[z, part], s.at_w(s.yp))
 
     def when_inside(self, step, fn):
         there = self.spot.z + step
@@ -286,34 +289,36 @@
         def _():
             fn(there)
 
-    def open(self):
-        for half in range(self.halves):
-            self.over(self.spot.z, half).start()
-        for i, step in enumerate(self.steps):
-            for half in range(self.halves):
-                self.when_inside(step, lambda there: self.along(i, half).start())
-
-    def forward(self, distance):
-        for half in range(self.halves):
+    def open_y(self):
+        for part in self.parts:
+            self.over(self.spot.z, part).start()
+
+    def open_z(self):
+        for part in self.parts:
+            for i, step in enumerate(self.steps):
+                self.when_inside(step, lambda there: self.along(i, part).start())
+
+    def forward(self, distance, *parts):
+        for part in parts or self.parts:
             for step in (distance, -distance):
 
                 def pass_on(there):
-                    self.came(there, half).wait_recv()
-                    self.over(there, half).start()
+                    self.came(there, part).wait_recv()
+                    self.over(there, part).start()
 
                 self.when_inside(step, pass_on)
 
-    def have(self):
-        for half in range(self.halves):
+    def have(self, *parts):
+        for part in parts or self.parts:
             for z in range(4):
-                self.crossed(z, half).wait_recv()
+                self.crossed(z, part).wait_recv()
 
     def finish(self):
-        for half in range(self.halves):
+        for part in self.parts:
             for z in range(4):
-                self.over(z, half).wait_send()
+                self.over(z, part).wait_send()
             for i, step in enumerate(self.steps):
-                self.when_inside(step, lambda there: self.along(i, half).wait_send())
+                self.when_inside(step, lambda there: self.along(i, part).wait_send())
 
 
 class WideReduce:
@@ -387,34 +392,42 @@
             self, ps=DMA((3,)), pr=DMA((3,)), zs=DMA((4,)), zr=DMA((4,)), held=four, inn=VM((3, rows, cols), F32), zin=four
         )
 
-    def run(self, spot, value, out):
-        held, inn, zin = self.held, self.inn, self.zin
-        held[0] = value
-        devs = (spot.at_n(spot.sib), spot.at_n(spot.xp), spot.at_w(spot.yp))
-        copies = []
+    def bind(self, spot):
+        self.spot = spot
+
+    def pair(self, i):
+        s = self.spot
+        dev = (s.at_n(s.sib), s.at_n(s.xp), s.at_w(s.yp))[i]
+        return remote(self.held.at[i], self.inn.at[i], self.ps.at[i], self.pr.at[i], dev)
+
+    def hop(self, step, landed):
+        other = (self.spot.z + step) % 4
+        return remote(
+            self.held.at[3], self.zin.at[landed], self.zs.at[step], self.zr.at[landed], self.spot.at_z(other)
+        )
+
+    def begin(self, value):
+        self.held[0] = value
+        self.pair(0).start()
+
+    def step(self, i):
+        self.pair(i).wait_recv()
+        self.held[i + 1] = self.held[i] + self.inn[i]
+        if i < 2:
+            self.pair(i + 1).start()
+        else:
+            self.zin[self.spot.z] = self.held[3]
+            for step in range(1, 4):
+                self.hop(step, self.spot.z).start()
+
+    def end(self, out):
+        for step in range(1, 4):
+            self.hop(step, (self.spot.z + step) % 4).wait_recv()
+        out[...] = ((self.zin[0] + self.zin[1]) + self.zin[2]) + self.zin[3]
         for i in range(3):
-            copy = remote(held.at[i], inn.at[i], self.ps.at[i], self.pr.at[i], devs[i])
-            copy.start()
-            copies.append(copy)
-            copy.wait_recv()
-            held[i + 1] = held[i] + inn[i]
-        zin[spot.z] = held[3]
-
-        def hop(step, landed):
-            other = (spot.z + step) % 4
-            return remote(
-                held.at[3], zin.at[landed], self.zs.at[step], self.zr.at[landed], spot.at_z(other)
-            )
-
+            self.pair(i).wait_send()
         for step in range(1, 4):
-            hop(step, spot.z).start()
-        for step in range(1, 4):
-            hop(step, (spot.z + step) % 4).wait_recv()
-        out[...] = ((zin[0] + zin[1]) + zin[2]) + zin[3]
-        for copy in copies:
-            copy.wait_send()
-        for step in range(1, 4):
-            hop(step, spot.z).wait_send()
+            self.hop(step, self.spot.z).wait_send()
 
 
 class Idle:
@@ -423,7 +436,7 @@
     def bind(self, *args):
         pass
 
-    open = forward = have = finish = first = total = bind
+    open = open_y = open_z = forward = have = finish = first = total = bind
 
 
 def nt(left, right):
@@ -473,6 +486,21 @@
         rows = rows // 2
         tile = tile[:rows] + pltpu.roll(tile[rows:], width - rows, 1)
     return tile
+
+
+class Tile:
+    def __init__(self, slot, first, second):
+        self.slot, self.halves = slot, (first, second)
+
+    def rows(self, half):
+        return aligned(half * HALF, HALF)
+
+    def load(self, ref):
+        return jnp.concatenate([ref[self.rows(h), :] for h in self.halves], axis=0)
+
+    def store(self, ref, value, at=0):
+        for i, h in enumerate(self.halves):
+            ref[self.rows(h), at : at + value.shape[1]] = value[i * HALF : (i + 1) * HALF]
 
 
 class Attention:
@@ -493,10 +521,11 @@
     def wcols(self, first, count):
         return self.w[:, first * self.cols : (first + count) * self.cols]
 
-    def mask(self, b, kb):
+    def mask(self, t, kb):
         sk = self.kcol[self.blk(kb), :]
         sk = jnp.concatenate([sk, sk], axis=1)
-        return jnp.where(sk == self.shared.segq[b], 0.0, NEG)
+        sq = jnp.concatenate([self.shared.segq[h] for h in t.halves], axis=1)
+        return jnp.where(sk == sq, 0.0, NEG)
 
     def score(self, k, q, madd, h, kind):
         s = nt(k, q) + madd
@@ -504,17 +533,17 @@
             s = s + self.shared.bias[kind, h]
         return s
 
-    def kind(self, b, kb):
-        return jnp.minimum(b - kb, 2) if self.causal else None
-
-    def key_blocks(self, b):
-        return b + 1 if self.causal else 4
+    def kind(self, t, kb):
+        return jnp.minimum(t.slot - kb, 2) if self.causal else None
+
+    def key_blocks(self, t):
+        return (jnp.maximum(t.slot - 2, 0), t.slot + 1) if self.causal else (0, 4)
 
     def project_kv(self, source):
         c = self.cols
 
         def one(b, carry):
-            kv = nn(source[self.blk(b), :], self.wcols(1, 2))
+            kv = nn(source[self.blk(b), :], self.wcols(0, 2))
             k, v = kv[:, :c], kv[:, c:]
             self.k[self.blk(b), :] = k.astype(BF16)
             self.v[self.blk(b), :] = v.astype(BF16)
@@ -524,11 +553,11 @@
 
         lax.fori_loop(0, 4, one, 0)
 
-    def project_q(self, source, b):
-        self.q[self.blk(b), :] = nn(source[self.blk(b), :], self.wcols(0, 1)).astype(BF16)
-
-    def out_part(self, dest, b):
-        dest[self.blk(b), :] = nt(self.ctx[self.blk(b), :], self.wcols(3, 1)).astype(BF16)
+    def project_q(self, source, t):
+        t.store(self.q, nn(t.load(source), self.wcols(2, 1)).astype(BF16))
+
+    def out_part(self, dest, t):
+        t.store(dest, nt(t.load(self.ctx), self.wcols(3, 1)).astype(BF16))
 
     def rows_of(self, h):
         return slice(h * DH, (h + 1) * DH)
@@ -536,9 +565,9 @@
     def wide_of(self, h):
         return slice(h * QB, (h + 1) * QB)
 
-    def forward(self, b):
+    def forward(self, t):
         s_ = self.shared
-        q = self.q[self.blk(b), :]
+        q = t.load(self.q)
         for h in range(self.heads):
             s_.qm[self.wide_of(h), :] = head_rows(q, h)
         s_.peak[...] = jnp.full_like(s_.peak, NEG)
@@ -546,11 +575,11 @@
         s_.oacc[...] = jnp.zeros_like(s_.oacc)
 
         def tile(kb, carry):
-            madd = self.mask(b, kb)
+            madd = self.mask(t, kb)
             k = self.k[self.blk(kb), :]
             for h in range(self.heads):
                 hs = self.rows_of(h)
-                s = self.score(k, s_.qm[self.wide_of(h), :], madd, h, self.kind(b, kb))
+                s = self.score(k, s_.qm[self.wide_of(h), :], madd, h, self.kind(t, kb))
                 old = s_.peak[h]
                 new = jnp.maximum(old, jnp.max(s, axis=0, keepdims=True))
                 fade = jnp.exp(old - new)
@@ -560,17 +589,17 @@
                 s_.oacc[hs, :] = s_.oacc[hs, :] * fade + nn(self.vt[kb, hs, :], x.astype(BF16))
             return carry
 
-        lax.fori_loop(0, self.key_blocks(b), tile, 0)
+        lax.fori_loop(*self.key_blocks(t), tile, 0)
         for h in range(self.heads):
             hs = self.rows_of(h)
             s_.oacc[hs, :] = s_.oacc[hs, :] / s_.total[h]
-            self.lse[b, h] = s_.peak[h] + jnp.log(s_.total[h])
-        self.ctx[self.blk(b), :] = s_.oacc[...].T.astype(BF16)
-
-    def backward(self, b, dctx):
+            self.lse[t.slot, h] = s_.peak[h] + jnp.log(s_.total[h])
+        t.store(self.ctx, s_.oacc[...].T.astype(BF16))
+
+    def backward(self, t, dctx):
         s_ = self.shared
-        q = self.q[self.blk(b), :]
-        prod = (dctx.astype(F32) * self.ctx[self.blk(b), :].astype(F32)).T
+        q = t.load(self.q)
+        prod = (dctx.astype(F32) * t.load(self.ctx).astype(F32)).T
         for h in range(self.heads):
             s_.qm[self.wide_of(h), :] = head_rows(q, h)
             s_.dm[self.wide_of(h), :] = head_rows(dctx, h)
@@ -578,13 +607,13 @@
         s_.oacc[...] = jnp.zeros_like(s_.oacc)
 
         def tile(kb, carry):
-            madd = self.mask(b, kb)
+            madd = self.mask(t, kb)
             keys = self.blk(kb)
             k, v = self.k[keys, :], self.v[keys, :]
-            kind = self.kind(b, kb)
+            kind = self.kind(t, kb)
             for h in range(self.heads):
                 hs, wide = self.rows_of(h), self.wide_of(h)
-                p = jnp.exp(self.score(k, s_.qm[wide, :], madd, h, kind) - self.lse[b, h])
+                p = jnp.exp(self.score(k, s_.qm[wide, :], madd, h, kind) - self.lse[t.slot, h])
                 ds = p * (nt(v, s_.dm[wide, :]) - s_.total[h])
                 if self.causal:
                     s_.gb[kind, h] += ds
@@ -596,7 +625,7 @@
             s_.dka[keys, :] += nn(s_.dcat[...], s_.qm[...])
             return carry
 
-        lax.fori_loop(0, self.key_blocks(b), tile, 0)
+        lax.fori_loop(*self.key_blocks(t), tile, 0)
         return s_.oacc[...].T.astype(BF16)
 
 
@@ -613,11 +642,6 @@
         s_.bias[1, h] = turned[:, QB:]
         s_.bias[2, h] = jnp.full((QB, QB), table[h, NB - 1])
     s_.gb[...] = jnp.zeros_like(s_.gb)
-
-
-def table_rows(s_, heads, ranges, n):
-    near = [diagonal_sums(jnp.concatenate([s_.gb[0, h], s_.gb[1, h]], axis=1)) for h in range(heads)]
-    near = jnp.concatenate(near + [jnp.zeros((8 - heads, 2 * QB), F32)], axis=0)
     lane = lax.broadcasted_iota(jnp.int32, (1, 128), 1)
     first = jnp.full((1, 128), 2 * QB, jnp.int32)
     after = jnp.zeros((1, 128), jnp.int32)
@@ -625,10 +649,18 @@
         first = jnp.where(lane == which, start, first)
         after = jnp.where(lane == which, stop, after)
     dist = lax.broadcasted_iota(jnp.int32, (2 * QB, 128), 0)
-    pick = jnp.where(jnp.logical_and(dist >= first, dist < after), 1.0, 0.0)
-    sums = lax.dot_general(
-        near, pick, (((1,), (0,)), ((), ())), precision=lax.Precision.HIGHEST, preferred_element_type=F32
-    )
+    s_.pick[...] = jnp.where(jnp.logical_and(dist >= first, dist < after), 1.0, 0.0).astype(BF16)
+
+
+def table_rows(s_, heads, n):
+    near = [diagonal_sums(jnp.concatenate([s_.gb[0, h], s_.gb[1, h]], axis=1)) for h in range(heads)]
+    near = jnp.concatenate(near + [jnp.zeros((8 - heads, 2 * QB), F32)], axis=0)
+    sums = jnp.zeros((8, 128), F32)
+    for _ in range(3):
+        term = near.astype(BF16)
+        sums = sums + nn(term, s_.pick[...])
+        near = near - term.astype(F32)
+    lane = lax.broadcasted_iota(jnp.int32, (1, 128), 1)
     place = lax.broadcasted_iota(jnp.int32, (16, 128), 0)
     rows = jnp.zeros((16, 128), F32)
     for h in range(heads):
@@ -638,12 +670,10 @@
     return rows
 
 
-def weight_grad(dest, column, left, right):
-    width = right.shape[1]
-
+def weight_grad(dest, column, left, right, first, width):
     def one(m, carry):
         part = pl.ds(pl.multiple_of(m * 256, 256), 256)
-        dest[part, column : column + width] = tn(left[:, part], right[...]).astype(BF16)
+        dest[part, column : column + width] = tn(left[:, part], right[:, first : first + width]).astype(BF16)
         return carry
 
     lax.fori_loop(0, left.shape[1] // 256, one, 0)
@@ -661,27 +691,32 @@
         wide_rows, acc = VM((heads * QB, cols), BF16), VM((length, cols), F32)
         line, tiles, cat = VM((heads, 1, QB), F32), VM((3, heads, QB, QB), F32), VM((QB, heads * QB), BF16)
         slots.add(
-            s_, segq=VM((4, 1, QB), F32), bias=tiles, gb=tiles, qm=wide_rows, dm=wide_rows, peak=line, total=line,
-            oacc=VM((cols, QB), F32), pcat=cat, dcat=cat, dva=acc, dka=acc,
+            s_, segq=VM((length // HALF, 1, HALF), F32), bias=tiles, gb=tiles, qm=wide_rows, dm=wide_rows, peak=line, total=line,
+            oacc=VM((cols, QB), F32), pcat=cat, dcat=cat, dva=acc, dka=acc, pick=VM((2 * QB, 128), BF16),
         )
-        full, own, head_out = VM((length, model), BF16), VM((rows, model), F32), VM((length, cols), BF16)
+        full, own = VM((length, model), BF16), VM((rows, model), F32)
         slots.add(
             self, full_self=full, full_mem=full, full_cross=full, full_ff=full, dy3=full, dy2=full, dy1=full,
-            pa=full, pb=full, x_two=own, x_three=own, g=own, dq=head_out, dk=head_out, dv=head_out,
+            pa=full, pb=full, x_two=own, x_three=own, g=own, dkvq=VM((length, 3 * cols), BF16),
             hidden=VM((length, hid), BF16), dgu=VM((length, 2 * hid), BF16), small=VM((16, model), F32),
         )
         self.gathers = [RowGather(slots, rows) for _ in range(7)]
         self.g_self, self.g_mem, self.g_cross, self.g_ff, self.g_dy3, self.g_dy2, self.g_dy1 = self.gathers
         self.reduces = [RowReduce(slots, rows, model) for _ in range(7)]
         self.r_out1, self.r_out2, self.r_out3, self.r_dn3, self.r_dn2, self.r_mem, self.r_dn1 = self.reduces
-        self.groups = [SimpleNamespace(width=w) for w in (4 * cols, 4 * cols, 3 * hid)]
+        kinds = (
+            (4 * cols, (2 * cols, 256, 4 * cols - 2 * cols - 256), 128),
+            (4 * cols, (2 * cols, 2 * cols), 384),
+            (3 * hid, (768, 3 * hid - 768), 384),
+        )
+        self.groups = [SimpleNamespace(width=w, parts=p, step=s) for w, p, s in kinds]
         self.ws, self.wc, self.wf = self.groups
         for group in self.groups:
             if zy:
                 both = VM((model, group.width), BF16)
                 slots.add(group, w=both, gp=both)
-                group.gather = WideGather(slots, wrows)
-                group.reduce = WideReduce(slots, wrows, group.width, 384)
+                group.gather = WideGather(slots, wrows, group.parts)
+                group.reduce = WideReduce(slots, wrows, group.width, group.step)
             else:
                 outs.add(group, gp=((model, group.width), BF16))
                 group.gather = group.reduce = Idle()
@@ -700,10 +735,20 @@
         far = jnp.where(i < 2, 1 - s.x, s.x)
         return far * 2 + jnp.where(i % 2 == 0, 1 - s.c, s.c)
 
-    def near_first(self, i):
+    def near_tile(self, i):
+        s = self.spot
+        near = jnp.where(i == 0, s.n, s.sib)
+        first = jnp.where(i < 2, 2 * near, 2 * s.xsib + i - 2)
+        second = jnp.where(i < 2, 2 * near + 1, 2 * s.xp + i - 2)
+        return Tile(i, first, second)
+
+    def near_block(self, i):
         s = self.spot
         far = jnp.where(i < 2, s.x, 1 - s.x)
-        return far * 2 + jnp.where(jnp.logical_or(i == 0, i == 3), s.c, 1 - s.c)
+        return far * 2 + jnp.where(i % 2 == 0, s.c, 1 - s.c)
+
+    def block_tile(self, b):
+        return Tile(b, 2 * b, 2 * b + 1)
 
     def near_waits(self, i, gather):
         @pl.when(i == 1)
@@ -713,8 +758,13 @@
 
         @pl.when(i == 2)
         def _():
-            gather.forward(1, ROW_CHUNKS)
-            gather.have_xsib()
+            gather.forward(1, 2)
+            gather.have_xsib(0, 2)
+
+        @pl.when(i == 3)
+        def _():
+            gather.forward(2, 4)
+            gather.have_xsib(2, 4)
 
     def near_sends(self, i, reduce):
         @pl.when(i == 1)
@@ -723,11 +773,13 @@
 
         @pl.when(i == 2)
         def _():
-            reduce.send_far()
+            reduce.send_far(0, 2)
+            reduce.cross(0, 2)
 
         @pl.when(i == 3)
         def _():
-            reduce.cross()
+            reduce.send_far(2, 4)
+            reduce.cross(2, 4)
 
     def at(self, i, *actions):
         for j, action in enumerate(actions):
@@ -740,20 +792,26 @@
         parts = [p if p.shape[0] == rows else p.T for p in parts]
         group.w[aligned(self.spot.w * rows, rows), :] = jnp.concatenate(parts, axis=1).astype(BF16)
 
-    def ff_block(self, b):
+    def ff_tile(self, t):
         f = self.sizes[3]
         step = f // 2
-        w, blk = self.wf.w, self.blk(b)
-        x, dy = self.full_ff[blk, :], self.dy3[blk, :]
+        w = self.wf.w
+        x, dy = t.load(self.full_ff), t.load(self.dy3)
         for j in range(0, f, step):
             gate = nn(x, w[:, j : j + step])
             up = nn(x, w[:, f + j : f + j + step])
             dh = nn(dy, w[:, 2 * f + j : 2 * f + j + step])
             value, slope = gelu_parts(gate)
-            self.hidden[blk, j : j + step] = (value * up).astype(BF16)
-            self.dgu[blk, j : j + step] = (dh * up * slope).astype(BF16)
-            self.dgu[blk, f + j : f + j + step] = (dh * value).astype(BF16)
-        self.pa[blk, :] = nt(self.dgu[blk, :], w[:, : 2 * f]).astype(BF16)
+            t.store(self.hidden, (value * up).astype(BF16), j)
+            t.store(self.dgu, (dh * up * slope).astype(BF16), j)
+            t.store(self.dgu, (dh * value).astype(BF16), f + j)
+        t.store(self.pa, nt(t.load(self.dgu), w[:, : 2 * f]).astype(BF16))
+
+    def grads_kv(self):
+        c = self.sizes[2]
+        self.dkvq[:, : 2 * c] = jnp.concatenate(
+            [self.shared.dka[...], self.shared.dva[...]], axis=1
+        ).astype(BF16)
 
     def norm_backward(self, values, gain, reduce, base, done):
         gain_sum = jnp.zeros((1, self.sizes[1]), F32)
@@ -776,7 +834,7 @@
         ):
             gather.bind(spot, full)
         for reduce, part in zip(
-            self.reduces, (self.pa, self.pb, self.pb, self.pa, self.pa, self.pb, self.pa)
+            self.reduces, (self.pa, self.pb, self.pb, self.pa, self.pa, self.dgu, self.pa)
         ):
             reduce.bind(spot, part)
         column = 0
@@ -789,85 +847,100 @@
         gain_s, gain_c, gain_f = (ref[...].reshape(1, model) for ref in (self.gain_s, self.gain_c, self.gain_f))
 
         if zy:
-            self.pack(ws, self.sq, self.sk, self.sv, self.so)
-        ws.gather.open()
+            self.ss.bind(spot)
+            self.pack(ws, self.sk, self.sv, self.sq, self.so)
+        ws.gather.open_z()
+        ws.gather.open_y()
         for k in range(ROW_CHUNKS):
             x = self.x[self.chunk(k), :].astype(F32)
             self.full_self[self.chunk(k, spot.n), :] = norm_rows(x, gain_s).astype(BF16)
             self.g_self.send(k)
         self.full_mem[self.blk(spot.n), :] = self.m[...]
         self.g_mem.send_all()
+        self.dy3[self.blk(spot.n), :] = self.cot[...]
+        self.g_dy3.send_all(0, 2)
         if zy:
-            self.pack(wc, self.cq, self.ck, self.cv, self.co)
+            self.pack(wc, self.ck, self.cv, self.cq, self.co)
             self.pack(wf, self.fg, self.fu, self.fd)
         ranges = bucket_ranges(2 * QB)
-        for attention, ids in ((one, self.sid), (two, self.mid)):
-            values = ids[...].astype(F32)
-            attention.kcol[...] = jnp.broadcast_to(values, (128, length)).T
-        for b in range(4):
-            s_.segq[b] = self.sid[:, b * QB : (b + 1) * QB].astype(F32)
+        values = self.sid[...].astype(F32)
+        one.kcol[...] = jnp.broadcast_to(values, (128, length)).T
+        for h in range(length // HALF):
+            s_.segq[h] = values[:, h * HALF : (h + 1) * HALF]
         make_bias(s_, self.table, heads, ranges)
-        ws.gather.forward(1)
+        ws.gather.forward(1, 0)
+        ws.gather.forward(2, 0)
         self.g_self.forward(0, 2)
-        ws.gather.forward(2)
+        ws.gather.forward(3, 0)
+        ws.gather.forward(1, 1)
         self.g_self.forward(2, 4)
-        ws.gather.forward(3)
-        wc.gather.open()
+        ws.gather.forward(2, 1)
+        ws.gather.forward(3, 1)
         self.g_self.have_sib()
-        self.g_self.have_xsib()
-        ws.gather.have()
+        self.g_self.have_xsib(0, 4)
+        ws.gather.have(0)
+        wc.gather.open_z()
 
         one.project_kv(self.full_self)
+        for distance in (1, 2, 3):
+            ws.gather.forward(distance, 2)
+        wc.gather.open_y()
+        ws.gather.have(1, 2)
 
         def self_block(i, carry):
             b = self.far_first(i)
-            one.project_q(self.full_self, b)
-            one.forward(b)
-            one.out_part(self.pa, b)
+            t = self.block_tile(b)
+            one.project_q(self.full_self, t)
+            one.forward(t)
+            one.out_part(self.pa, t)
 
             def after_first():
                 self.r_out1.send_far()
                 wc.gather.forward(1)
+                wf.gather.open_z()
+                wc.gather.forward(2, 0)
 
             def after_second():
                 self.r_out1.cross()
                 self.g_mem.forward(0, 4)
+                wc.gather.forward(3, 0)
+                wc.gather.forward(2, 1)
 
             def after_third():
                 self.r_out1.send_own()
-                wc.gather.forward(2)
+                wc.gather.forward(3, 1)
+                wf.gather.open_y()
 
             self.at(i, after_first, after_second, after_third)
             return carry
 
         lax.fori_loop(0, 4, self_block, 0)
-        wc.gather.forward(3)
-        wf.gather.open()
+        two.kcol[...] = jnp.broadcast_to(self.mid[...].astype(F32), (128, length)).T
         self.g_mem.have_sib()
-        self.g_mem.have_xsib()
+        self.g_mem.have_xsib(0, 4)
         wc.gather.have()
         two.project_kv(self.full_mem)
-        wf.gather.forward(1)
+        self.g_dy3.forward(0, 2)
         for k in range(ROW_CHUNKS):
             value = self.x[self.chunk(k), :].astype(F32) + self.r_out1.total(k)
             self.x_two[self.chunk(k), :] = value
             self.full_cross[self.chunk(k, spot.n), :] = norm_rows(value, gain_c).astype(BF16)
             self.g_cross.send(k)
-        self.dy3[self.blk(spot.n), :] = self.cot[...]
-        self.g_dy3.send_all()
+        self.g_dy3.send_all(2, 4)
+        wf.gather.forward(1, 0)
 
         def cross_block(i, carry):
-            b = self.near_first(i)
+            t = self.near_tile(i)
             self.near_waits(i, self.g_cross)
-            two.project_q(self.full_cross, b)
-            two.forward(b)
-            two.out_part(self.pb, b)
+            two.project_q(self.full_cross, t)
+            two.forward(t)
+            two.out_part(self.pb, t)
             self.near_sends(i, self.r_out2)
-            self.at(i, None, lambda: wf.gather.forward(2), None, lambda: wf.gather.forward(3))
+            self.at(i, lambda: [wf.gather.forward(2, 0)] and None, lambda: [wf.gather.forward(3, 0), wf.gather.forward(1, 1)] and None, lambda: [wf.gather.forward(2, 1), wf.gather.forward(3, 1)] and None)
             return carry
 
         lax.fori_loop(0, 4, cross_block, 0)
-        self.g_dy3.forward(0, 4)
+        self.g_dy3.forward(2, 4)
         for k in range(ROW_CHUNKS):
             value = self.x_two[self.chunk(k), :] + self.r_out2.total(k)
             self.x_three[self.chunk(k), :] = value
@@ -876,18 +949,17 @@
         self.r_out1.finish()
         self.r_out2.finish()
         self.g_dy3.have_sib()
-        self.g_dy3.have_xsib()
+        self.g_dy3.have_xsib(0, 4)
         wf.gather.have()
 
         def ff_step(i, carry):
-            b = self.near_first(i)
             self.near_waits(i, self.g_ff)
-            self.ff_block(b)
+            self.ff_tile(self.near_tile(i))
             self.near_sends(i, self.r_dn3)
             return carry
 
         lax.fori_loop(0, 4, ff_step, 0)
-        weight_grad(wf.gp, 0, self.full_ff, self.dgu)
+        weight_grad(wf.gp, 0, self.full_ff, self.dgu, 0, 2 * hid)
         split = wf.reduce.chunks * 2 // 3
         for c in range(split):
             wf.reduce.open(c)
@@ -899,7 +971,7 @@
         lax.fori_loop(0, 4, ff_out, 0)
         self.r_out3.send_far()
         self.r_out3.send_own()
-        weight_grad(wf.gp, 2 * hid, self.dy3, self.hidden)
+        weight_grad(wf.gp, 2 * hid, self.dy3, self.hidden, 0, hid)
         for c in range(split, wf.reduce.chunks):
             wf.reduce.open(c)
 
@@ -910,36 +982,30 @@
 
         gain_ff = self.norm_backward(self.x_three, gain_f, self.r_dn3, self.cot, back_three)
         self.small[14:15, :] = gain_ff
-        self.r_out3.cross()
+        self.r_out3.cross(0, 2)
 
         self.r_dn3.finish()
         s_.dka[...] = jnp.zeros_like(s_.dka)
         s_.dva[...] = jnp.zeros_like(s_.dva)
 
         def cross_back(i, carry):
-            b = self.near_first(i)
-            blk = self.blk(b)
+            t = self.near_tile(i)
             self.near_waits(i, self.g_dy2)
-            dctx = nn(self.dy2[blk, :], two.wcols(3, 1)).astype(BF16)
-            dq = two.backward(b, dctx)
-            self.dq[blk, :] = dq
-            self.pa[blk, :] = nt(dq, two.wcols(0, 1)).astype(BF16)
+            dctx = nn(t.load(self.dy2), two.wcols(3, 1)).astype(BF16)
+            dq = two.backward(t, dctx)
+            t.store(self.dkvq, dq, 2 * cols)
+            t.store(self.pa, nt(dq, two.wcols(2, 1)).astype(BF16))
             self.near_sends(i, self.r_dn2)
             if zy:
                 self.at(i, lambda: wf.reduce.first(0), lambda: wf.reduce.first(1), None, lambda: wf.reduce.first(2))
             return carry
 
         lax.fori_loop(0, 4, cross_back, 0)
-        for k in range(ROW_CHUNKS):
-            value = self.x_three[self.chunk(k), :] + self.r_out3.total(k)
-            self.result[self.chunk(k), :] = value.astype(BF16)
-        self.r_out3.finish()
-        self.dk[...] = s_.dka[...].astype(BF16)
-        self.dv[...] = s_.dva[...].astype(BF16)
+        self.grads_kv()
 
         def memory_part(b, carry):
             blk = self.blk(b)
-            self.pb[blk, :] = (nt(self.dk[blk, :], two.wcols(1, 1)) + nt(self.dv[blk, :], two.wcols(2, 1))).astype(BF16)
+            self.dgu[blk, 0:model] = nt(self.dkvq[blk, : 2 * cols], two.wcols(0, 2)).astype(BF16)
             return carry
 
         lax.fori_loop(0, 4, memory_part, 0)
@@ -955,23 +1021,37 @@
 
         gain_cross = self.norm_backward(self.x_two, gain_c, self.r_dn2, self.g, back_two)
         self.small[13:14, :] = gain_cross
+        self.r_out3.cross(2, 4)
         self.r_mem.cross()
-        weight_grad(wc.gp, 0, self.full_cross, self.dq)
-        weight_grad(wc.gp, cols, self.full_mem, self.dk)
+        weight_grad(wc.gp, 0, self.full_mem, self.dkvq, 0, 2 * cols)
         wc.reduce.open(0)
-        weight_grad(wc.gp, 2 * cols, self.full_mem, self.dv)
-        weight_grad(wc.gp, 3 * cols, self.dy2, two.ctx)
+        weight_grad(wc.gp, 2 * cols, self.full_cross, self.dkvq, 2 * cols, cols)
+        weight_grad(wc.gp, 3 * cols, self.dy2, two.ctx, 0, cols)
         wc.reduce.open(1)
 
         s_.dka[...] = jnp.zeros_like(s_.dka)
         s_.dva[...] = jnp.zeros_like(s_.dva)
 
+        def self_waits(i):
+            @pl.when(i == 1)
+            def _():
+                self.g_dy1.have_sib()
+                self.g_dy1.forward(0, 1)
+
+            @pl.when(i == 2)
+            def _():
+                self.g_dy1.forward(1, 4)
+
+            @pl.when(i == 3)
+            def _():
+                self.g_dy1.have_xsib(0, 4)
+
         def self_back(i, carry):
-            b = self.near_first(i)
-            blk = self.blk(b)
-            self.near_waits(i, self.g_dy1)
-            dctx = nn(self.dy1[blk, :], one.wcols(3, 1)).astype(BF16)
-            self.dq[blk, :] = one.backward(b, dctx)
+            b = self.near_block(i)
+            t = self.block_tile(b)
+            self_waits(i)
+            dctx = nn(t.load(self.dy1), one.wcols(3, 1)).astype(BF16)
+            t.store(self.dkvq, one.backward(t, dctx), 2 * cols)
 
             def ff_totals():
                 for c in range(wf.reduce.chunks):
@@ -981,55 +1061,73 @@
             return carry
 
         lax.fori_loop(0, 4, self_back, 0)
-        self.dk[...] = s_.dka[...].astype(BF16)
-        self.dv[...] = s_.dva[...].astype(BF16)
+        self.grads_kv()
         self.r_dn2.finish()
 
         def last_part(i, carry):
             blk = self.blk(self.far_first(i))
-            self.pa[blk, :] = (
-                nt(self.dq[blk, :], one.wcols(0, 1))
-                + nt(self.dk[blk, :], one.wcols(1, 1))
-                + nt(self.dv[blk, :], one.wcols(2, 1))
-            ).astype(BF16)
-            self.at(i, self.r_dn1.send_far, self.r_dn1.cross, self.r_dn1.send_own)
+            self.pa[blk, :] = nt(self.dkvq[blk, :], one.wcols(0, 3)).astype(BF16)
             return carry
 
-        lax.fori_loop(0, 4, last_part, 0)
-        weight_grad(ws.gp, 0, self.full_self, self.dq)
-        weight_grad(ws.gp, cols, self.full_self, self.dk)
-        ws.reduce.open(0)
-        weight_grad(ws.gp, 2 * cols, self.full_self, self.dv)
-        weight_grad(ws.gp, 3 * cols, self.dy1, one.ctx)
-        ws.reduce.open(1)
-
+        lax.fori_loop(0, 2, last_part, 0)
+        self.r_dn1.send_far()
+        weight_grad(ws.gp, 0, self.full_self, self.dkvq, 0, 3 * cols)
+        weight_grad(ws.gp, 3 * cols, self.dy1, one.ctx, 0, cols)
+        for c in range(ws.reduce.chunks):
+            ws.reduce.open(c)
+        self.r_dn1.cross()
+        lax.fori_loop(2, 4, last_part, 0)
+        self.r_dn1.send_own()
+
+        def gain_part(b, total):
+            blk = self.blk(b)
+            both = self.full_self[blk, :].astype(F32) * self.pa[blk, :].astype(F32)
+            return total + jnp.sum(both, axis=0, keepdims=True)
+
+        gain_self = lax.fori_loop(0, 4, gain_part, jnp.zeros((1, model), F32)) / gain_s
         keep = self.small[13:15, :]
         self.small[...] = jnp.zeros_like(self.small)
-        self.small[:, 0:128] = table_rows(s_, heads, ranges, spot.n)
+        self.small[:, 0:128] = table_rows(s_, heads, spot.n)
+        self.small[12:13, :] = gain_self
         self.small[13:15, :] = keep
-        wc.reduce.total(0)
-        wc.reduce.total(1)
-        ws.reduce.first(0)
-
-        def back_one(k, at, value):
-            self.gx[at, :] = value.astype(BF16)
-
-        gain_self = self.norm_backward(self.x, gain_s, self.r_dn1, self.g, back_one)
-        self.small[12:13, :] = gain_self
-        ws.reduce.first(1)
         if zy:
-            self.ss.run(spot, self.small[...], self.tot)
+            self.ss.begin(self.small[...])
         else:
             self.tot[...] = self.small[...]
         for k in range(ROW_CHUNKS):
+            value = self.x_three[self.chunk(k), :] + self.r_out3.total(k)
+            self.result[self.chunk(k), :] = value.astype(BF16)
+        if zy:
+            self.ss.step(0)
+            ws.reduce.first(0)
+            ws.reduce.first(1)
+        for k in range(ROW_CHUNKS):
             self.gm[self.chunk(k), :] = self.r_mem.total(k).astype(BF16)
-        ws.reduce.total(0)
-        ws.reduce.total(1)
+        for c in range(wc.reduce.chunks):
+            wc.reduce.total(c)
+        if zy:
+            ws.reduce.first(2)
+
+        def back_one(k, at, value):
+            self.gx[at, :] = value.astype(BF16)
+            if zy and k == 1:
+                ws.reduce.first(3)
+            if zy and k == 3:
+                self.ss.step(1)
+
+        self.norm_backward(self.x, gain_s, self.r_dn1, self.g, back_one)
+        if zy:
+            ws.reduce.first(4)
+            self.ss.step(2)
+            ws.reduce.first(5)
+            for c in range(ws.reduce.chunks):
+                ws.reduce.total(c)
+            self.ss.end(self.tot)
 
         for gather in self.gathers:
             gather.finish()
-        self.r_mem.finish()
-        self.r_dn1.finish()
+        for reduce in (self.r_out3, self.r_mem, self.r_dn1):
+            reduce.finish()
         for group in self.groups:
             group.gather.finish()
             group.reduce.finish()
@@ -1045,12 +1143,13 @@
     for value, source, dest in zip(passed, sources, dests):
         ins.add(source, ref=(value, VM))
         outs.add(dest, ref=(value.shape, value.dtype))
-    cuts, at = [], 0
-    for width, turn in [(cols, False)] * 3 + [(cols, True)] + [(cols, False)] * 3 + [(cols, True)] + [(hid, False)] * 3:
+    places = [(i * cols, cols, i % 4 == 3) for i in (2, 0, 1, 3, 6, 4, 5, 7)]
+    places += [(8 * cols + i * hid, hid, False) for i in range(3)]
+    cuts = []
+    for at, width, turn in places:
         cut = SimpleNamespace(at=at, width=width, turn=turn)
         outs.add(cut, ref=((width, wrows) if turn else (wrows, width), F32))
         cuts.append(cut)
-        at += width
     gains, table = [SimpleNamespace() for _ in range(3)], SimpleNamespace()
     for gain in gains:
         outs.add(gain, ref=((model,), F32))
@@ -1104,8 +1203,8 @@
         def whole(*parts):
             return lax.all_gather(jnp.concatenate(parts, axis=1), WIDE, axis=0, tiled=True)
 
-        ins.add(layer.ws, w=(whole(self_query, self_key, self_value, self_out.T), VM))
-        ins.add(layer.wc, w=(whole(cross_query, cross_key, cross_value, cross_out.T), VM))
+        ins.add(layer.ws, w=(whole(self_key, self_value, self_query, self_out.T), VM))
+        ins.add(layer.wc, w=(whole(cross_key, cross_value, cross_query, cross_out.T), VM))
         ins.add(layer.wf, w=(whole(ff_gate, ff_up, ff_down.T), VM))
     got = run_kernel(layer.run, ins, outs, slots, 0, "layer")
     if zy:

time: 206 us -> 188 us (0.913)
  Pallas kernels: 204 us -> 187 us
    pallas_call x2, Pallas kernels: 204 us -> 187 us  [run_kernel(): pl.pallas_call(kernel, out_shape=[jax.ShapeDtypeStruct(*spec) for _, _, s...]
where the time goes in v3:
time: 188 us
  Pallas kernels  187 us (99%)
    pallas_call x2, Pallas kernels, run_kernel(): pl.pallas_call(kernel, out_shape=[jax.ShapeDtypeStruct(*spec) for _, _, s...  187 us

profile of v3, /device:TPU:0, one launch (start us, length us, event | category | flops | bytes accessed | tf_op | source)
XLA Modules:
  0.0 188.1 jit_solution(12721644164810255833)
XLA Ops:
  0.7 184.0 %layer.1 = (bf16[256,768]{1,0:T(8,128)(2,1)}, bf16[256,768]{1,0:T(8,128)(2,1)}, bf16[256,768]{1,0:T(8,128)(2,1)}, f32[16,768]{1,0:T(8,128)}, f32[96,3072]{1,0:T(8,128)}) custom-call(bf16[256,768]{1,0:T(8,128)(2,1)} %refs_0_.1, bf16[256,768]{1,0:T(8,128)(2,1)} %refs_1_.1, bf16[256,768]{1,0:T(8,128)(2,1)} %refs_2_.1, s32[1,1024]{1,0:T(1,128)} %refs_3_.1, ...), custom_call_target="tpu_custom_call" | custom-call | tf_op jit(solution)/shard_map/layer/pallas_call | solution.py:74
  184.7 3.2 %deliver.1 = (bf16[256,768]{1,0:T(8,128)(2,1)}, bf16[256,768]{1,0:T(8,128)(2,1)}, bf16[256,768]{1,0:T(8,128)(2,1)}, f32[96,192]{1,0:T(8,128)}, f32[96,192]{1,0:T...) custom-call(f32[96,3072]{1,0:T(8,128)} %get-tuple-element.41.refs_0_, ...), custom_call_target="tpu_custom_call" | custom-call | tf_op jit(solution)/shard_map/deliver/pallas_call | solution.py:74

commit v4 on v3

--- a/solution.py
+++ b/solution.py
@@ -475,9 +475,21 @@
     return value, slope
 
 
-def head_rows(values, h):
-    lane = lax.broadcasted_iota(jnp.int32, values.shape, 1)
-    return jnp.where(lane // DH == h, values, jnp.zeros_like(values))
+def head_rows(values, h, heads):
+    lane = lax.broadcasted_iota(jnp.int32, values.shape, 1) // DH
+    return jnp.where(jnp.logical_or(lane == h, lane >= heads), values, jnp.zeros_like(values))
+
+
+def document_columns(query_ref, key_ref, ids, first):
+    column = jnp.broadcast_to(ids[...].astype(F32), (128, ids.shape[1])).T[:, :DH]
+    lane = lax.broadcasted_iota(jnp.int32, column.shape, 1)
+    same = column == lane.astype(F32)
+    if query_ref is not None:
+        for ref in query_ref:
+            ref[:, first : first + DH] = jnp.where(same, 1.0, 0.0).astype(BF16)
+    if key_ref is not None:
+        other = jnp.logical_and(jnp.logical_not(same), lane < 4)
+        key_ref[:, first : first + DH] = jnp.where(other, NEG, 0.0).astype(BF16)
 
 
 def diagonal_sums(tile):
@@ -506,14 +518,13 @@
 class Attention:
     def __init__(self, slots, shared, length, cols, causal):
         self.shared, self.cols, self.heads, self.causal = shared, cols, cols // DH, causal
-        rows, turned = VM((length, cols), BF16), VM((4, cols, QB), BF16)
+        rows, marked, turned = VM((length, cols), BF16), VM((length, cols + DH), BF16), VM((4, cols, QB), BF16)
         slots.add(
-            self, q=rows, k=rows, v=rows, ctx=rows, kt=turned, vt=turned,
-            lse=VM((4, self.heads, 1, QB), F32), kcol=VM((length, 128), F32),
+            self, q=marked, k=marked, v=rows, ctx=rows, kt=turned, vt=turned, lse=VM((4, self.heads, 1, QB), F32)
         )
 
-    def bind(self, weights):
-        self.w = weights
+    def bind(self, weights, pcat, dcat):
+        self.w, self.pcat, self.dcat = weights, pcat, dcat
 
     def blk(self, b):
         return aligned(b * QB, QB)
@@ -521,23 +532,28 @@
     def wcols(self, first, count):
         return self.w[:, first * self.cols : (first + count) * self.cols]
 
-    def mask(self, t, kb):
-        sk = self.kcol[self.blk(kb), :]
-        sk = jnp.concatenate([sk, sk], axis=1)
-        sq = jnp.concatenate([self.shared.segq[h] for h in t.halves], axis=1)
-        return jnp.where(sk == sq, 0.0, NEG)
-
-    def score(self, k, q, madd, h, kind):
-        s = nt(k, q) + madd
+    def window(self, t, body):
+        if not self.causal:
+            body(0, 4)
+            return
+        for count in (1, 2, 3):
+            pl.when(jnp.minimum(t.slot + 1, 3) == count)(lambda: body(t.slot + 1 - count, count))
+
+    def keys(self, first, count):
+        return aligned(first * QB, count * QB)
+
+    def score(self, k, h, count):
+        s = nt(k, self.shared.qm[self.wide_of(h), :])
         if self.causal:
-            s = s + self.shared.bias[kind, h]
+            s = s + jnp.concatenate([self.shared.bias[self.kind(j, count), h] for j in range(count)], axis=0)
         return s
 
-    def kind(self, t, kb):
-        return jnp.minimum(t.slot - kb, 2) if self.causal else None
-
-    def key_blocks(self, t):
-        return (jnp.maximum(t.slot - 2, 0), t.slot + 1) if self.causal else (0, 4)
+    def kind(self, j, count):
+        return min(count - 1 - j, 2)
+
+    def over_keys(self, turned, first, count, hs, right):
+        parts = [nn(turned[first + j, hs, :], right[j * QB : (j + 1) * QB]) for j in range(count)]
+        return sum(parts[1:], parts[0])
 
     def project_kv(self, source):
         c = self.cols
@@ -545,7 +561,7 @@
         def one(b, carry):
             kv = nn(source[self.blk(b), :], self.wcols(0, 2))
             k, v = kv[:, :c], kv[:, c:]
-            self.k[self.blk(b), :] = k.astype(BF16)
+            self.k[self.blk(b), :c] = k.astype(BF16)
             self.v[self.blk(b), :] = v.astype(BF16)
             self.kt[b] = k.T.astype(BF16)
             self.vt[b] = v.T.astype(BF16)
@@ -569,31 +585,20 @@
         s_ = self.shared
         q = t.load(self.q)
         for h in range(self.heads):
-            s_.qm[self.wide_of(h), :] = head_rows(q, h)
-        s_.peak[...] = jnp.full_like(s_.peak, NEG)
-        s_.total[...] = jnp.zeros_like(s_.total)
-        s_.oacc[...] = jnp.zeros_like(s_.oacc)
-
-        def tile(kb, carry):
-            madd = self.mask(t, kb)
-            k = self.k[self.blk(kb), :]
+            s_.qm[self.wide_of(h), :] = head_rows(q, h, self.heads)
+
+        def attend(first, count):
+            k = self.k[self.keys(first, count), :]
             for h in range(self.heads):
                 hs = self.rows_of(h)
-                s = self.score(k, s_.qm[self.wide_of(h), :], madd, h, self.kind(t, kb))
-                old = s_.peak[h]
-                new = jnp.maximum(old, jnp.max(s, axis=0, keepdims=True))
-                fade = jnp.exp(old - new)
-                x = jnp.exp(s - new)
-                s_.peak[h] = new
-                s_.total[h] = s_.total[h] * fade + jnp.sum(x, axis=0, keepdims=True)
-                s_.oacc[hs, :] = s_.oacc[hs, :] * fade + nn(self.vt[kb, hs, :], x.astype(BF16))
-            return carry
-
-        lax.fori_loop(*self.key_blocks(t), tile, 0)
-        for h in range(self.heads):
-            hs = self.rows_of(h)
-            s_.oacc[hs, :] = s_.oacc[hs, :] / s_.total[h]
-            self.lse[t.slot, h] = s_.peak[h] + jnp.log(s_.total[h])
+                s = self.score(k, h, count)
+                peak = jnp.max(s, axis=0, keepdims=True)
+                x = jnp.exp(s - peak)
+                total = jnp.sum(x, axis=0, keepdims=True)
+                s_.oacc[hs, :] = self.over_keys(self.vt, first, count, hs, x.astype(BF16)) / total
+                self.lse[t.slot, h] = peak + jnp.log(total)
+
+        self.window(t, attend)
         t.store(self.ctx, s_.oacc[...].T.astype(BF16))
 
     def backward(self, t, dctx):
@@ -601,31 +606,28 @@
         q = t.load(self.q)
         prod = (dctx.astype(F32) * t.load(self.ctx).astype(F32)).T
         for h in range(self.heads):
-            s_.qm[self.wide_of(h), :] = head_rows(q, h)
-            s_.dm[self.wide_of(h), :] = head_rows(dctx, h)
-            s_.total[h] = jnp.sum(prod[self.rows_of(h), :], axis=0, keepdims=True)
-        s_.oacc[...] = jnp.zeros_like(s_.oacc)
-
-        def tile(kb, carry):
-            madd = self.mask(t, kb)
-            keys = self.blk(kb)
+            s_.qm[self.wide_of(h), :] = head_rows(q, h, self.heads)
+            s_.dm[self.wide_of(h), :] = head_rows(dctx, h, self.heads)
+            s_.delta[h] = jnp.sum(prod[self.rows_of(h), :], axis=0, keepdims=True)
+
+        def attend(first, count):
+            keys, span = self.keys(first, count), count * QB
             k, v = self.k[keys, :], self.v[keys, :]
-            kind = self.kind(t, kb)
             for h in range(self.heads):
                 hs, wide = self.rows_of(h), self.wide_of(h)
-                p = jnp.exp(self.score(k, s_.qm[wide, :], madd, h, kind) - self.lse[t.slot, h])
-                ds = p * (nt(v, s_.dm[wide, :]) - s_.total[h])
+                p = jnp.exp(self.score(k, h, count) - self.lse[t.slot, h])
+                ds = p * (nt(v, s_.dm[wide, :]) - s_.delta[h])
                 if self.causal:
-                    s_.gb[kind, h] += ds
+                    for j in range(count):
+                        s_.gb[self.kind(j, count), h] += ds[j * QB : (j + 1) * QB]
                 low = ds.astype(BF16)
-                s_.pcat[:, wide] = p.astype(BF16)
-                s_.dcat[:, wide] = low
-                s_.oacc[hs, :] += nn(self.kt[kb, hs, :], low)
-            s_.dva[keys, :] += nn(s_.pcat[...], s_.dm[...])
-            s_.dka[keys, :] += nn(s_.dcat[...], s_.qm[...])
-            return carry
-
-        lax.fori_loop(*self.key_blocks(t), tile, 0)
+                self.pcat[:span, wide] = p.astype(BF16)
+                self.dcat[:span, wide] = low
+                s_.oacc[hs, :] = self.over_keys(self.kt, first, count, hs, low)
+            s_.dva[keys, :] += nn(self.pcat[:span, :], s_.dm[...])
+            s_.dka[keys, :] += nn(self.dcat[:span, :], s_.qm[...])
+
+        self.window(t, attend)
         return s_.oacc[...].T.astype(BF16)
 
 
@@ -689,16 +691,17 @@
         self.one = Attention(slots, s_, length, cols, True)
         self.two = Attention(slots, s_, length, cols, False)
         wide_rows, acc = VM((heads * QB, cols), BF16), VM((length, cols), F32)
-        line, tiles, cat = VM((heads, 1, QB), F32), VM((3, heads, QB, QB), F32), VM((QB, heads * QB), BF16)
+        marked, marked_acc = VM((heads * QB, cols + DH), BF16), VM((length, cols + DH), F32)
+        line, tiles = VM((heads, 1, QB), F32), VM((3, heads, QB, QB), F32)
         slots.add(
-            s_, segq=VM((length // HALF, 1, HALF), F32), bias=tiles, gb=tiles, qm=wide_rows, dm=wide_rows, peak=line, total=line,
-            oacc=VM((cols, QB), F32), pcat=cat, dcat=cat, dva=acc, dka=acc, pick=VM((2 * QB, 128), BF16),
+            s_, bias=tiles, gb=tiles, qm=marked, dm=wide_rows, delta=line,
+            oacc=VM((cols, QB), F32), dva=acc, dka=marked_acc, pick=VM((2 * QB, 128), BF16),
         )
         full, own = VM((length, model), BF16), VM((rows, model), F32)
         slots.add(
             self, full_self=full, full_mem=full, full_cross=full, full_ff=full, dy3=full, dy2=full, dy1=full,
             pa=full, pb=full, x_two=own, x_three=own, g=own, dkvq=VM((length, 3 * cols), BF16),
-            hidden=VM((length, hid), BF16), dgu=VM((length, 2 * hid), BF16), small=VM((16, model), F32),
+            hidden=VM((length, hid), BF16), cat=VM((length, heads * QB), BF16), dgu=VM((length, 2 * hid), BF16), small=VM((16, model), F32),
         )
         self.gathers = [RowGather(slots, rows) for _ in range(7)]
         self.g_self, self.g_mem, self.g_cross, self.g_ff, self.g_dy3, self.g_dy2, self.g_dy1 = self.gathers
@@ -810,7 +813,7 @@
     def grads_kv(self):
         c = self.sizes[2]
         self.dkvq[:, : 2 * c] = jnp.concatenate(
-            [self.shared.dka[...], self.shared.dva[...]], axis=1
+            [self.shared.dka[:, :c], self.shared.dva[...]], axis=1
         ).astype(BF16)
 
     def norm_backward(self, values, gain, reduce, base, done):
@@ -842,8 +845,9 @@
             group.gather.bind(spot, group.w)
             group.reduce.bind(spot, group.gp, self.red if zy else None, column)
             column += group.width
-        one.bind(ws.w)
-        two.bind(wc.w)
+        width = heads * QB
+        one.bind(ws.w, self.full_mem, self.cat)
+        two.bind(wc.w, self.dgu.at[:, :width], self.cat)
         gain_s, gain_c, gain_f = (ref[...].reshape(1, model) for ref in (self.gain_s, self.gain_c, self.gain_f))
 
         if zy:
@@ -863,10 +867,7 @@
             self.pack(wc, self.ck, self.cv, self.cq, self.co)
             self.pack(wf, self.fg, self.fu, self.fd)
         ranges = bucket_ranges(2 * QB)
-        values = self.sid[...].astype(F32)
-        one.kcol[...] = jnp.broadcast_to(values, (128, length)).T
-        for h in range(length // HALF):
-            s_.segq[h] = values[:, h * HALF : (h + 1) * HALF]
+        document_columns((one.q, two.q), one.k, self.sid, cols)
         make_bias(s_, self.table, heads, ranges)
         ws.gather.forward(1, 0)
         ws.gather.forward(2, 0)
@@ -915,7 +916,7 @@
             return carry
 
         lax.fori_loop(0, 4, self_block, 0)
-        two.kcol[...] = jnp.broadcast_to(self.mid[...].astype(F32), (128, length)).T
+        document_columns(None, two.k, self.mid, cols)
         self.g_mem.have_sib()
         self.g_mem.have_xsib(0, 4)
         wc.gather.have()
@@ -1029,6 +1030,7 @@
         weight_grad(wc.gp, 3 * cols, self.dy2, two.ctx, 0, cols)
         wc.reduce.open(1)
 
+        self.g_mem.finish()
         s_.dka[...] = jnp.zeros_like(s_.dka)
         s_.dva[...] = jnp.zeros_like(s_.dva)
 
@@ -1125,7 +1127,8 @@
             self.ss.end(self.tot)
 
         for gather in self.gathers:
-            gather.finish()
+            if gather is not self.g_mem:
+                gather.finish()
         for reduce in (self.r_out3, self.r_mem, self.r_dn1):
             reduce.finish()
         for group in self.groups:

time: 188 us -> 179 us (0.952)
  Pallas kernels: 187 us -> 178 us
    pallas_call x2, Pallas kernels: 187 us -> 178 us  [run_kernel(): pl.pallas_call(kernel, out_shape=[jax.ShapeDtypeStruct(*spec) for _, _, s...]
where the time goes in v4:
time: 179 us
  Pallas kernels  178 us (99%)
    pallas_call x2, Pallas kernels, run_kernel(): pl.pallas_call(kernel, out_shape=[jax.ShapeDtypeStruct(*spec) for _, _, s...  178 us

profile of v4, /device:TPU:0, one launch (start us, length us, event | category | flops | bytes accessed | tf_op | source)
XLA Modules:
  0.0 178.6 jit_solution(9493592967959982088)
XLA Ops:
  0.7 174.5 %layer.1 = (bf16[256,768]{1,0:T(8,128)(2,1)}, bf16[256,768]{1,0:T(8,128)(2,1)}, bf16[256,768]{1,0:T(8,128)(2,1)}, f32[16,768]{1,0:T(8,128)}, f32[96,3072]{1,0:T(8,128)}) custom-call(bf16[256,768]{1,0:T(8,128)(2,1)} %refs_0_.1, bf16[256,768]{1,0:T(8,128)(2,1)} %refs_1_.1, bf16[256,768]{1,0:T(8,128)(2,1)} %refs_2_.1, s32[1,1024]{1,0:T(1,128)} %refs_3_.1, ...), custom_call_target="tpu_custom_call" | custom-call | tf_op jit(solution)/shard_map/layer/pallas_call | solution.py:74
  175.2 3.2 %deliver.1 = (bf16[256,768]{1,0:T(8,128)(2,1)}, bf16[256,768]{1,0:T(8,128)(2,1)}, bf16[256,768]{1,0:T(8,128)(2,1)}, f32[96,192]{1,0:T(8,128)}, f32[96,192]{1,0:T...) custom-call(f32[96,3072]{1,0:T(8,128)} %get-tuple-element.41.refs_0_, ...), custom_call_target="tpu_custom_call" | custom-call | tf_op jit(solution)/shard_map/deliver/pallas_call | solution.py:74

commit v5 on v4

--- a/solution.py
+++ b/solution.py
@@ -397,33 +397,40 @@
 
     def pair(self, i):
         s = self.spot
-        dev = (s.at_n(s.sib), s.at_n(s.xp), s.at_w(s.yp))[i]
-        return remote(self.held.at[i], self.inn.at[i], self.ps.at[i], self.pr.at[i], dev)
+        source, dev = ((0, s.at_n(s.sib)), (2, s.at_n(s.xp)), (3, s.at_w(s.yp)))[i]
+        return remote(self.held.at[source], self.inn.at[i], self.ps.at[i], self.pr.at[i], dev)
 
     def hop(self, step, landed):
         other = (self.spot.z + step) % 4
         return remote(
-            self.held.at[3], self.zin.at[landed], self.zs.at[step], self.zr.at[landed], self.spot.at_z(other)
+            self.held.at[1], self.zin.at[landed], self.zs.at[step], self.zr.at[landed], self.spot.at_z(other)
         )
 
     def begin(self, value):
         self.held[0] = value
         self.pair(0).start()
 
-    def step(self, i):
-        self.pair(i).wait_recv()
-        self.held[i + 1] = self.held[i] + self.inn[i]
-        if i < 2:
-            self.pair(i + 1).start()
-        else:
-            self.zin[self.spot.z] = self.held[3]
-            for step in range(1, 4):
-                self.hop(step, self.spot.z).start()
-
-    def end(self, out):
+    def to_z(self):
+        self.pair(0).wait_recv()
+        self.held[1] = self.held[0] + self.inn[0]
+        self.zin[self.spot.z] = self.held[1]
+        for step in range(1, 4):
+            self.hop(step, self.spot.z).start()
+
+    def to_x(self):
         for step in range(1, 4):
             self.hop(step, (self.spot.z + step) % 4).wait_recv()
-        out[...] = ((self.zin[0] + self.zin[1]) + self.zin[2]) + self.zin[3]
+        self.held[2] = ((self.zin[0] + self.zin[1]) + self.zin[2]) + self.zin[3]
+        self.pair(1).start()
+
+    def to_y(self):
+        self.pair(1).wait_recv()
+        self.held[3] = self.held[2] + self.inn[1]
+        self.pair(2).start()
+
+    def end(self, out):
+        self.pair(2).wait_recv()
+        out[...] = self.held[3] + self.inn[2]
         for i in range(3):
             self.pair(i).wait_send()
         for step in range(1, 4):
@@ -877,10 +884,10 @@
         self.g_self.forward(2, 4)
         ws.gather.forward(2, 1)
         ws.gather.forward(3, 1)
+        wc.gather.open_z()
         self.g_self.have_sib()
         self.g_self.have_xsib(0, 4)
         ws.gather.have(0)
-        wc.gather.open_z()
 
         one.project_kv(self.full_self)
         for distance in (1, 2, 3):
@@ -1059,7 +1066,7 @@
                 for c in range(wf.reduce.chunks):
                     wf.reduce.total(c)
 
-            self.at(i, lambda: wc.reduce.first(0), ff_totals, lambda: wc.reduce.first(1))
+            self.at(i, None, lambda: wc.reduce.first(0), ff_totals, lambda: wc.reduce.first(1))
             return carry
 
         lax.fori_loop(0, 4, self_back, 0)
@@ -1100,9 +1107,10 @@
             value = self.x_three[self.chunk(k), :] + self.r_out3.total(k)
             self.result[self.chunk(k), :] = value.astype(BF16)
         if zy:
-            self.ss.step(0)
+            self.ss.to_z()
             ws.reduce.first(0)
             ws.reduce.first(1)
+            self.ss.to_x()
         for k in range(ROW_CHUNKS):
             self.gm[self.chunk(k), :] = self.r_mem.total(k).astype(BF16)
         for c in range(wc.reduce.chunks):
@@ -1114,13 +1122,11 @@
             self.gx[at, :] = value.astype(BF16)
             if zy and k == 1:
                 ws.reduce.first(3)
-            if zy and k == 3:
-                self.ss.step(1)
 
         self.norm_backward(self.x, gain_s, self.r_dn1, self.g, back_one)
         if zy:
+            self.ss.to_y()
             ws.reduce.first(4)
-            self.ss.step(2)
             ws.reduce.first(5)
             for c in range(ws.reduce.chunks):
                 ws.reduce.total(c)

time: 179 us -> 175 us (0.978)
  Pallas kernels: 178 us -> 174 us
    pallas_call x2, Pallas kernels: 178 us -> 174 us  [run_kernel(): pl.pallas_call(kernel, out_shape=[jax.ShapeDtypeStruct(*spec) for _, _, s...]
where the time goes in v5:
time: 175 us
  Pallas kernels  174 us (99%)
    pallas_call x2, Pallas kernels, run_kernel(): pl.pallas_call(kernel, out_shape=[jax.ShapeDtypeStruct(*spec) for _, _, s...  174 us

profile of v5, /device:TPU:0, one launch (start us, length us, event | category | flops | bytes accessed | tf_op | source)
XLA Modules:
  0.0 174.9 jit_solution(666105318769988656)
XLA Ops:
  0.7 170.8 %layer.1 = (bf16[256,768]{1,0:T(8,128)(2,1)}, bf16[256,768]{1,0:T(8,128)(2,1)}, bf16[256,768]{1,0:T(8,128)(2,1)}, f32[16,768]{1,0:T(8,128)}, f32[96,3072]{1,0:T(8,128)}) custom-call(bf16[256,768]{1,0:T(8,128)(2,1)} %refs_0_.1, bf16[256,768]{1,0:T(8,128)(2,1)} %refs_1_.1, bf16[256,768]{1,0:T(8,128)(2,1)} %refs_2_.1, s32[1,1024]{1,0:T(1,128)} %refs_3_.1, ...), custom_call_target="tpu_custom_call" | custom-call | tf_op jit(solution)/shard_map/layer/pallas_call | solution.py:74
  171.4 3.2 %deliver.1 = (bf16[256,768]{1,0:T(8,128)(2,1)}, bf16[256,768]{1,0:T(8,128)(2,1)}, bf16[256,768]{1,0:T(8,128)(2,1)}, f32[96,192]{1,0:T(8,128)}, f32[96,192]{1,0:T...) custom-call(f32[96,3072]{1,0:T(8,128)} %get-tuple-element.41.refs_0_, ...), custom_call_target="tpu_custom_call" | custom-call | tf_op jit(solution)/shard_map/deliver/pallas_call | solution.py:74

commit v6 on v5

--- a/solution.py
+++ b/solution.py
@@ -869,7 +869,6 @@
         self.full_mem[self.blk(spot.n), :] = self.m[...]
         self.g_mem.send_all()
         self.dy3[self.blk(spot.n), :] = self.cot[...]
-        self.g_dy3.send_all(0, 2)
         if zy:
             self.pack(wc, self.ck, self.cv, self.cq, self.co)
             self.pack(wf, self.fg, self.fu, self.fd)
@@ -928,13 +927,12 @@
         self.g_mem.have_xsib(0, 4)
         wc.gather.have()
         two.project_kv(self.full_mem)
-        self.g_dy3.forward(0, 2)
         for k in range(ROW_CHUNKS):
             value = self.x[self.chunk(k), :].astype(F32) + self.r_out1.total(k)
             self.x_two[self.chunk(k), :] = value
             self.full_cross[self.chunk(k, spot.n), :] = norm_rows(value, gain_c).astype(BF16)
             self.g_cross.send(k)
-        self.g_dy3.send_all(2, 4)
+        self.g_dy3.send_all(0, 4)
         wf.gather.forward(1, 0)
 
         def cross_block(i, carry):
@@ -948,7 +946,7 @@
             return carry
 
         lax.fori_loop(0, 4, cross_block, 0)
-        self.g_dy3.forward(2, 4)
+        self.g_dy3.forward(0, 4)
         for k in range(ROW_CHUNKS):
             value = self.x_two[self.chunk(k), :] + self.r_out2.total(k)
             self.x_three[self.chunk(k), :] = value

time: 175 us -> 175 us (level)
  no operation moved by 1% of the time
where the time goes in v6:
time: 175 us
  Pallas kernels  174 us (99%)
    pallas_call x2, Pallas kernels, run_kernel(): pl.pallas_call(kernel, out_shape=[jax.ShapeDtypeStruct(*spec) for _, _, s...  174 us

profile of v6, /device:TPU:0, one launch (start us, length us, event | category | flops | bytes accessed | tf_op | source)
XLA Modules:
  0.0 174.9 jit_solution(7006726582504311728)
XLA Ops:
  0.7 170.8 %layer.1 = (bf16[256,768]{1,0:T(8,128)(2,1)}, bf16[256,768]{1,0:T(8,128)(2,1)}, bf16[256,768]{1,0:T(8,128)(2,1)}, f32[16,768]{1,0:T(8,128)}, f32[96,3072]{1,0:T(8,128)}) custom-call(bf16[256,768]{1,0:T(8,128)(2,1)} %refs_0_.1, bf16[256,768]{1,0:T(8,128)(2,1)} %refs_1_.1, bf16[256,768]{1,0:T(8,128)(2,1)} %refs_2_.1, s32[1,1024]{1,0:T(1,128)} %refs_3_.1, ...), custom_call_target="tpu_custom_call" | custom-call | tf_op jit(solution)/shard_map/layer/pallas_call | solution.py:74
  171.4 3.2 %deliver.1 = (bf16[256,768]{1,0:T(8,128)(2,1)}, bf16[256,768]{1,0:T(8,128)(2,1)}, bf16[256,768]{1,0:T(8,128)(2,1)}, f32[96,192]{1,0:T(8,128)}, f32[96,192]{1,0:T...) custom-call(f32[96,3072]{1,0:T(8,128)} %get-tuple-element.41.refs_0_, ...), custom_call_target="tpu_custom_call" | custom-call | tf_op jit(solution)/shard_map/deliver/pallas_call | solution.py:74
